TPU v7x, 32 devices: a whole 2x2x4 slice. The times are simulated.
32 devices in a mesh: groups: 1, row: 32 (over z, y, x, core).
Axes of the slice: x: 2, y: 2, z: 4, core: 2. Of those that a mesh axis runs over, the one named last changes fastest.
Arguments:
- features: bfloat16 [64, 256, 256], P('groups', 'row'), may hold values from -6 to 6
- w_conv: bfloat16 [7, 9, 32, 64], replicated, may hold values from -0.25 to 0.25
- bias_in: float32 [7, 32], replicated, may hold values from -3 to 3
- w_out: bfloat16 [7, 64, 32], replicated, may hold values from -1 to 1
- bias_out: float32 [7, 64], replicated, may hold values from -2 to 2
Outputs:
- contacts: bfloat16 [64, 256, 256], P('groups', 'row')
All inputs are finite; a program needn't handle non-finite values.
Results may differ from a plain program's by a relative error of at most 0.014.
Values may be sent and summed in bfloat16 or wider, within the bound.
No kernel may reach another device: no remote copies, remote signals or barrier semaphores. Data moves between devices by JAX's collectives and lax.ppermute only.
A program may use at most 64 MiB of HBM per device.

v0:
```python
import jax
import jax.numpy as jnp
from jax import lax
from jax.sharding import PartitionSpec as P

SECTIONS = 2
DEPTH = 3


dilations = (1, 2, 4)


def extended_2(array, sides, width):
    for axis, dim in sides:
        size, length = (lax.axis_size(axis), array.shape[dim])
        up = [(i, (i + 1) % size) for i in range(size - 1)]
        down = [(j, i) for i, j in up]
        last = lax.slice_in_dim(array, length - width, length, axis=dim)
        leading = lax.slice_in_dim(array, 0, width, axis=dim)
        before = lax.ppermute(last, axis, up)
        after = lax.ppermute(leading, axis, down)
        array = jnp.concatenate([before, array, after], axis=dim)
    return array


def conv_rows(extended, w_conv, bias_in, w_out, bias_out, layer, dilation, first_row, map_rows):
    channels, rows_in, width_all = extended.shape
    rows_out = rows_in - 2 * dilation
    padded = jnp.pad(extended, ((0, 0), (0, 0), (dilation, dilation)))
    total_sum = jnp.zeros((w_conv.shape[2], rows_out, width_all), jnp.float32)
    for row_tap in range(3):
        for col_tap in range(3):
            window = padded[
                :,
                row_tap * dilation : row_tap * dilation + rows_out,
                col_tap * dilation : col_tap * dilation + width_all,
            ]
            total_sum = total_sum + jnp.einsum(
                "hc,crm->hrm",
                w_conv[layer, row_tap * 3 + col_tap],
                window,
                preferred_element_type=jnp.float32,
            )
    hidden = jax.nn.relu(total_sum + bias_in[layer][:, None, None]).astype(jnp.bfloat16)
    blended = jnp.einsum("ch,hrm->crm", w_out[layer], hidden, preferred_element_type=jnp.float32)
    residual = extended[:, dilation : rows_in - dilation, :].astype(jnp.float32)
    result = (residual + blended + bias_out[layer][:, None, None]).astype(jnp.bfloat16)
    row_ids = first_row + dilation + jnp.arange(rows_out, dtype=jnp.int32)
    inside = (row_ids >= 0) & (row_ids < map_rows)
    return jnp.where(inside[None, :, None], result, jnp.zeros_like(result))


def mirror_plain(field):
    channels, shard_rows, width_all = field.shape
    blocks = width_all // shard_rows
    tiles = (
        field.reshape(channels, shard_rows, blocks, shard_rows)
        .transpose(2, 3, 1, 0)
        .reshape(blocks, shard_rows, shard_rows * channels)
    )
    received = lax.all_to_all(tiles, "row", split_axis=0, concat_axis=0, tiled=True)
    flipped = (
        received.reshape(blocks, shard_rows, shard_rows, channels)
        .transpose(3, 1, 0, 2)
        .reshape(channels, shard_rows, width_all)
    )
    return ((field.astype(jnp.float32) + flipped.astype(jnp.float32)) * 0.5).astype(jnp.bfloat16)


def on_device(features, w_conv, bias_in, w_out, bias_out):
    shard_rows = features.shape[1]
    map_rows = shard_rows * lax.axis_size("row")
    my_start = lax.axis_index("row") * shard_rows
    params = (w_conv, bias_in, w_out, bias_out)
    field = features
    for section_idx in range(SECTIONS):
        layer = section_idx * DEPTH
        for position, dilation in enumerate(dilations):
            extended = extended_2(field, (("row", 1),), dilation)
            field = conv_rows(
                extended, *params, layer + position, dilation, my_start - dilation, map_rows
            )
        field = mirror_plain(field)
    extended = extended_2(field, (("row", 1),), 1)
    return conv_rows(extended, *params, SECTIONS * DEPTH, 1, my_start - 1, map_rows)


def solution(mesh):
    in_specs = (P("groups", "row", None), P(), P(), P(), P())
    out_specs = P("groups", "row", None)
    return jax.shard_map(
        on_device, mesh=mesh, in_specs=in_specs, out_specs=out_specs, check_vma=False
    )
```

profile of v0, /device:TPU:1, one launch (start us, length us, event | category | flops | bytes accessed | tf_op | source)
XLA Modules:
  0.0 119.1 jit_solution(11581948878868281379)
XLA Ops:
  0.0 1.1 copy.16
  1.1 4.5 %collective-permute-start = (bf16[64,1,256]{2,0,1:T(8,128)(2,1)S(1)}, bf16[64,1,256]{2,0,1:T(8,128)(2,1)S(1)}, u32[]{:S(2)}, u32[]{:S(2)}) collective-permute-start(bf16[64,1,256]{2,0,1:T(8,128)(2,1)S(1)} %get-tuple-element.17), channel_id=1, source_target_pairs={{0,1},{1,2},{2,3},{3,4},{4,5},{5,6},{6,7},{7,8},{8,9},{9,10},{10,1... | collective-permute-start | bytes 98312 | tf_op jit(solution)/shard_map/ppermute | solution.py:20
  5.6 1.9 %collective-permute-start.1 = (bf16[64,1,256]{2,0,1:T(8,128)(2,1)S(1)}, bf16[64,1,256]{2,0,1:T(8,128)(2,1)S(1)}, u32[]{:S(2)}, u32[]{:S(2)}) collective-permute-start(bf16[64,1,256]{2,0,1:T(8,128)(2,1)S(1)} %get-tuple-element.18), channel_id=1, source_target_pairs={{1,0},{2,1},{3,2},{4,3},{5,4},{6,5},{7,6},{8,7},{9,8},{10,9},{11,1... | collective-permute-start | bytes 98312 | tf_op jit(solution)/shard_map/ppermute | solution.py:21
  7.5 0.9 slice_bitcast_fusion.1
  8.5 0.9 slice_bitcast_fusion
  9.4 1.1 fusion.227
  12.6 0.6 copy-done
  13.1 0.5 fusion.49
  13.6 3.4 %collective-permute-start.2 = (bf16[64,2,256]{2,0,1:T(8,128)(2,1)S(1)}, bf16[64,2,256]{2,0,1:T(8,128)(2,1)S(1)}, u32[]{:S(2)}, u32[]{:S(2)}) collective-permute-start(bf16[64,2,256]{2,0,1:T(8,128)(2,1)S(1)} %get-tuple-element.15), channel_id=1, source_target_pairs={{0,1},{1,2},{2,3},{3,4},{4,5},{5,6},{6,7},{7,8},{8,9},{9,10},{10,1... | collective-permute-start | bytes 196616 | tf_op jit(solution)/shard_map/ppermute | solution.py:20
  17.0 1.9 %collective-permute-start.3 = (bf16[64,2,256]{2,0,1:T(8,128)(2,1)S(1)}, bf16[64,2,256]{2,0,1:T(8,128)(2,1)S(1)}, u32[]{:S(2)}, u32[]{:S(2)}) collective-permute-start(bf16[64,2,256]{2,0,1:T(8,128)(2,1)S(1)} %get-tuple-element.16), channel_id=1, source_target_pairs={{1,0},{2,1},{3,2},{4,3},{5,4},{6,5},{7,6},{8,7},{9,8},{10,9},{11,1... | collective-permute-start | bytes 196616 | tf_op jit(solution)/shard_map/ppermute | solution.py:21
  19.0 3.6 %collective-permute-done.3 = bf16[64,2,256]{2,0,1:T(8,128)(2,1)S(1)} collective-permute-done((bf16[64,2,256]{2,0,1:T(8,128)(2,1)S(1)}, bf16[64,2,256]{2,0,1:T(8,128)(2,1)S(1)}, u32[]{:S(2)}, u32[]{:S(2)}) %collective-permute-start.3) | collective-permute-done | bytes 65568 | tf_op jit(solution)/shard_map/ppermute | solution.py:21
  24.6 0.4 fusion.50
  25.0 1.9 %collective-permute-start.4 = (bf16[64,4,256]{2,0,1:T(8,128)(2,1)S(1)}, bf16[64,4,256]{2,0,1:T(8,128)(2,1)S(1)}, u32[]{:S(2)}, u32[]{:S(2)}) collective-permute-start(bf16[64,4,256]{2,0,1:T(8,128)(2,1)S(1)} %get-tuple-element.13), channel_id=1, source_target_pairs={{0,1},{1,2},{2,3},{3,4},{4,5},{5,6},{6,7},{7,8},{8,9},{9,10},{10,1... | collective-permute-start | bytes 393224 | tf_op jit(solution)/shard_map/ppermute | solution.py:20
  27.0 2.4 %collective-permute-start.5 = (bf16[64,4,256]{2,0,1:T(8,128)(2,1)S(1)}, bf16[64,4,256]{2,0,1:T(8,128)(2,1)S(1)}, u32[]{:S(2)}, u32[]{:S(2)}) collective-permute-start(bf16[64,4,256]{2,0,1:T(8,128)(2,1)S(1)} %get-tuple-element.14), channel_id=1, source_target_pairs={{1,0},{2,1},{3,2},{4,3},{5,4},{6,5},{7,6},{8,7},{9,8},{10,9},{11,1... | collective-permute-start | bytes 393224 | tf_op jit(solution)/shard_map/ppermute | solution.py:21
  29.4 5.5 %collective-permute-done.5 = bf16[64,4,256]{2,0,1:T(8,128)(2,1)S(1)} collective-permute-done((bf16[64,4,256]{2,0,1:T(8,128)(2,1)S(1)}, bf16[64,4,256]{2,0,1:T(8,128)(2,1)S(1)}, u32[]{:S(2)}, u32[]{:S(2)}) %collective-permute-start.5) | collective-permute-done | bytes 131104 | tf_op jit(solution)/shard_map/ppermute | solution.py:21
  34.9 0.4 select_maximum_fusion.2
  38.0 18.5 %all_to_all.10 = bf16[32,8,512]{2,1,0:T(8,128)(2,1)S(1)} all-to-all(bf16[32,8,512]{2,1,0:T(8,128)(2,1)S(1)} %reshape.60), channel_id=1, replica_groups=mesh['groups'=1,'row'=32] {'row'}, dimensions={0} | all-to-all | bytes 524288 | tf_op jit(solution)/shard_map/all_to_all | solution.py:61
  57.2 2.4 %collective-permute-start.6 = (bf16[64,1,256]{2,0,1:T(8,128)(2,1)S(1)}, bf16[64,1,256]{2,0,1:T(8,128)(2,1)S(1)}, u32[]{:S(2)}, u32[]{:S(2)}) collective-permute-start(bf16[64,1,256]{2,0,1:T(8,128)(2,1)S(1)} %get-tuple-element.11), channel_id=1, source_target_pairs={{0,1},{1,2},{2,3},{3,4},{4,5},{5,6},{6,7},{7,8},{8,9},{9,10},{10,1... | collective-permute-start | bytes 98312 | tf_op jit(solution)/shard_map/ppermute | solution.py:20
  59.6 2.0 %collective-permute-start.7 = (bf16[64,1,256]{2,0,1:T(8,128)(2,1)S(1)}, bf16[64,1,256]{2,0,1:T(8,128)(2,1)S(1)}, u32[]{:S(2)}, u32[]{:S(2)}) collective-permute-start(bf16[64,1,256]{2,0,1:T(8,128)(2,1)S(1)} %get-tuple-element.12), channel_id=1, source_target_pairs={{1,0},{2,1},{3,2},{4,3},{5,4},{6,5},{7,6},{8,7},{9,8},{10,9},{11,1... | collective-permute-start | bytes 98312 | tf_op jit(solution)/shard_map/ppermute | solution.py:21
  61.6 3.3 %collective-permute-done.7 = bf16[64,1,256]{2,0,1:T(8,128)(2,1)S(1)} collective-permute-done((bf16[64,1,256]{2,0,1:T(8,128)(2,1)S(1)}, bf16[64,1,256]{2,0,1:T(8,128)(2,1)S(1)}, u32[]{:S(2)}, u32[]{:S(2)}) %collective-permute-start.7) | collective-permute-done | bytes 32800 | tf_op jit(solution)/shard_map/ppermute | solution.py:21
  67.2 1.9 %collective-permute-start.8 = (bf16[64,2,256]{2,0,1:T(8,128)(2,1)S(1)}, bf16[64,2,256]{2,0,1:T(8,128)(2,1)S(1)}, u32[]{:S(2)}, u32[]{:S(2)}) collective-permute-start(bf16[64,2,256]{2,0,1:T(8,128)(2,1)S(1)} %get-tuple-element.9), channel_id=1, source_target_pairs={{0,1},{1,2},{2,3},{3,4},{4,5},{5,6},{6,7},{7,8},{8,9},{9,10},{10,1... | collective-permute-start | bytes 196616 | tf_op jit(solution)/shard_map/ppermute | solution.py:20
  69.1 2.4 %collective-permute-start.9 = (bf16[64,2,256]{2,0,1:T(8,128)(2,1)S(1)}, bf16[64,2,256]{2,0,1:T(8,128)(2,1)S(1)}, u32[]{:S(2)}, u32[]{:S(2)}) collective-permute-start(bf16[64,2,256]{2,0,1:T(8,128)(2,1)S(1)} %get-tuple-element.10), channel_id=1, source_target_pairs={{1,0},{2,1},{3,2},{4,3},{5,4},{6,5},{7,6},{8,7},{9,8},{10,9},{11,1... | collective-permute-start | bytes 196616 | tf_op jit(solution)/shard_map/ppermute | solution.py:21
  71.6 4.5 %collective-permute-done.9 = bf16[64,2,256]{2,0,1:T(8,128)(2,1)S(1)} collective-permute-done((bf16[64,2,256]{2,0,1:T(8,128)(2,1)S(1)}, bf16[64,2,256]{2,0,1:T(8,128)(2,1)S(1)}, u32[]{:S(2)}, u32[]{:S(2)}) %collective-permute-start.9) | collective-permute-done | bytes 65568 | tf_op jit(solution)/shard_map/ppermute | solution.py:21
  78.5 1.9 %collective-permute-start.10 = (bf16[64,4,256]{2,0,1:T(8,128)(2,1)S(1)}, bf16[64,4,256]{2,0,1:T(8,128)(2,1)S(1)}, u32[]{:S(2)}, u32[]{:S(2)}) collective-permute-start(bf16[64,4,256]{2,0,1:T(8,128)(2,1)S(1)} %get-tuple-element.7), channel_id=1, source_target_pairs={{0,1},{1,2},{2,3},{3,4},{4,5},{5,6},{6,7},{7,8},{8,9},{9,10},{10,1... | collective-permute-start | bytes 393224 | tf_op jit(solution)/shard_map/ppermute | solution.py:20
  80.4 2.4 %collective-permute-start.11 = (bf16[64,4,256]{2,0,1:T(8,128)(2,1)S(1)}, bf16[64,4,256]{2,0,1:T(8,128)(2,1)S(1)}, u32[]{:S(2)}, u32[]{:S(2)}) collective-permute-start(bf16[64,4,256]{2,0,1:T(8,128)(2,1)S(1)} %get-tuple-element.8), channel_id=1, source_target_pairs={{1,0},{2,1},{3,2},{4,3},{5,4},{6,5},{7,6},{8,7},{9,8},{10,9},{11,1... | collective-permute-start | bytes 393224 | tf_op jit(solution)/shard_map/ppermute | solution.py:21
  82.9 4.7 %collective-permute-done.11 = bf16[64,4,256]{2,0,1:T(8,128)(2,1)S(1)} collective-permute-done((bf16[64,4,256]{2,0,1:T(8,128)(2,1)S(1)}, bf16[64,4,256]{2,0,1:T(8,128)(2,1)S(1)}, u32[]{:S(2)}, u32[]{:S(2)}) %collective-permute-start.11) | collective-permute-done | bytes 131104 | tf_op jit(solution)/shard_map/ppermute | solution.py:21
  87.6 0.4 select_maximum_fusion
  90.7 16.9 %all_to_all.11 = bf16[32,8,512]{2,1,0:T(8,128)(2,1)S(1)} all-to-all(bf16[32,8,512]{2,1,0:T(8,128)(2,1)S(1)} %reshape.62), channel_id=1, replica_groups=mesh['groups'=1,'row'=32] {'row'}, dimensions={0} | all-to-all | bytes 524288 | tf_op jit(solution)/shard_map/all_to_all | solution.py:61
  108.3 2.4 %collective-permute-start.12 = (bf16[64,1,256]{2,0,1:T(8,128)(2,1)S(1)}, bf16[64,1,256]{2,0,1:T(8,128)(2,1)S(1)}, u32[]{:S(2)}, u32[]{:S(2)}) collective-permute-start(bf16[64,1,256]{2,0,1:T(8,128)(2,1)S(1)} %get-tuple-element.5), channel_id=1, source_target_pairs={{0,1},{1,2},{2,3},{3,4},{4,5},{5,6},{6,7},{7,8},{8,9},{9,10},{10,1... | collective-permute-start | bytes 98312 | tf_op jit(solution)/shard_map/ppermute | solution.py:20
  110.7 2.0 %collective-permute-start.13 = (bf16[64,1,256]{2,0,1:T(8,128)(2,1)S(1)}, bf16[64,1,256]{2,0,1:T(8,128)(2,1)S(1)}, u32[]{:S(2)}, u32[]{:S(2)}) collective-permute-start(bf16[64,1,256]{2,0,1:T(8,128)(2,1)S(1)} %get-tuple-element.6), channel_id=1, source_target_pairs={{1,0},{2,1},{3,2},{4,3},{5,4},{6,5},{7,6},{8,7},{9,8},{10,9},{11,1... | collective-permute-start | bytes 98312 | tf_op jit(solution)/shard_map/ppermute | solution.py:21
  112.7 3.3 %collective-permute-done.13 = bf16[64,1,256]{2,0,1:T(8,128)(2,1)S(1)} collective-permute-done((bf16[64,1,256]{2,0,1:T(8,128)(2,1)S(1)}, bf16[64,1,256]{2,0,1:T(8,128)(2,1)S(1)}, u32[]{:S(2)}, u32[]{:S(2)}) %collective-permute-start.13) | collective-permute-done | bytes 32800 | tf_op jit(solution)/shard_map/ppermute | solution.py:21
  118.3 0.9 copy.31
  (98 shorter events, 17.5 us)
Async XLA Ops:
  0.0 11.1 %copy-start.1 = (bf16[7,9,32,64]{3,2,1,0:T(8,128)(2,1)S(1)}, bf16[7,9,32,64]{3,2,1,0:T(8,128)(2,1)}, u32[]{:S(2)}) copy-start(bf16[7,9,32,64]{3,2,1,0:T(8,128)(2,1)} %param.6) | copy-start | bytes 774148
  1.1 9.5 %collective-permute-start = (bf16[64,1,256]{2,0,1:T(8,128)(2,1)S(1)}, bf16[64,1,256]{2,0,1:T(8,128)(2,1)S(1)}, u32[]{:S(2)}, u32[]{:S(2)}) collective-permute-start(bf16[64,1,256]{2,0,1:T(8,128)(2,1)S(1)} %get-tuple-element.17), channel_id=1, source_target_pairs={{0,1},{1,2},{2,3},{3,4},{4,5},{5,6},{6,7},{7,8},{8,9},{9,10},{10,1... | collective-permute-start | bytes 98312 | tf_op jit(solution)/shard_map/ppermute | solution.py:20
  5.6 5.2 %collective-permute-start.1 = (bf16[64,1,256]{2,0,1:T(8,128)(2,1)S(1)}, bf16[64,1,256]{2,0,1:T(8,128)(2,1)S(1)}, u32[]{:S(2)}, u32[]{:S(2)}) collective-permute-start(bf16[64,1,256]{2,0,1:T(8,128)(2,1)S(1)} %get-tuple-element.18), channel_id=1, source_target_pairs={{1,0},{2,1},{3,2},{4,3},{5,4},{6,5},{7,6},{8,7},{9,8},{10,9},{11,1... | collective-permute-start | bytes 98312 | tf_op jit(solution)/shard_map/ppermute | solution.py:21
  12.2 1.0 copy-start
  12.2 0.9 copy-start.2
  13.6 5.4 %collective-permute-start.2 = (bf16[64,2,256]{2,0,1:T(8,128)(2,1)S(1)}, bf16[64,2,256]{2,0,1:T(8,128)(2,1)S(1)}, u32[]{:S(2)}, u32[]{:S(2)}) collective-permute-start(bf16[64,2,256]{2,0,1:T(8,128)(2,1)S(1)} %get-tuple-element.15), channel_id=1, source_target_pairs={{0,1},{1,2},{2,3},{3,4},{4,5},{5,6},{6,7},{7,8},{8,9},{9,10},{10,1... | collective-permute-start | bytes 196616 | tf_op jit(solution)/shard_map/ppermute | solution.py:20
  17.0 5.6 %collective-permute-start.3 = (bf16[64,2,256]{2,0,1:T(8,128)(2,1)S(1)}, bf16[64,2,256]{2,0,1:T(8,128)(2,1)S(1)}, u32[]{:S(2)}, u32[]{:S(2)}) collective-permute-start(bf16[64,2,256]{2,0,1:T(8,128)(2,1)S(1)} %get-tuple-element.16), channel_id=1, source_target_pairs={{1,0},{2,1},{3,2},{4,3},{5,4},{6,5},{7,6},{8,7},{9,8},{10,9},{11,1... | collective-permute-start | bytes 196616 | tf_op jit(solution)/shard_map/ppermute | solution.py:21
  25.0 4.3 %collective-permute-start.4 = (bf16[64,4,256]{2,0,1:T(8,128)(2,1)S(1)}, bf16[64,4,256]{2,0,1:T(8,128)(2,1)S(1)}, u32[]{:S(2)}, u32[]{:S(2)}) collective-permute-start(bf16[64,4,256]{2,0,1:T(8,128)(2,1)S(1)} %get-tuple-element.13), channel_id=1, source_target_pairs={{0,1},{1,2},{2,3},{3,4},{4,5},{5,6},{6,7},{7,8},{8,9},{9,10},{10,1... | collective-permute-start | bytes 393224 | tf_op jit(solution)/shard_map/ppermute | solution.py:20
  27.0 7.9 %collective-permute-start.5 = (bf16[64,4,256]{2,0,1:T(8,128)(2,1)S(1)}, bf16[64,4,256]{2,0,1:T(8,128)(2,1)S(1)}, u32[]{:S(2)}, u32[]{:S(2)}) collective-permute-start(bf16[64,4,256]{2,0,1:T(8,128)(2,1)S(1)} %get-tuple-element.14), channel_id=1, source_target_pairs={{1,0},{2,1},{3,2},{4,3},{5,4},{6,5},{7,6},{8,7},{9,8},{10,9},{11,1... | collective-permute-start | bytes 393224 | tf_op jit(solution)/shard_map/ppermute | solution.py:21
  57.2 4.3 %collective-permute-start.6 = (bf16[64,1,256]{2,0,1:T(8,128)(2,1)S(1)}, bf16[64,1,256]{2,0,1:T(8,128)(2,1)S(1)}, u32[]{:S(2)}, u32[]{:S(2)}) collective-permute-start(bf16[64,1,256]{2,0,1:T(8,128)(2,1)S(1)} %get-tuple-element.11), channel_id=1, source_target_pairs={{0,1},{1,2},{2,3},{3,4},{4,5},{5,6},{6,7},{7,8},{8,9},{9,10},{10,1... | collective-permute-start | bytes 98312 | tf_op jit(solution)/shard_map/ppermute | solution.py:20
  59.6 5.2 %collective-permute-start.7 = (bf16[64,1,256]{2,0,1:T(8,128)(2,1)S(1)}, bf16[64,1,256]{2,0,1:T(8,128)(2,1)S(1)}, u32[]{:S(2)}, u32[]{:S(2)}) collective-permute-start(bf16[64,1,256]{2,0,1:T(8,128)(2,1)S(1)} %get-tuple-element.12), channel_id=1, source_target_pairs={{1,0},{2,1},{3,2},{4,3},{5,4},{6,5},{7,6},{8,7},{9,8},{10,9},{11,1... | collective-permute-start | bytes 98312 | tf_op jit(solution)/shard_map/ppermute | solution.py:21
  67.2 4.3 %collective-permute-start.8 = (bf16[64,2,256]{2,0,1:T(8,128)(2,1)S(1)}, bf16[64,2,256]{2,0,1:T(8,128)(2,1)S(1)}, u32[]{:S(2)}, u32[]{:S(2)}) collective-permute-start(bf16[64,2,256]{2,0,1:T(8,128)(2,1)S(1)} %get-tuple-element.9), channel_id=1, source_target_pairs={{0,1},{1,2},{2,3},{3,4},{4,5},{5,6},{6,7},{7,8},{8,9},{9,10},{10,1... | collective-permute-start | bytes 196616 | tf_op jit(solution)/shard_map/ppermute | solution.py:20
  69.1 7.0 %collective-permute-start.9 = (bf16[64,2,256]{2,0,1:T(8,128)(2,1)S(1)}, bf16[64,2,256]{2,0,1:T(8,128)(2,1)S(1)}, u32[]{:S(2)}, u32[]{:S(2)}) collective-permute-start(bf16[64,2,256]{2,0,1:T(8,128)(2,1)S(1)} %get-tuple-element.10), channel_id=1, source_target_pairs={{1,0},{2,1},{3,2},{4,3},{5,4},{6,5},{7,6},{8,7},{9,8},{10,9},{11,1... | collective-permute-start | bytes 196616 | tf_op jit(solution)/shard_map/ppermute | solution.py:21
  78.5 4.3 %collective-permute-start.10 = (bf16[64,4,256]{2,0,1:T(8,128)(2,1)S(1)}, bf16[64,4,256]{2,0,1:T(8,128)(2,1)S(1)}, u32[]{:S(2)}, u32[]{:S(2)}) collective-permute-start(bf16[64,4,256]{2,0,1:T(8,128)(2,1)S(1)} %get-tuple-element.7), channel_id=1, source_target_pairs={{0,1},{1,2},{2,3},{3,4},{4,5},{5,6},{6,7},{7,8},{8,9},{9,10},{10,1... | collective-permute-start | bytes 393224 | tf_op jit(solution)/shard_map/ppermute | solution.py:20
  80.4 7.2 %collective-permute-start.11 = (bf16[64,4,256]{2,0,1:T(8,128)(2,1)S(1)}, bf16[64,4,256]{2,0,1:T(8,128)(2,1)S(1)}, u32[]{:S(2)}, u32[]{:S(2)}) collective-permute-start(bf16[64,4,256]{2,0,1:T(8,128)(2,1)S(1)} %get-tuple-element.8), channel_id=1, source_target_pairs={{1,0},{2,1},{3,2},{4,3},{5,4},{6,5},{7,6},{8,7},{9,8},{10,9},{11,1... | collective-permute-start | bytes 393224 | tf_op jit(solution)/shard_map/ppermute | solution.py:21
  108.3 4.3 %collective-permute-start.12 = (bf16[64,1,256]{2,0,1:T(8,128)(2,1)S(1)}, bf16[64,1,256]{2,0,1:T(8,128)(2,1)S(1)}, u32[]{:S(2)}, u32[]{:S(2)}) collective-permute-start(bf16[64,1,256]{2,0,1:T(8,128)(2,1)S(1)} %get-tuple-element.5), channel_id=1, source_target_pairs={{0,1},{1,2},{2,3},{3,4},{4,5},{5,6},{6,7},{7,8},{8,9},{9,10},{10,1... | collective-permute-start | bytes 98312 | tf_op jit(solution)/shard_map/ppermute | solution.py:20
  110.7 5.2 %collective-permute-start.13 = (bf16[64,1,256]{2,0,1:T(8,128)(2,1)S(1)}, bf16[64,1,256]{2,0,1:T(8,128)(2,1)S(1)}, u32[]{:S(2)}, u32[]{:S(2)}) collective-permute-start(bf16[64,1,256]{2,0,1:T(8,128)(2,1)S(1)} %get-tuple-element.6), channel_id=1, source_target_pairs={{1,0},{2,1},{3,2},{4,3},{5,4},{6,5},{7,6},{8,7},{9,8},{10,9},{11,1... | collective-permute-start | bytes 98312 | tf_op jit(solution)/shard_map/ppermute | solution.py:21
where the time goes:
time: 121 us; the launch traced here: 119 us
  blocking collectives  35.3 us (29%)
  starting transfers between devices  33.4 us (28%)
  waiting for transfers between devices  25.2 us (21%)
  matrix products  15.2 us (13%)
  local copies, waits for them, and re-layouts  6.93 us (6%)
  other arithmetic  2.28 us (2%)
    all_to_all x2, blocking collectives, mirror_plain(): lax.all_to_all(tiles, 'row', split_axis=0, concat_axis=0, tiled=True)  35.3 us
    ppermute x7, waiting for transfers between devices, extended_2(): after = lax.ppermute(leading, axis, down)  25.2 us
    ppermute x7, starting transfers between devices, extended_2(): before = lax.ppermute(last, axis, up)  18.4 us
    ppermute x7, starting transfers between devices, extended_2(): after = lax.ppermute(leading, axis, down)  15 us
    dot_general x56, matrix products, conv_rows(): jnp.einsum('hc,crm->hrm', w_conv[layer, row_tap * 3 + col_tap], window, p...  12.5 us
    dot_general x7, matrix products, conv_rows(): jnp.einsum('ch,hrm->crm', w_out[layer], hidden, preferred_element_type=jn...  2.67 us
  transfers between devices with their start and end apart: 14, of which 7 were waited for; matrix products, arithmetic and copies ran while one was open for 3% of the time, Pallas kernels for 0%

commit v1 on v0

v1 whole, which is shorter than its diff:
```python
import jax
import jax.numpy as jnp
from jax import lax
from jax.experimental import pallas as pl
from jax.experimental.pallas import tpu as pltpu
from jax.sharding import PartitionSpec as P

SECTIONS = 2
DEPTH = 3

dilations = (1, 2, 4)
LANES = 128


def shifted(row, dilation):
    channels, width = row.shape
    wide = row.astype(jnp.float32)
    column = lax.broadcasted_iota(jnp.int32, (channels, width), 1)
    left = jnp.where(column >= dilation, pltpu.roll(wide, dilation, 1), 0.0)
    right = jnp.where(column < width - dilation, pltpu.roll(wide, width - dilation, 1), 0.0)
    return left.astype(jnp.bfloat16), row, right.astype(jnp.bfloat16)


def put_row(stack, index, row, dilation):
    channels = row.shape[0]
    for place, part in enumerate(shifted(row, dilation)):
        stack[index, place * channels : (place + 1) * channels, :] = part


def taps(stack, index, dilation):
    return jnp.concatenate([stack[index + tap * dilation] for tap in range(3)], axis=0)


def hidden_of(window, kernel, bias):
    inner = jnp.dot(kernel, window, preferred_element_type=jnp.float32)
    return jnp.maximum(inner + bias, 0.0).astype(jnp.bfloat16)


def output_of(residual, hidden, kernel, bias):
    blended = jnp.dot(kernel, hidden, preferred_element_type=jnp.float32)
    return (residual.astype(jnp.float32) + blended + bias).astype(jnp.bfloat16)


def masked(row, row_id, map_rows):
    inside = jnp.logical_and(row_id >= 0, row_id < map_rows)
    return jnp.where(inside, row, jnp.zeros_like(row))


def loop(count, body, unroll):
    def step(index, carry):
        body(index)
        return carry

    lax.fori_loop(0, count, step, 0, unroll=unroll)


def load_shards(place, own, across, beside, wide, stack, dilation, margin):
    odd = place[0]
    shard_rows = own.shape[1]
    channels = own.shape[0]
    slots = ((own, 1), (beside, jnp.where(odd == 1, 0, 2)), (across, jnp.where(odd == 1, 2, 0)))
    blocks = own.shape[2] // LANES
    for shard, slot in slots:
        whole = shard[...].astype(jnp.float32).reshape(channels * shard_rows, own.shape[2])
        for block in range(blocks):
            wide[slot, block] = whole[:, block * LANES : (block + 1) * LANES]
    total = 3 * shard_rows - 2 * margin

    def body(index):
        source = index + margin
        slot = source // shard_rows
        picked = pl.ds(source % shard_rows, channels, stride=shard_rows)
        row = jnp.concatenate([wide[slot, block, picked, :] for block in range(blocks)], axis=1)
        put_row(stack, index, row.astype(jnp.bfloat16), dilation)

    loop(total, body, 2)
    return total


def section_one(place, own, across, beside, w_conv, bias_in, w_out, bias_out, out, wide, first, second):
    channels, shard_rows, _ = own.shape
    margin = shard_rows - sum(dilations)
    rows = load_shards(place, own, across, beside, wide, first, dilations[0], margin)
    row_id = place[1] - sum(dilations)
    source, target = first, second
    for layer, dilation in enumerate(dilations):
        rows = rows - 2 * dilation
        row_id = row_id + dilation
        last = layer == DEPTH - 1

        def body(index, source=source, target=target, row_id=row_id, layer=layer, dilation=dilation, last=last):
            hidden = hidden_of(taps(source, index, dilation), w_conv[layer], bias_in[layer])
            residual = source[index + dilation, channels : 2 * channels, :]
            row = output_of(residual, hidden, w_out[layer], bias_out[layer])
            if last:
                out[index] = row
            else:
                put_row(target, index, masked(row, row_id + index, place[2]), dilations[layer + 1])

        loop(rows, body, 2)
        source, target = target, source


def section_two(place, own, across, beside, w_conv, w_turned, bias_in, w_out, bias_out, out, first, plain, turned, plain_2, turned_2):
    channels = own.shape[1]
    inner = w_out.shape[2]
    shard_rows = own.shape[0]
    odd = place[0]
    slots = ((own, 1), (beside, jnp.where(odd == 1, 0, 2)), (across, jnp.where(odd == 1, 2, 0)))
    for shard, slot in slots:
        def copy_row(index, shard=shard, slot=slot):
            put_row(first, slot * shard_rows + index, shard[index], dilations[0])

        loop(shard_rows, copy_row, 2)
    reach = sum(dilations) + 1
    rows = shard_rows + 2 * reach
    row_id = place[1] - reach
    base = shard_rows - reach

    dilation = dilations[0]
    rows, row_id = rows - 2 * dilation, row_id + dilation
    both = jnp.concatenate([w_conv[0], w_turned[0]], axis=0)

    def block_a(index, row_id=row_id):
        bias = jnp.concatenate([bias_in[0], bias_in[0]], axis=0)
        hidden = hidden_of(taps(first, base + index, dilations[0]), both, bias)
        residual = first[base + index + dilations[0], channels : 2 * channels, :]
        for part, target in enumerate((plain, turned)):
            row = output_of(residual, hidden[part * inner : (part + 1) * inner], w_out[0], bias_out[0])
            put_row(target, index, masked(row, row_id + index, place[2]), dilations[1])

    loop(rows, block_a, 2)

    dilation = dilations[1]
    rows, row_id = rows - 2 * dilation, row_id + dilation

    def block_b(index, row_id=row_id):
        for source, target, kernel in ((plain, plain_2, w_conv), (turned, turned_2, w_turned)):
            hidden = hidden_of(taps(source, index, dilations[1]), kernel[1], bias_in[1])
            residual = source[index + dilations[1], channels : 2 * channels, :]
            row = output_of(residual, hidden, w_out[1], bias_out[1])
            put_row(target, index, masked(row, row_id + index, place[2]), dilations[2])

    loop(rows, block_b, 2)

    dilation = dilations[2]
    rows, row_id = rows - 2 * dilation, row_id + dilation

    def block_c(index, row_id=row_id):
        halves = []
        for source, kernel in ((plain_2, w_conv), (turned_2, w_turned)):
            hidden = hidden_of(taps(source, index, dilations[2]), kernel[2], bias_in[2])
            residual = source[index + dilations[2], channels : 2 * channels, :]
            halves.append(output_of(residual, hidden, w_out[2], bias_out[2]).astype(jnp.float32))
        row = ((halves[0] + halves[1]) * 0.5).astype(jnp.bfloat16)
        put_row(first, index, masked(row, row_id + index, place[2]), dilations[0])

    loop(rows, block_c, 2)

    def block_d(index):
        hidden = hidden_of(taps(first, index, dilations[0]), w_conv[3], bias_in[3])
        residual = first[index + dilations[0], channels : 2 * channels, :]
        out[index] = output_of(residual, hidden, w_out[3], bias_out[3])

    loop(shard_rows, block_d, 2)


def neighbours(array, axis):
    size = lax.axis_size(axis)
    inside = [(i, i ^ 1) for i in range(size)]
    edges = [(i, i + 1) for i in range(1, size - 1, 2)]
    edges = edges + [(j, i) for i, j in edges]
    across = lax.ppermute(array, axis, edges)
    beside = lax.ppermute(array, axis, inside)
    return across, beside


VMEM = pl.BlockSpec(memory_space=pltpu.VMEM)
SMEM = pl.BlockSpec(memory_space=pltpu.SMEM)


def on_device(features, w_conv, bias_in, w_out, bias_out):
    channels, shard_rows, width = features.shape
    layers, _, inner, _ = w_conv.shape
    size = lax.axis_size("row")
    device = lax.axis_index("row")
    place = jnp.stack([device % 2, device * shard_rows, jnp.int32(shard_rows * size)])

    across, beside = neighbours(features, "row")
    kernels = w_conv.transpose(0, 2, 1, 3).reshape(layers, inner, 9 * channels)
    swapped = w_conv[DEPTH : 2 * DEPTH].reshape(DEPTH, 3, 3, inner, channels).transpose(0, 3, 2, 1, 4)
    swapped = swapped.reshape(DEPTH, inner, 9 * channels)
    bias_in = bias_in[:, :, None]
    bias_out = bias_out[:, :, None]

    stack = pltpu.VMEM((3 * shard_rows, 3 * channels, width), jnp.bfloat16)
    params = pltpu.CompilerParams(vmem_limit_bytes=56 * 1024 * 1024)
    one = pl.pallas_call(
        section_one,
        out_shape=jax.ShapeDtypeStruct((shard_rows, channels, width), jnp.bfloat16),
        in_specs=[SMEM] + [VMEM] * 7,
        out_specs=VMEM,
        scratch_shapes=[pltpu.VMEM((3, width // LANES, channels * shard_rows, LANES), jnp.float32), stack, stack],
        compiler_params=params,
        name="section_one",
    )
    field = one(place, features, across, beside, kernels[:DEPTH], bias_in[:DEPTH], w_out[:DEPTH], bias_out[:DEPTH])

    tiles = field.reshape(shard_rows, channels, size, shard_rows).transpose(2, 3, 0, 1)
    tiles = tiles.reshape(size, shard_rows, shard_rows * channels)
    received = lax.all_to_all(tiles, "row", split_axis=0, concat_axis=0, tiled=True)
    flipped = received.reshape(size, shard_rows, shard_rows, channels).transpose(1, 3, 0, 2)
    flipped = flipped.reshape(shard_rows, channels, width)
    field = ((field.astype(jnp.float32) + flipped.astype(jnp.float32)) * 0.5).astype(jnp.bfloat16)

    across, beside = neighbours(field, "row")
    two = pl.pallas_call(
        section_two,
        out_shape=jax.ShapeDtypeStruct((shard_rows, channels, width), jnp.bfloat16),
        in_specs=[SMEM] + [VMEM] * 8,
        out_specs=VMEM,
        scratch_shapes=[stack] * 5,
        compiler_params=params,
        name="section_two",
    )
    out = two(
        place, field, across, beside, kernels[DEPTH:], swapped, bias_in[DEPTH:], w_out[DEPTH:], bias_out[DEPTH:]
    )
    return out.transpose(1, 0, 2)


def solution(mesh):
    in_specs = (P("groups", "row", None), P(), P(), P(), P())
    out_specs = P("groups", "row", None)
    return jax.shard_map(
        on_device, mesh=mesh, in_specs=in_specs, out_specs=out_specs, check_vma=False
    )
```

time: 121 us -> 88.5 us (0.73); the launches traced: 119 us -> 88.1 us
  Pallas kernels: 0 us -> 42.3 us
  starting transfers between devices: 33.4 us -> 7.14 us
  waiting for transfers between devices: 25.2 us -> 4.08 us
  blocking collectives: 35.3 us -> 16.9 us
  matrix products: 15.2 us -> 0 us
  local copies, waits for them, and re-layouts: 6.93 us -> 16.7 us
  other arithmetic: 2.28 us -> 0.72 us
    pallas_call x0 -> x2, Pallas kernels: none -> 42.3 us  [the longest x1 25.7 us: on_device(): two(place, field, across, beside, kernels[DEPTH:], swapped, bias_in[DEPTH...]
    ppermute x14 -> x4, starting transfers between devices: 33.4 us -> 7.14 us  [the longest x2 6.99 us: neighbours(): across = lax.ppermute(array, axis, edges)]
    ppermute x14 -> x4, waiting for transfers between devices: 25.2 us -> 4.08 us  [the longest x2 4.08 us: neighbours(): across = lax.ppermute(array, axis, edges)]
    all_to_all x2 -> x1, blocking collectives: 35.3 us -> 16.9 us  [on_device(): lax.all_to_all(tiles, 'row', split_axis=0, concat_axis=0, tiled=True)]
    dot_general x63 -> x0, matrix products: 15.2 us -> none  [the longest x56 12.5 us: conv_rows(): jnp.einsum('hc,crm->hrm', w_conv[layer, row_tap * 3 + col_tap], window, p...]
    slice x7 -> x19, local copies, waits for them, and re-layouts: 0.08 us -> 6.86 us  [the longest x3 1.96 us: on_device(): kernels[:DEPTH]]
    unnamed x7 -> x20, local copies, waits for them, and re-layouts: 1.64 us -> 4.85 us
    transpose x2, local copies, waits for them, and re-layouts: 0.63 us -> 3.07 us  [the longest x1 1.8 us: on_device(): return out.transpose(1, 0, 2)]
  transfers between devices with their start and end apart: 14 -> 4, of which waited for: 7 -> 2; matrix products, arithmetic and copies ran while one was open for 3% -> 10% of each run, Pallas kernels for 0% -> 0%
where the time goes in v1:
time: 88.5 us; the launch traced here: 88.1 us
  Pallas kernels  42.3 us (48%)
  blocking collectives  16.9 us (19%)
  local copies, waits for them, and re-layouts  16.7 us (19%)
  starting transfers between devices  7.14 us (8%)
  waiting for transfers between devices  4.08 us (5%)
    pallas_call x1, Pallas kernels, on_device(): two(place, field, across, beside, kernels[DEPTH:], swapped, bias_in[DEPTH...  25.7 us
    all_to_all x1, blocking collectives, on_device(): lax.all_to_all(tiles, 'row', split_axis=0, concat_axis=0, tiled=True)  16.9 us
    pallas_call x1, Pallas kernels, on_device(): one(place, features, across, beside, kernels[:DEPTH], bias_in[:DEPTH], w_...  16.7 us
    ppermute x2, starting transfers between devices, neighbours(): across = lax.ppermute(array, axis, edges)  6.99 us
    unnamed x20, local copies, waits for them, and re-layouts  4.85 us
    ppermute x2, waiting for transfers between devices, neighbours(): across = lax.ppermute(array, axis, edges)  4.08 us
    slice x3, local copies, waits for them, and re-layouts, on_device(): kernels[:DEPTH]  1.96 us
    transpose x1, local copies, waits for them, and re-layouts, on_device(): return out.transpose(1, 0, 2)  1.8 us
  transfers between devices with their start and end apart: 4, of which 2 were waited for; matrix products, arithmetic and copies ran while one was open for 10% of the time, Pallas kernels for 0%

profile of v1, /device:TPU:1, one launch (start us, length us, event | category | flops | bytes accessed | tf_op | source)
XLA Modules:
  0.0 88.1 jit_solution(16663443958196438493)
XLA Ops:
  0.0 4.5 %collective-permute-start = (bf16[64,8,256]{2,1,0:T(8,128)(2,1)}, bf16[64,8,256]{2,1,0:T(8,128)(2,1)S(1)}, u32[]{:S(2)}, u32[]{:S(2)}) collective-permute-start(bf16[64,8,256]{2,1,0:T(8,128)(2,1)} %own.1), channel_id=1, source_target_pairs={{1,2},{3,4},{5,6},{7,8},{9,10},{11,12},{13,14},{15,16},{17,18},{19... | collective-permute-start | bytes 786440 | tf_op jit(solution)/shard_map/ppermute | solution.py:173
  4.6 1.0 %slice.60 = bf16[3,32,9,64]{3,1,2,0:T(8,128)(2,1)S(1)} slice(bf16[7,32,9,64]{3,1,2,0:T(8,128)(2,1)} %bitcast.28), slice={[0:3], [0:32], [0:9], [0:64]} | slice | bytes 221184 | tf_op jit(solution)/shard_map/slice | solution.py:207
  5.6 0.1 copy.27
  5.7 0.9 %slice.46.w_conv = bf16[3,32,576]{2,1,0:T(8,128)(2,1)} reshape(bf16[3,32,9,64]{3,2,1,0:T(8,128)(2,1)S(1)} %copy.27) | data formatting | bytes 221184 | tf_op jit(solution)/shard_map/slice | solution.py:207
  6.6 0.8 copy.30.bias_out
  7.4 0.7 slice-done
  8.1 0.7 copy.42.w_out
  8.8 0.7 copy.29.bias_in
  9.5 0.7 pad_add_fusion.place
  10.2 0.7 collective-permute-done.across
  10.9 0.7 copy-done.3
  11.6 0.7 copy-done.4
  12.3 16.7 %section_one.1 = bf16[8,64,256]{2,1,0:T(8,128)(2,1)} custom-call(s32[3]{0:T(128)} %pad_add_fusion.place, bf16[64,8,256]{2,1,0:T(8,128)(2,1)} %own.1, bf16[64,8,256]{2,1,0:T(8,128)(2,1)} %copy-done.3, bf16[64,8,256]{2,1,0:T(8,128)(2,1)} %copy-done.4, bf16[3,32,576]{2,1,0:T(8,128)(2,1)} %slice.46.w_conv, f32[3,32,1]{2,1,0:T(8,128)} %copy.29.bias_in, ...), custom_call_target="tpu_custom_call" | custom-call | tf_op jit(solution)/shard_map/section_one/pallas_call | solution.py:207
  29.0 1.3 %copy.41 = bf16[8,64,256]{1,0,2:T(8,128)(2,1)S(1)} copy(bf16[8,64,256]{2,1,0:T(8,128)(2,1)} %section_one.1) | data formatting | bytes 524288 | tf_op jit(solution)/shard_map/transpose | solution.py:209
  30.3 0.3 reshape.26
  30.6 16.9 %all_to_all.5 = bf16[32,8,512]{2,1,0:T(8,128)(2,1)S(1)} all-to-all(bf16[32,8,512]{2,1,0:T(8,128)(2,1)S(1)} %reshape.26), channel_id=1, replica_groups=mesh['groups'=1,'row'=32] {'row'}, dimensions={0} | all-to-all | bytes 524288 | tf_op jit(solution)/shard_map/all_to_all | solution.py:211
  47.5 0.2 reshape.30
  47.8 0.3 copy.34
  48.1 0.6 copy-done
  48.8 2.5 %collective-permute-start.2 = (bf16[8,64,256]{2,1,0:T(8,128)(2,1)S(1)}, bf16[8,64,256]{2,1,0:T(8,128)(2,1)S(1)}, u32[]{:S(2)}, u32[]{:S(2)}) collective-permute-start(bf16[8,64,256]{2,1,0:T(8,128)(2,1)S(1)} %multiply_convert_fusion.own), channel_id=1, source_target_pairs={{1,2},{3,4},{5,6},{7,8},{9,10},{11,12},{13,14},{15,16},{17,18},{19... | collective-permute-start | bytes 786440 | tf_op jit(solution)/shard_map/ppermute | solution.py:173
  51.5 0.2 copy.35
  51.6 1.0 %slice.53.w_conv = bf16[4,32,576]{2,1,0:T(8,128)(2,1)} reshape(bf16[4,32,9,64]{3,2,1,0:T(8,128)(2,1)S(1)} %copy.35) | data formatting | bytes 294912 | tf_op jit(solution)/shard_map/slice | solution.py:227
  52.6 0.2 copy.46
  52.8 0.9 %reshape.28.w_turned = bf16[3,32,576]{2,1,0:T(8,128)(2,1)} reshape(bf16[3,32,3,3,64]{4,3,2,1,0:T(4,128)(2,1)S(1)} %bitcast.27) | data formatting | bytes 221184 | tf_op jit(solution)/shard_map/reshape | solution.py:192
  53.6 0.8 copy.39.bias_out
  54.4 0.7 copy.43.w_out
  55.1 0.7 copy.38.bias_in
  55.9 3.3 %collective-permute-done.2.across = bf16[8,64,256]{2,1,0:T(8,128)(2,1)S(1)} collective-permute-done((bf16[8,64,256]{2,1,0:T(8,128)(2,1)S(1)}, bf16[8,64,256]{2,1,0:T(8,128)(2,1)S(1)}, u32[]{:S(2)}, u32[]{:S(2)}) %collective-permute-start.2) | collective-permute-done | bytes 262176 | tf_op jit(solution)/shard_map/ppermute | solution.py:173
  59.2 0.7 copy-done.5
  59.9 0.7 copy-done.6
  60.6 25.7 %section_two.1 = bf16[8,64,256]{2,1,0:T(8,128)(2,1)} custom-call(s32[3]{0:T(128)} %pad_add_fusion.place, bf16[8,64,256]{2,1,0:T(8,128)(2,1)} %copy-done.2, bf16[8,64,256]{2,1,0:T(8,128)(2,1)} %copy-done.5, bf16[8,64,256]{2,1,0:T(8,128)(2,1)} %copy-done.6, bf16[4,32,576]{2,1,0:T(8,128)(2,1)} %slice.53.w_conv, bf16[3,32,576]{2,1,0:T(8,128)(2,1)} %reshape.28.w_turned, ...), custom_call_target="tpu_custom_call" | custom-call | tf_op jit(solution)/shard_map/section_two/pallas_call | solution.py:226
  86.3 1.8 %copy.40 = bf16[64,8,256]{2,1,0:T(8,128)(2,1)} copy(bf16[64,8,256]{2,0,1:T(8,128)(2,1)} %bitcast.30) | data formatting | bytes 524288 | tf_op jit(solution)/shard_map/transpose | solution.py:229
  (28 shorter events, 0.4 us)
Async XLA Ops:
  0.0 10.9 %collective-permute-start = (bf16[64,8,256]{2,1,0:T(8,128)(2,1)}, bf16[64,8,256]{2,1,0:T(8,128)(2,1)S(1)}, u32[]{:S(2)}, u32[]{:S(2)}) collective-permute-start(bf16[64,8,256]{2,1,0:T(8,128)(2,1)} %own.1), channel_id=1, source_target_pairs={{1,2},{3,4},{5,6},{7,8},{9,10},{11,12},{13,14},{15,16},{17,18},{19... | collective-permute-start | bytes 786440 | tf_op jit(solution)/shard_map/ppermute | solution.py:173
  4.5 6.4 %collective-permute-start.1 = (bf16[64,8,256]{2,1,0:T(8,128)(2,1)}, bf16[64,8,256]{2,1,0:T(8,128)(2,1)S(1)}, u32[]{:S(2)}, u32[]{:S(2)}) collective-permute-start(bf16[64,8,256]{2,1,0:T(8,128)(2,1)} %own.1), channel_id=1, source_target_pairs={{0,1},{1,0},{2,3},{3,2},{4,5},{5,4},{6,7},{7,6},{8,9},{9,8},{10,11... | collective-permute-start | bytes 786440 | tf_op jit(solution)/shard_map/ppermute | solution.py:174
  5.7 0.9 %copy-start.7 = (f32[7,64]{1,0:T(8,128)S(1)}, f32[7,64]{1,0:T(8,128)}, u32[]{:S(2)}) copy-start(f32[7,64]{1,0:T(8,128)} %param.9) | copy-start | bytes 5380
  7.4 0.7 slice-start
  8.1 0.7 copy-start.8
  10.9 0.7 copy-start.3
  11.6 0.7 copy-start.4
  47.8 1.0 %copy-start = (bf16[8,64,256]{2,1,0:T(8,128)(2,1)S(1)}, bf16[8,64,256]{2,1,0:T(8,128)(2,1)}, u32[]{:S(2)}) copy-start(bf16[8,64,256]{2,1,0:T(8,128)(2,1)} %section_one.1) | copy-start | bytes 786436
  48.7 2.7 %copy-start.1 = (bf16[7,9,32,64]{3,2,1,0:T(8,128)(2,1)S(1)}, bf16[7,9,32,64]{3,2,1,0:T(8,128)(2,1)}, u32[]{:S(2)}) copy-start(bf16[7,9,32,64]{3,2,1,0:T(8,128)(2,1)} %param.6) | copy-start | bytes 774148
  48.8 2.6 %copy-start.2 = (bf16[8,64,256]{2,1,0:T(8,128)(2,1)}, bf16[8,64,256]{2,1,0:T(8,128)(2,1)S(1)}, u32[]{:S(2)}) copy-start(bf16[8,64,256]{2,1,0:T(8,128)(2,1)S(1)} %multiply_convert_fusion.own) | copy-start | bytes 786436
  48.8 10.4 %collective-permute-start.2 = (bf16[8,64,256]{2,1,0:T(8,128)(2,1)S(1)}, bf16[8,64,256]{2,1,0:T(8,128)(2,1)S(1)}, u32[]{:S(2)}, u32[]{:S(2)}) collective-permute-start(bf16[8,64,256]{2,1,0:T(8,128)(2,1)S(1)} %multiply_convert_fusion.own), channel_id=1, source_target_pairs={{1,2},{3,4},{5,6},{7,8},{9,10},{11,12},{13,14},{15,16},{17,18},{19... | collective-permute-start | bytes 786440 | tf_op jit(solution)/shard_map/ppermute | solution.py:173
  51.3 7.9 %collective-permute-start.3 = (bf16[8,64,256]{2,1,0:T(8,128)(2,1)S(1)}, bf16[8,64,256]{2,1,0:T(8,128)(2,1)S(1)}, u32[]{:S(2)}, u32[]{:S(2)}) collective-permute-start(bf16[8,64,256]{2,1,0:T(8,128)(2,1)S(1)} %multiply_convert_fusion.own), channel_id=1, source_target_pairs={{0,1},{1,0},{2,3},{3,2},{4,5},{5,4},{6,7},{7,6},{8,9},{9,8},{10,11... | collective-permute-start | bytes 786440 | tf_op jit(solution)/shard_map/ppermute | solution.py:174
  53.6 0.8 slice-start.1
  59.2 0.7 copy-start.5
  59.9 0.7 copy-start.6

commit v2 on v0

v2 whole, which is shorter than its diff:
```python
import jax
import jax.numpy as jnp
from jax import lax
from jax.experimental import pallas as pl
from jax.experimental.pallas import tpu as pltpu
from jax.sharding import PartitionSpec as P

SECTIONS = 2
DEPTH = 3

dilations = (1, 2, 4)
LANES = 128
LAG = 2


def column_masks(channels, width, dilation):
    column = lax.broadcasted_iota(jnp.int16, (channels, width), 1)
    return column >= jnp.int16(dilation), column < jnp.int16(width - dilation)


def put_row(stack, index, row, dilation, masks):
    channels, width = row.shape
    zeros = jnp.zeros_like(row)
    stack[index, :channels, :] = jnp.where(masks[0], pltpu.roll(row, dilation, 1), zeros)
    stack[index, channels : 2 * channels, :] = row
    stack[index, 2 * channels :, :] = jnp.where(masks[1], pltpu.roll(row, width - dilation, 1), zeros)


def pairs(rows, dilation):
    covered, starts = set(), []
    for row in range(rows):
        if row not in covered:
            start = row if row + dilation < rows else row - dilation
            starts.append(start)
            covered |= {start, start + dilation}
    return starts


def window(stack, start, dilation, channels):
    parts = []
    for place in range(3):
        for tap in range(4):
            parts.append(stack[start + tap * dilation, place * channels : (place + 1) * channels, :])
    return jnp.concatenate(parts, axis=0)


def spread_conv(banded, slot, w_conv, layer, turned, row_offset):
    inner, channels = w_conv.shape[2], w_conv.shape[3]
    zeros = jnp.zeros((inner, channels), jnp.bfloat16)
    for col_tap in range(3):
        for second in range(2):
            parts = [zeros] * 4
            for row_tap in range(3):
                tap = col_tap * 3 + row_tap if turned else row_tap * 3 + col_tap
                parts[row_tap + second] = w_conv[layer, tap]
            top = row_offset + second * inner
            left = col_tap * 4 * channels
            banded[slot, top : top + inner, left : left + 4 * channels] = jnp.concatenate(parts, axis=1)


def spread_out(doubled, slot, w_out, layer):
    channels, inner = w_out.shape[1], w_out.shape[2]
    block = w_out[layer]
    zeros = jnp.zeros_like(block)
    doubled[slot] = jnp.concatenate(
        [jnp.concatenate([block, zeros], axis=1), jnp.concatenate([zeros, block], axis=1)], axis=0
    )


def as_column(row, copies):
    size = row.shape[1]
    across = lax.broadcasted_iota(jnp.int32, (size, size), 1)
    down = lax.broadcasted_iota(jnp.int32, (size, size), 0)
    spread = jnp.where(across == down, jnp.broadcast_to(row, (size, size)), 0.0)
    column = jnp.sum(spread, axis=1, keepdims=True)
    return jnp.concatenate([column] * copies, axis=0)


def run_block(rows, dilation, hidden_of, finish):
    waiting = []
    for start in pairs(rows, dilation):
        waiting.append((start, hidden_of(start)))
        if len(waiting) > LAG:
            finish(*waiting.pop(0))
    for item in waiting:
        finish(*item)


def conv_hidden(stack, start, dilation, channels, kernel, bias):
    inner = jnp.dot(kernel, window(stack, start, dilation, channels), preferred_element_type=jnp.float32)
    return jnp.maximum(inner + bias, 0.0).astype(jnp.bfloat16)


def two_rows(stack, start, dilation, channels, hidden, kernel, bias):
    blended = jnp.dot(kernel, hidden, preferred_element_type=jnp.float32)
    here = slice(channels, 2 * channels)
    residual = [stack[start + step * dilation, here, :].astype(jnp.float32) for step in (1, 2)]
    total = jnp.concatenate(residual, axis=0) + blended + bias
    return total[:channels], total[channels:]


def masked(row, row_id, map_rows):
    inside = jnp.logical_and(row_id >= 0, row_id < map_rows)
    return jnp.where(inside, row, jnp.zeros_like(row))


def fetch(copies):
    for copy in copies:
        copy.start()
    return copies


def section_one(place, own, across, beside, w_conv, bias_in, w_out, bias_out, out,
                shards, wide, first, second, conv, proj, banded, doubled, sems):
    channels, shard_rows, width = own.shape
    inner = w_out.shape[2]
    odd = place[0]
    blocks = width // LANES
    before = jnp.where(odd == 1, 0, 2)
    weights = fetch([
        pltpu.make_async_copy(w_conv.at[pl.ds(0, DEPTH)], conv, sems.at[0]),
        pltpu.make_async_copy(w_out.at[pl.ds(0, DEPTH)], proj, sems.at[1]),
    ])
    arrays = fetch([
        pltpu.make_async_copy(own, shards.at[1], sems.at[2]),
        pltpu.make_async_copy(beside, shards.at[before], sems.at[3]),
        pltpu.make_async_copy(across, shards.at[2 - before], sems.at[4]),
    ])
    for copy in weights:
        copy.wait()
    for layer in range(DEPTH):
        spread_conv(banded, layer, conv, layer, False, 0)
        spread_out(doubled, layer, proj, layer)
    masks = {dilation: column_masks(channels, width, dilation) for dilation in dilations}
    for copy in arrays:
        copy.wait()

    for slot in range(3):
        whole = shards[slot].astype(jnp.float32).reshape(channels * shard_rows, width)
        for block in range(blocks):
            wide[slot, block] = whole[:, block * LANES : (block + 1) * LANES]
    reach = sum(dilations)
    for index in range(shard_rows + 2 * reach):
        slot, line = divmod(index + shard_rows - reach, shard_rows)
        picked = pl.ds(line, channels, stride=shard_rows)
        row = jnp.concatenate([wide[slot, block, picked, :] for block in range(blocks)], axis=1)
        put_row(first, index, row.astype(jnp.bfloat16), dilations[0], masks[dilations[0]])

    source, target = first, second
    for layer, dilation in enumerate(dilations):
        reach = reach - dilation
        kernel, kernel_out = banded[layer], doubled[layer]
        bias = as_column(bias_in[layer : layer + 1, :], 2)
        bias_2 = as_column(bias_out[layer : layer + 1, :], 2)

        def hidden_of(start):
            return conv_hidden(source, start, dilation, channels, kernel, bias)

        def finish(start, hidden):
            rows = two_rows(source, start, dilation, channels, hidden, kernel_out, bias_2)
            for index, row in zip((start, start + dilation), rows):
                row = row.astype(jnp.bfloat16)
                if layer == DEPTH - 1:
                    out[index] = row
                    continue
                if index < reach or index >= reach + shard_rows:
                    row = masked(row, place[1] - reach + index, place[2])
                put_row(target, index, row, dilations[layer + 1], masks[dilations[layer + 1]])

        run_block(shard_rows + 2 * reach, dilation, hidden_of, finish)
        source, target = target, source


def section_two(place, own, across, beside, w_conv, bias_in, w_out, bias_out, out,
                shards, wide, first, plain, turned, plain_2, turned_2, conv, proj, banded, turned_banded, doubled, sems):
    shard_rows, channels, width = own.shape
    inner = w_out.shape[2]
    odd = place[0]
    blocks = width // LANES
    before = jnp.where(odd == 1, 0, 2)
    weights = fetch([
        pltpu.make_async_copy(w_conv.at[pl.ds(DEPTH, DEPTH + 1)], conv, sems.at[0]),
        pltpu.make_async_copy(w_out.at[pl.ds(DEPTH, DEPTH + 1)], proj, sems.at[1]),
    ])
    arrays = fetch([
        pltpu.make_async_copy(own, shards.at[1], sems.at[2]),
        pltpu.make_async_copy(beside, shards.at[before], sems.at[3]),
        pltpu.make_async_copy(across, shards.at[2 - before], sems.at[4]),
    ])
    for copy in weights:
        copy.wait()
    for layer in range(DEPTH + 1):
        spread_conv(banded, layer, conv, layer, False, 0)
        spread_out(doubled, layer, proj, layer)
        if layer < DEPTH:
            spread_conv(turned_banded, layer, conv, layer, True, 0)
    masks = {dilation: column_masks(channels, width, dilation) for dilation in dilations}
    for copy in arrays:
        copy.wait()

    reach = sum(dilations) + 1
    for index in range(shard_rows + 2 * reach):
        slot, line = divmod(index + shard_rows - reach, shard_rows)
        put_row(first, index, shards[slot, line], dilations[0], masks[dilations[0]])

    sources, targets = (first, first), (plain, turned)
    for layer, dilation in enumerate(dilations):
        reach = reach - dilation
        kernels = (banded[layer], turned_banded[layer])
        kernel_out = doubled[layer]
        bias = as_column(bias_in[DEPTH + layer : DEPTH + layer + 1, :], 2)
        bias_2 = as_column(bias_out[DEPTH + layer : DEPTH + layer + 1, :], 2)

        def hidden_of(start):
            if layer == 0:
                both = conv_hidden(
                    first, start, dilation, channels,
                    jnp.concatenate(kernels, axis=0), jnp.concatenate([bias, bias], axis=0),
                )
                return both[: 2 * inner], both[2 * inner :]
            return tuple(
                conv_hidden(source, start, dilation, channels, kernel, bias)
                for source, kernel in zip(sources, kernels)
            )

        def finish(start, hiddens):
            done = [
                two_rows(source, start, dilation, channels, hidden, kernel_out, bias_2)
                for source, hidden in zip(sources, hiddens)
            ]
            for step, index in enumerate((start, start + dilation)):
                rows = [rows[step].astype(jnp.bfloat16) for rows in done]
                following = dilations[(layer + 1) % DEPTH]
                places = targets
                if layer == DEPTH - 1:
                    rows = [((rows[0].astype(jnp.float32) + rows[1].astype(jnp.float32)) * 0.5).astype(jnp.bfloat16)]
                    places = (first,)
                for row, target in zip(rows, places):
                    if index < reach or index >= reach + shard_rows:
                        row = masked(row, place[1] - reach + index, place[2])
                    put_row(target, index, row, following, masks[following])

        run_block(shard_rows + 2 * reach, dilation, hidden_of, finish)
        sources, targets = targets, (plain_2, turned_2)

    kernel, kernel_out = banded[DEPTH], doubled[DEPTH]
    bias = as_column(bias_in[2 * DEPTH : 2 * DEPTH + 1, :], 2)
    bias_2 = as_column(bias_out[2 * DEPTH : 2 * DEPTH + 1, :], 2)
    dilation = dilations[0]

    def last_hidden(start):
        return conv_hidden(first, start, dilation, channels, kernel, bias)

    def last_finish(start, hidden):
        rows = two_rows(first, start, dilation, channels, hidden, kernel_out, bias_2)
        for index, row in zip((start, start + dilation), rows):
            for block in range(blocks):
                picked = pl.ds(index, channels, stride=shard_rows)
                wide[block, picked, :] = row[:, block * LANES : (block + 1) * LANES]

    run_block(shard_rows, dilation, last_hidden, last_finish)
    whole = jnp.concatenate([wide[block] for block in range(blocks)], axis=1)
    out[...] = whole.reshape(channels, shard_rows, width).astype(jnp.bfloat16)


def neighbours(array, axis):
    size = lax.axis_size(axis)
    inside = [(i, i ^ 1) for i in range(size)]
    edges = [(i, i + 1) for i in range(1, size - 1, 2)]
    edges = edges + [(j, i) for i, j in edges]
    across = lax.ppermute(array, axis, edges)
    beside = lax.ppermute(array, axis, inside)
    return across, beside


VMEM = pl.BlockSpec(memory_space=pltpu.VMEM)
SMEM = pl.BlockSpec(memory_space=pltpu.SMEM)
HBM = pl.BlockSpec(memory_space=pl.ANY)
PARAMS = pltpu.CompilerParams(vmem_limit_bytes=60 * 1024 * 1024)
IN_SPECS = [SMEM, HBM, HBM, HBM, HBM, VMEM, HBM, VMEM]


def call_one(channels, shard_rows, width, inner):
    reach = sum(dilations)

    def stack(rows):
        return pltpu.VMEM((rows, 3 * channels, width), jnp.bfloat16)

    return pl.pallas_call(
        section_one,
        out_shape=jax.ShapeDtypeStruct((shard_rows, channels, width), jnp.bfloat16),
        in_specs=IN_SPECS,
        out_specs=VMEM,
        scratch_shapes=[
            pltpu.VMEM((3, channels, shard_rows, width), jnp.bfloat16),
            pltpu.VMEM((3, width // LANES, channels * shard_rows, LANES), jnp.float32),
            stack(shard_rows + 2 * reach),
            stack(shard_rows + 2 * reach - 2 * dilations[0]),
            pltpu.VMEM((DEPTH, 9, inner, channels), jnp.bfloat16),
            pltpu.VMEM((DEPTH, channels, inner), jnp.bfloat16),
            pltpu.VMEM((DEPTH, 2 * inner, 12 * channels), jnp.bfloat16),
            pltpu.VMEM((DEPTH, 2 * channels, 2 * inner), jnp.bfloat16),
            pltpu.SemaphoreType.DMA((5,)),
        ],
        compiler_params=PARAMS,
        name="section_one",
    )


def call_two(channels, shard_rows, width, inner):
    reach = sum(dilations) + 1

    def stack(rows):
        return pltpu.VMEM((rows, 3 * channels, width), jnp.bfloat16)

    first = shard_rows + 2 * reach
    second = first - 2 * dilations[0]
    third = second - 2 * dilations[1]
    return pl.pallas_call(
        section_two,
        out_shape=jax.ShapeDtypeStruct((channels, shard_rows, width), jnp.bfloat16),
        in_specs=IN_SPECS,
        out_specs=VMEM,
        scratch_shapes=[
            pltpu.VMEM((3, shard_rows, channels, width), jnp.bfloat16),
            pltpu.VMEM((width // LANES, channels * shard_rows, LANES), jnp.float32),
            stack(first), stack(second), stack(second), stack(third), stack(third),
            pltpu.VMEM((DEPTH + 1, 9, inner, channels), jnp.bfloat16),
            pltpu.VMEM((DEPTH + 1, channels, inner), jnp.bfloat16),
            pltpu.VMEM((DEPTH + 1, 2 * inner, 12 * channels), jnp.bfloat16),
            pltpu.VMEM((DEPTH, 2 * inner, 12 * channels), jnp.bfloat16),
            pltpu.VMEM((DEPTH + 1, 2 * channels, 2 * inner), jnp.bfloat16),
            pltpu.SemaphoreType.DMA((5,)),
        ],
        compiler_params=PARAMS,
        name="section_two",
    )


def on_device(features, w_conv, bias_in, w_out, bias_out):
    channels, shard_rows, width = features.shape
    inner = w_conv.shape[2]
    size = lax.axis_size("row")
    device = lax.axis_index("row")
    place = jnp.stack([device % 2, device * shard_rows, jnp.int32(shard_rows * size)])
    weights = (w_conv, bias_in, w_out, bias_out)

    across, beside = neighbours(features, "row")
    field = call_one(channels, shard_rows, width, inner)(place, features, across, beside, *weights)

    tiles = field.reshape(shard_rows, channels, size, shard_rows).transpose(2, 3, 0, 1)
    tiles = tiles.reshape(size, shard_rows, shard_rows * channels)
    received = lax.all_to_all(tiles, "row", split_axis=0, concat_axis=0, tiled=True)
    flipped = received.reshape(size, shard_rows, shard_rows, channels).transpose(1, 3, 0, 2)
    flipped = flipped.reshape(shard_rows, channels, width)
    field = ((field.astype(jnp.float32) + flipped.astype(jnp.float32)) * 0.5).astype(jnp.bfloat16)

    across, beside = neighbours(field, "row")
    return call_two(channels, shard_rows, width, inner)(place, field, across, beside, *weights)


def solution(mesh):
    in_specs = (P("groups", "row", None), P(), P(), P(), P())
    out_specs = P("groups", "row", None)
    return jax.shard_map(
        on_device, mesh=mesh, in_specs=in_specs, out_specs=out_specs, check_vma=False
    )
```

time: 121 us -> 56.7 us (0.47); the launches traced: 119 us -> 56.3 us
  starting transfers between devices: 33.4 us -> 7.56 us
  blocking collectives: 35.3 us -> 16.9 us
  matrix products: 15.2 us -> 0 us
  waiting for transfers between devices: 25.2 us -> 12 us
  Pallas kernels: 0 us -> 12.6 us
  other arithmetic: 2.28 us -> 0.65 us
    ppermute x14 -> x4, starting transfers between devices: 33.4 us -> 7.56 us  [the longest x2 6.82 us: neighbours(): across = lax.ppermute(array, axis, edges)]
    all_to_all x2 -> x1, blocking collectives: 35.3 us -> 16.9 us  [on_device(): lax.all_to_all(tiles, 'row', split_axis=0, concat_axis=0, tiled=True)]
    dot_general x63 -> x0, matrix products: 15.2 us -> none  [the longest x56 12.5 us: conv_rows(): jnp.einsum('hc,crm->hrm', w_conv[layer, row_tap * 3 + col_tap], window, p...]
    ppermute x14 -> x4, waiting for transfers between devices: 25.2 us -> 12 us  [the longest x2 12 us: neighbours(): across = lax.ppermute(array, axis, edges)]
    pallas_call x0 -> x2, Pallas kernels: none -> 12.6 us  [the longest x1 7.02 us: on_device(): call_two(channels, shard_rows, width, inner)]
    unnamed x7 -> x13, local copies, waits for them, and re-layouts: 1.64 us -> 4.3 us
    concatenate x7 -> x0, other arithmetic: 2.14 us -> none  [extended_2(): array = jnp.concatenate([before, array, after], axis=dim)]
    add x2 -> x0, local copies, waits for them, and re-layouts: 1.9 us -> none  [the longest x1 0.95 us: conv_rows(): total_sum + bias_in[layer][:, None, None]]
  transfers between devices with their start and end apart: 14 -> 4, of which waited for: 7 -> 2; matrix products, arithmetic and copies ran while one was open for 3% -> 4% of each run, Pallas kernels for 0% -> 0%
where the time goes in v2:
time: 56.7 us; the launch traced here: 56.3 us
  blocking collectives  16.9 us (30%)
  Pallas kernels  12.6 us (22%)
  waiting for transfers between devices  12 us (21%)
  starting transfers between devices  7.56 us (13%)
  local copies, waits for them, and re-layouts  6.49 us (11%)
  other arithmetic  0.65 us (1%)
    all_to_all x1, blocking collectives, on_device(): lax.all_to_all(tiles, 'row', split_axis=0, concat_axis=0, tiled=True)  16.9 us
    ppermute x2, waiting for transfers between devices, neighbours(): across = lax.ppermute(array, axis, edges)  12 us
    pallas_call x1, Pallas kernels, on_device(): call_two(channels, shard_rows, width, inner)  7.02 us
    ppermute x2, starting transfers between devices, neighbours(): across = lax.ppermute(array, axis, edges)  6.82 us
    pallas_call x1, Pallas kernels, on_device(): call_one(channels, shard_rows, width, inner)  5.57 us
    unnamed x13, local copies, waits for them, and re-layouts  4.3 us
    transpose x1, local copies, waits for them, and re-layouts, on_device(): field.reshape(shard_rows, channels, size, shard_rows).transpose(2, 3, 0, 1)  1.27 us
  transfers between devices with their start and end apart: 4, of which 2 were waited for; matrix products, arithmetic and copies ran while one was open for 4% of the time, Pallas kernels for 0%

profile of v2, /device:TPU:1, one launch (start us, length us, event | category | flops | bytes accessed | tf_op | source)
XLA Modules:
  0.0 56.3 jit_solution(1938500420513116268)
XLA Ops:
  0.0 4.5 %collective-permute-start = (bf16[64,8,256]{2,1,0:T(8,128)(2,1)}, bf16[64,8,256]{2,1,0:T(8,128)(2,1)S(1)}, u32[]{:S(2)}, u32[]{:S(2)}) collective-permute-start(bf16[64,8,256]{2,1,0:T(8,128)(2,1)} %own.1), channel_id=1, source_target_pairs={{1,2},{3,4},{5,6},{7,8},{9,10},{11,12},{13,14},{15,16},{17,18},{19... | collective-permute-start | bytes 786440 | tf_op jit(solution)/shard_map/ppermute | solution.py:271
  4.5 0.1 collective-permute-start.1
  4.6 1.6 %copy.13.w_out = bf16[7,64,32]{2,1,0:T(8,128)(2,1)} copy(bf16[7,64,32]{1,2,0:T(8,128)(2,1)} %param.8) | data formatting | bytes 57344 | tf_op args[3]
  6.2 0.6 %pad_add_fusion.place = s32[3]{0:T(128)} fusion(s32[1]{0:T(128)} %constant.21.clone.1, s32[1]{0:T(128)} %bitcast.1, s32[1]{0:T(128)} %bitcast), kind=kLoop, calls=%fused_computation.2 | loop fusion | flops 6 | bytes 24 | tf_op jit(solution)/shard_map/stack | solution.py:345
  6.8 4.2 %collective-permute-done.across = bf16[64,8,256]{2,1,0:T(8,128)(2,1)S(1)} collective-permute-done((bf16[64,8,256]{2,1,0:T(8,128)(2,1)}, bf16[64,8,256]{2,1,0:T(8,128)(2,1)S(1)}, u32[]{:S(2)}, u32[]{:S(2)}) %collective-permute-start) | collective-permute-done | bytes 262176 | tf_op jit(solution)/shard_map/ppermute | solution.py:271
  10.9 0.0 copy-start.2
  10.9 0.0 collective-permute-done.1.beside
  10.9 0.7 %copy-done.2 = bf16[64,8,256]{2,1,0:T(8,128)(2,1)} copy-done((bf16[64,8,256]{2,1,0:T(8,128)(2,1)}, bf16[64,8,256]{2,1,0:T(8,128)(2,1)S(1)}, u32[]{:S(2)}) %copy-start.2) | copy-done | bytes 262168
  11.6 0.0 copy-start.3
  11.6 0.7 %copy-done.3 = bf16[64,8,256]{2,1,0:T(8,128)(2,1)} copy-done((bf16[64,8,256]{2,1,0:T(8,128)(2,1)}, bf16[64,8,256]{2,1,0:T(8,128)(2,1)S(1)}, u32[]{:S(2)}) %copy-start.3) | copy-done | bytes 262168
  12.3 5.6 %section_one.1 = bf16[8,64,256]{2,1,0:T(8,128)(2,1)} custom-call(s32[3]{0:T(128)} %pad_add_fusion.place, bf16[64,8,256]{2,1,0:T(8,128)(2,1)} %own.1, bf16[64,8,256]{2,1,0:T(8,128)(2,1)} %copy-done.2, bf16[64,8,256]{2,1,0:T(8,128)(2,1)} %copy-done.3, bf16[7,9,32,64]{3,2,1,0:T(8,128)(2,1)} %w_conv.3, f32[7,32]{1,0:T(8,128)} %bias_in.3, ...), custom_call_target="tpu_custom_call" | custom-call | tf_op jit(solution)/shard_map/section_one/pallas_call | solution.py:349
  17.9 1.3 %copy.19 = bf16[8,64,256]{1,0,2:T(8,128)(2,1)S(1)} copy(bf16[8,64,256]{2,1,0:T(8,128)(2,1)} %section_one.1) | data formatting | bytes 524288 | tf_op jit(solution)/shard_map/transpose | solution.py:351
  19.2 0.3 reshape.13
  19.5 16.9 %all_to_all.5 = bf16[32,8,512]{2,1,0:T(8,128)(2,1)S(1)} all-to-all(bf16[32,8,512]{2,1,0:T(8,128)(2,1)S(1)} %reshape.13), channel_id=1, replica_groups=mesh['groups'=1,'row'=32] {'row'}, dimensions={0} | all-to-all | bytes 524288 | tf_op jit(solution)/shard_map/all_to_all | solution.py:353
  36.4 0.2 reshape.15
  36.6 0.1 copy_bitcast_fusion
  36.7 0.0 copy-start
  36.7 0.3 copy.17
  37.0 0.6 %copy-done = bf16[8,64,256]{2,1,0:T(8,128)(2,1)S(1)} copy-done((bf16[8,64,256]{2,1,0:T(8,128)(2,1)S(1)}, bf16[8,64,256]{2,1,0:T(8,128)(2,1)}, u32[]{:S(2)}) %copy-start) | copy-done | bytes 262168
  37.7 0.1 multiply_convert_fusion.own
  37.7 0.0 copy-start.1
  37.7 0.7 %collective-permute-start.3 = (bf16[8,64,256]{2,1,0:T(8,128)(2,1)S(1)}, bf16[8,64,256]{2,1,0:T(8,128)(2,1)S(1)}, u32[]{:S(2)}, u32[]{:S(2)}) collective-permute-start(bf16[8,64,256]{2,1,0:T(8,128)(2,1)S(1)} %multiply_convert_fusion.own), channel_id=1, source_target_pairs={{0,1},{1,0},{2,3},{3,2},{4,5},{5,4},{6,7},{7,6},{8,9},{9,8},{10,11... | collective-permute-start | bytes 786440 | tf_op jit(solution)/shard_map/ppermute | solution.py:272
  38.4 2.3 %collective-permute-start.2 = (bf16[8,64,256]{2,1,0:T(8,128)(2,1)S(1)}, bf16[8,64,256]{2,1,0:T(8,128)(2,1)S(1)}, u32[]{:S(2)}, u32[]{:S(2)}) collective-permute-start(bf16[8,64,256]{2,1,0:T(8,128)(2,1)S(1)} %multiply_convert_fusion.own), channel_id=1, source_target_pairs={{1,2},{3,4},{5,6},{7,8},{9,10},{11,12},{13,14},{15,16},{17,18},{19... | collective-permute-start | bytes 786440 | tf_op jit(solution)/shard_map/ppermute | solution.py:271
  40.7 0.0 collective-permute-done.3.beside
  40.7 0.0 copy-start.4
  40.8 7.8 %collective-permute-done.2.across = bf16[8,64,256]{2,1,0:T(8,128)(2,1)S(1)} collective-permute-done((bf16[8,64,256]{2,1,0:T(8,128)(2,1)S(1)}, bf16[8,64,256]{2,1,0:T(8,128)(2,1)S(1)}, u32[]{:S(2)}, u32[]{:S(2)}) %collective-permute-start.2) | collective-permute-done | bytes 262176 | tf_op jit(solution)/shard_map/ppermute | solution.py:271
  48.6 0.0 copy-done.1
  48.6 0.0 copy-done.4
  48.6 0.0 copy-start.5
  48.6 0.7 %copy-done.5 = bf16[8,64,256]{2,1,0:T(8,128)(2,1)} copy-done((bf16[8,64,256]{2,1,0:T(8,128)(2,1)}, bf16[8,64,256]{2,1,0:T(8,128)(2,1)S(1)}, u32[]{:S(2)}) %copy-start.5) | copy-done | bytes 262168
  49.3 7.0 %section_two.1 = bf16[64,8,256]{2,1,0:T(8,128)(2,1)} custom-call(s32[3]{0:T(128)} %pad_add_fusion.place, bf16[8,64,256]{2,1,0:T(8,128)(2,1)} %copy-done.1, bf16[8,64,256]{2,1,0:T(8,128)(2,1)} %copy-done.5, bf16[8,64,256]{2,1,0:T(8,128)(2,1)} %copy-done.4, bf16[7,9,32,64]{3,2,1,0:T(8,128)(2,1)} %w_conv.3, f32[7,32]{1,0:T(8,128)} %bias_in.3, ...), custom_call_target="tpu_custom_call" | custom-call | tf_op jit(solution)/shard_map/section_two/pallas_call | solution.py:359
Async XLA Ops:
  0.0 10.9 %collective-permute-start = (bf16[64,8,256]{2,1,0:T(8,128)(2,1)}, bf16[64,8,256]{2,1,0:T(8,128)(2,1)S(1)}, u32[]{:S(2)}, u32[]{:S(2)}) collective-permute-start(bf16[64,8,256]{2,1,0:T(8,128)(2,1)} %own.1), channel_id=1, source_target_pairs={{1,2},{3,4},{5,6},{7,8},{9,10},{11,12},{13,14},{15,16},{17,18},{19... | collective-permute-start | bytes 786440 | tf_op jit(solution)/shard_map/ppermute | solution.py:271
  4.5 6.4 %collective-permute-start.1 = (bf16[64,8,256]{2,1,0:T(8,128)(2,1)}, bf16[64,8,256]{2,1,0:T(8,128)(2,1)S(1)}, u32[]{:S(2)}, u32[]{:S(2)}) collective-permute-start(bf16[64,8,256]{2,1,0:T(8,128)(2,1)} %own.1), channel_id=1, source_target_pairs={{0,1},{1,0},{2,3},{3,2},{4,5},{5,4},{6,7},{7,6},{8,9},{9,8},{10,11... | collective-permute-start | bytes 786440 | tf_op jit(solution)/shard_map/ppermute | solution.py:272
  10.9 0.7 %copy-start.2 = (bf16[64,8,256]{2,1,0:T(8,128)(2,1)}, bf16[64,8,256]{2,1,0:T(8,128)(2,1)S(1)}, u32[]{:S(2)}) copy-start(bf16[64,8,256]{2,1,0:T(8,128)(2,1)S(1)} %collective-permute-done.across) | copy-start | bytes 786436
  11.6 0.7 %copy-start.3 = (bf16[64,8,256]{2,1,0:T(8,128)(2,1)}, bf16[64,8,256]{2,1,0:T(8,128)(2,1)S(1)}, u32[]{:S(2)}) copy-start(bf16[64,8,256]{2,1,0:T(8,128)(2,1)S(1)} %collective-permute-done.1.beside) | copy-start | bytes 786436
  36.7 1.0 %copy-start = (bf16[8,64,256]{2,1,0:T(8,128)(2,1)S(1)}, bf16[8,64,256]{2,1,0:T(8,128)(2,1)}, u32[]{:S(2)}) copy-start(bf16[8,64,256]{2,1,0:T(8,128)(2,1)} %section_one.1) | copy-start | bytes 786436
  37.7 10.8 %copy-start.1 = (bf16[8,64,256]{2,1,0:T(8,128)(2,1)}, bf16[8,64,256]{2,1,0:T(8,128)(2,1)S(1)}, u32[]{:S(2)}) copy-start(bf16[8,64,256]{2,1,0:T(8,128)(2,1)S(1)} %multiply_convert_fusion.own) | copy-start | bytes 786436
  37.7 3.0 %collective-permute-start.3 = (bf16[8,64,256]{2,1,0:T(8,128)(2,1)S(1)}, bf16[8,64,256]{2,1,0:T(8,128)(2,1)S(1)}, u32[]{:S(2)}, u32[]{:S(2)}) collective-permute-start(bf16[8,64,256]{2,1,0:T(8,128)(2,1)S(1)} %multiply_convert_fusion.own), channel_id=1, source_target_pairs={{0,1},{1,0},{2,3},{3,2},{4,5},{5,4},{6,7},{7,6},{8,9},{9,8},{10,11... | collective-permute-start | bytes 786440 | tf_op jit(solution)/shard_map/ppermute | solution.py:272
  38.4 10.1 %collective-permute-start.2 = (bf16[8,64,256]{2,1,0:T(8,128)(2,1)S(1)}, bf16[8,64,256]{2,1,0:T(8,128)(2,1)S(1)}, u32[]{:S(2)}, u32[]{:S(2)}) collective-permute-start(bf16[8,64,256]{2,1,0:T(8,128)(2,1)S(1)} %multiply_convert_fusion.own), channel_id=1, source_target_pairs={{1,2},{3,4},{5,6},{7,8},{9,10},{11,12},{13,14},{15,16},{17,18},{19... | collective-permute-start | bytes 786440 | tf_op jit(solution)/shard_map/ppermute | solution.py:271
  40.7 7.8 %copy-start.4 = (bf16[8,64,256]{2,1,0:T(8,128)(2,1)}, bf16[8,64,256]{2,1,0:T(8,128)(2,1)S(1)}, u32[]{:S(2)}) copy-start(bf16[8,64,256]{2,1,0:T(8,128)(2,1)S(1)} %collective-permute-done.3.beside) | copy-start | bytes 786436
  48.6 0.7 %copy-start.5 = (bf16[8,64,256]{2,1,0:T(8,128)(2,1)}, bf16[8,64,256]{2,1,0:T(8,128)(2,1)S(1)}, u32[]{:S(2)}) copy-start(bf16[8,64,256]{2,1,0:T(8,128)(2,1)S(1)} %collective-permute-done.2.across) | copy-start | bytes 786436

commit v3 on v0

v3 whole, which is shorter than its diff:
```python
import jax
import jax.numpy as jnp
from jax import lax
from jax.experimental import pallas as pl
from jax.experimental.pallas import tpu as pltpu
from jax.sharding import PartitionSpec as P

SECTIONS = 2
DEPTH = 3

dilations = (1, 2, 4)
LANES = 128
LAG = 2
F32 = jnp.float32
BF16 = jnp.bfloat16


class Stage:
    def __init__(self, dilation, low, high, early_low, late, early):
        self.dilation, self.low, self.high, self.early_low = dilation, low, high, early_low
        self.late, self.early = late, early
        self.keep = ()


def cover(low, high, limit, dilation):
    covered, starts = set(), []
    for row in range(low, high + 1):
        if row in covered:
            continue
        start = row
        if row + dilation > limit and row - dilation >= low:
            start = row - dilation
        starts.append(start)
        covered |= {start, start + dilation}
    return starts, covered


def plan(shard_rows, steps):
    reach = sum(steps)
    ready = 0
    stages = [Stage(0, -reach, shard_rows - 1 + reach, 0, [], [])]
    for dilation in steps:
        reach, ready = reach - dilation, ready + dilation
        low, high = -reach, shard_rows - 1 + reach
        late, covered = cover(low, min(ready - 1, high), high, dilation)
        early_low = low
        while early_low in covered and early_low <= high:
            early_low += 1
        early = cover(early_low, high, high, dilation)[0] if early_low <= high else []
        stage = Stage(dilation, low, high, early_low, late, early)
        need = min(max(covered) + dilation, stages[-1].high)
        stages[-1].keep = tuple(range(stages[-1].early_low, need + 1))
        stages.append(stage)
    return stages


def column_masks(channels, width, dilation):
    column = lax.broadcasted_iota(jnp.int16, (channels, width), 1)
    return column >= jnp.int16(dilation), column < jnp.int16(width - dilation)


class Stack:
    def __init__(self, ref, base, top, dilation, masks):
        self.ref, self.base, self.top, self.dilation, self.masks = ref, base, top, dilation, masks[dilation]

    def put(self, row, value):
        channels, width = value.shape
        index = row - self.base
        zeros = jnp.zeros_like(value)
        self.ref[index, :channels, :] = jnp.where(self.masks[0], pltpu.roll(value, self.dilation, 1), zeros)
        self.ref[index, channels : 2 * channels, :] = value
        self.ref[index, 2 * channels :, :] = jnp.where(
            self.masks[1], pltpu.roll(value, width - self.dilation, 1), zeros
        )

    def get(self, row, place):
        channels = self.ref.shape[1] // 3
        index = min(row, self.top) - self.base
        return self.ref[index, place * channels : (place + 1) * channels, :]

    def window(self, start):
        return jnp.concatenate(
            [self.get(start + (tap - 1) * self.dilation, place) for place in range(3) for tap in range(4)], axis=0
        )


def spread_conv(banded, slot, w_conv, layer, turned, odd):
    inner, channels = w_conv.shape[2], w_conv.shape[3]
    zeros = jnp.zeros((inner, channels), BF16)
    for col_tap in range(3):
        taps = []
        for row_tap in range(3):
            line = jnp.where(odd == 1, 2 - row_tap, row_tap)
            taps.append(w_conv[layer, col_tap * 3 + line if turned else line * 3 + col_tap])
        left = col_tap * 4 * channels
        banded[slot, :inner, left : left + 4 * channels] = jnp.concatenate(taps + [zeros], axis=1)
        banded[slot, inner:, left : left + 4 * channels] = jnp.concatenate([zeros] + taps, axis=1)


def spread_out(doubled, slot, w_out, layer):
    block = w_out[layer].astype(F32).T.astype(BF16)
    zeros = jnp.zeros_like(block)
    doubled[slot] = jnp.concatenate(
        [jnp.concatenate([block, zeros], axis=1), jnp.concatenate([zeros, block], axis=1)], axis=0
    )


def as_column(row, copies):
    size = row.shape[1]
    across = lax.broadcasted_iota(jnp.int32, (size, size), 1)
    down = lax.broadcasted_iota(jnp.int32, (size, size), 0)
    spread = jnp.where(across == down, jnp.broadcast_to(row, (size, size)), 0.0)
    column = jnp.sum(spread, axis=1, keepdims=True)
    return jnp.concatenate([column] * copies, axis=0)


def run_block(starts, rows, dilation, hidden_of, finish):
    waiting, done = [], set()

    def complete(start, hidden):
        steps = []
        for step, row in enumerate((start, start + dilation)):
            if row in rows and row not in done:
                steps.append((step, row))
                done.add(row)
        finish(start, hidden, steps)

    for start in starts:
        waiting.append((start, hidden_of(start)))
        if len(waiting) > LAG:
            complete(*waiting.pop(0))
    for item in waiting:
        complete(*item)


def conv_hidden(stack, start, kernel, bias):
    inner = jnp.dot(kernel, stack.window(start), preferred_element_type=F32)
    return jnp.maximum(inner + bias, 0.0).astype(BF16)


def two_rows(stack, start, hidden, kernel, bias):
    blended = jnp.dot(kernel, hidden, preferred_element_type=F32)
    residual = [stack.get(start + step * stack.dilation, 1).astype(F32) for step in range(2)]
    total = jnp.concatenate(residual, axis=0) + blended + bias
    channels = total.shape[0] // 2
    return total[:channels], total[channels:]


def fetch(pairs, sems, first):
    copies = [pltpu.make_async_copy(source, target, sems.at[first + i]) for i, (source, target) in enumerate(pairs)]
    for copy in copies:
        copy.start()
    return copies


def position():
    device = lax.axis_index("row")
    size = lax.axis_size("row")
    odd = device % 2
    edge = jnp.logical_or(device == 0, device == size - 1)
    return odd, edge


def line_of(row, shard_rows, odd):
    inside = row % shard_rows
    return jnp.where(odd == 1, shard_rows - 1 - inside, inside)


class Weights:
    def __init__(self, refs, base, layers, turned_layers, odd):
        w_conv, bias_in, w_out, bias_out, conv, proj, banded, turned, doubled, sems = refs
        copies = fetch([(w_conv.at[pl.ds(base, layers)], conv), (w_out.at[pl.ds(base, layers)], proj)], sems, 0)
        for copy in copies:
            copy.wait()
        self.bias, self.bias_out = [], []
        for layer in range(layers):
            spread_conv(banded, layer, conv, layer, False, odd)
            if layer < turned_layers:
                spread_conv(turned, layer, conv, layer, True, odd)
            spread_out(doubled, layer, proj, layer)
            self.bias.append(as_column(bias_in[base + layer : base + layer + 1, :], 2))
            self.bias_out.append(as_column(bias_out[base + layer : base + layer + 1, :], 2))
        self.banded, self.turned, self.doubled = banded, turned, doubled


def block_one(weights, layer, stage, starts, rows, source, store):
    kernel, kernel_out = weights.banded[layer], weights.doubled[layer]

    def hidden_of(start):
        return conv_hidden(source, start, kernel, weights.bias[layer])

    def finish(start, hidden, steps):
        values = two_rows(source, start, hidden, kernel_out, weights.bias_out[layer])
        for step, row in steps:
            store(row, values[step])

    run_block(starts, rows, stage.dilation, hidden_of, finish)


def block_two(weights, layer, stage, starts, rows, sources, store):
    kernels = (weights.banded[layer], weights.turned[layer])
    kernel_out, bias = weights.doubled[layer], weights.bias[layer]

    def hidden_of(start):
        if sources[0] is sources[1]:
            both = conv_hidden(
                sources[0], start, jnp.concatenate(kernels, axis=0), jnp.concatenate([bias, bias], axis=0)
            )
            half = both.shape[0] // 2
            return both[:half], both[half:]
        return tuple(conv_hidden(source, start, kernel, bias) for source, kernel in zip(sources, kernels))

    def finish(start, hiddens, steps):
        values = [
            two_rows(source, start, hidden, kernel_out, weights.bias_out[layer])
            for source, hidden in zip(sources, hiddens)
        ]
        for step, row in steps:
            store(row, [value[step].astype(BF16) for value in values])

    run_block(starts, rows, stage.dilation, hidden_of, finish)


def mean_of(first, second):
    return ((first.astype(F32) + second.astype(F32)) * 0.5).astype(BF16)


def masks_for(channels, width):
    return {dilation: column_masks(channels, width, dilation) for dilation in dilations}


def rows_of_raw(shards, wide, slots, shard_rows, channels, width):
    for slot in slots:
        whole = shards[slot].astype(F32).reshape(channels * shard_rows, width)
        for block in range(width // LANES):
            wide[slot, block] = whole[:, block * LANES : (block + 1) * LANES]


def raw_row(wide, slot, line, shard_rows, channels, width):
    picked = pl.ds(line, channels, stride=shard_rows)
    parts = [wide[slot, block, picked, :] for block in range(width // LANES)]
    return jnp.concatenate(parts, axis=1).astype(BF16)


def one_early(own, beside, w_conv, bias_in, w_out, bias_out, keep,
              shards, wide, stack_0, stack_1, conv, proj, banded, turned, doubled, sems):
    channels, shard_rows, width = own.shape
    odd, _ = position()
    stages = plan(shard_rows, dilations)
    arrays = fetch([(own, shards.at[0]), (beside, shards.at[1])], sems, 2)
    weights = Weights(
        (w_conv, bias_in, w_out, bias_out, conv, proj, banded, turned, doubled, sems), 0, DEPTH - 1, 0, odd
    )
    masks = masks_for(channels, width)
    for copy in arrays:
        copy.wait()
    rows_of_raw(shards, wide, range(2), shard_rows, channels, width)
    place = 0
    refs = (stack_0, stack_1)
    source = Stack(refs[0], 0, stages[0].high, dilations[0], masks)
    for row in range(stages[0].high + 1):
        value = raw_row(wide, row // shard_rows, line_of(row, shard_rows, odd), shard_rows, channels, width)
        source.put(row, value)
        if row in stages[0].keep:
            keep[row] = value
    place = len(stages[0].keep)
    for layer in range(DEPTH - 1):
        stage = stages[layer + 1]
        last = layer == DEPTH - 2
        target = None
        if not last:
            target = Stack(refs[layer + 1], stage.early_low, stage.high, dilations[layer + 1], masks)

        def store(row, value):
            value = value.astype(BF16)
            if target is not None:
                target.put(row, value)
            if row in stage.keep:
                keep[place + stage.keep.index(row)] = value

        block_one(weights, layer, stage, stage.early, range(stage.early_low, stage.high + 1), source, store)
        place += len(stage.keep)
        source = target


def chunks_turned(values, lines):
    values = list(values)
    chunk = lax.broadcasted_iota(jnp.int32, values[0].shape, 1) // lines
    for bit in range(3):
        step = 1 << bit
        clear = ((chunk >> bit) & 1) == 0
        for index in range(8):
            if index & step:
                continue
            first, second = values[index], values[index + step]
            values[index] = jnp.where(clear, first, pltpu.roll(second, lines * step, 1))
            values[index + step] = jnp.where(clear, pltpu.roll(first, LANES - lines * step, 1), second)
    return values


def one_late(across, keep, w_conv, bias_in, w_out, bias_out, out, tiles,
             shards, wide, kept, stack_0, stack_1, stack_2, conv, proj, banded, turned, doubled, sems):
    channels, shard_rows, width = across.shape
    odd, edge = position()
    stages = plan(shard_rows, dilations)
    arrays = fetch([(across, shards.at[0]), (keep, kept)], sems, 2)
    weights = Weights(
        (w_conv, bias_in, w_out, bias_out, conv, proj, banded, turned, doubled, sems), 0, DEPTH, 0, odd
    )
    masks = masks_for(channels, width)
    for copy in arrays:
        copy.wait()
    rows_of_raw(shards, wide, range(1), shard_rows, channels, width)
    refs = (stack_0, stack_1, stack_2)
    place = 0
    source = None
    for layer in range(DEPTH + 1):
        stage = stages[layer]
        target = None
        if layer < DEPTH:
            target = Stack(refs[layer], stage.low, stage.keep[-1], dilations[layer], masks)
            for index, row in enumerate(stage.keep):
                target.put(row, kept[place + index])
            place += len(stage.keep)
        if layer == 0:
            for row in range(stage.low, 0):
                target.put(row, raw_row(wide, 0, line_of(row, shard_rows, odd), shard_rows, channels, width))
        else:
            def store(row, value):
                value = value.astype(BF16)
                if target is None:
                    out[line_of(row, shard_rows, odd)] = value
                    return
                if row < 0:
                    value = jnp.where(edge, jnp.zeros_like(value), value)
                target.put(row, value)

            block_one(weights, layer - 1, stage, stage.late, range(stage.low, stage.early_low), source, store)
        source = target

    half = channels // 2
    low_lanes = lax.broadcasted_iota(jnp.int32, (half, LANES), 1) < LANES // 2
    for block in range(width // LANES):
        values = [out[row, :, block * LANES : (block + 1) * LANES] for row in range(shard_rows)]
        for index, value in enumerate(chunks_turned(values, shard_rows)):
            top, bottom = value[:half], value[half:]
            device = block * 16 + index
            tiles[device] = jnp.where(low_lanes, top, pltpu.roll(bottom, LANES // 2, 1))
            tiles[device + 8] = jnp.where(low_lanes, pltpu.roll(top, LANES // 2, 1), bottom)


def symmetrize(received, field, out, tiles, own, sems):
    shard_rows, channels, width = field.shape
    copies = fetch([(received, tiles), (field, own)], sems, 0)
    half = channels // 2
    low_lanes = lax.broadcasted_iota(jnp.int32, (half, LANES), 1) < LANES // 2
    lane_in = lax.broadcasted_iota(jnp.int32, (LANES, LANES), 0)
    lane_out = lax.broadcasted_iota(jnp.int32, (LANES, LANES), 1)
    size = shard_rows
    turned = (lane_out // (size * size)) * (size * size) + (lane_out % size) * size + (lane_out // size) % size
    swap = jnp.where(lane_in == turned, 1.0, 0.0).astype(BF16)
    for copy in copies:
        copy.wait()
    for block in range(width // LANES):
        values = []
        for index in range(8):
            first, second = tiles[block * 16 + index], tiles[block * 16 + index + 8]
            top = jnp.where(low_lanes, first, pltpu.roll(second, LANES // 2, 1))
            bottom = jnp.where(low_lanes, pltpu.roll(first, LANES // 2, 1), second)
            values += [top, bottom]
        stacked = jnp.concatenate(values, axis=0)
        stacked = jnp.dot(stacked, swap, preferred_element_type=F32).astype(BF16)
        values = [stacked[index * channels : (index + 1) * channels] for index in range(8)]
        lanes = slice(block * LANES, (block + 1) * LANES)
        for row, value in enumerate(chunks_turned(values, shard_rows)):
            out[row, :, lanes] = mean_of(own[row, :, lanes], value)


def two_steps():
    return dilations + (dilations[0],)


def two_early(own, beside, w_conv, bias_in, w_out, bias_out, keep,
              shards, stack_0, plain_1, turned_1, plain_2, turned_2, conv, proj, banded, turned, doubled, sems):
    shard_rows, channels, width = own.shape
    odd, _ = position()
    steps = two_steps()
    stages = plan(shard_rows, steps)
    arrays = fetch([(own, shards.at[0]), (beside, shards.at[1])], sems, 2)
    weights = Weights(
        (w_conv, bias_in, w_out, bias_out, conv, proj, banded, turned, doubled, sems), DEPTH, DEPTH, DEPTH, odd
    )
    masks = masks_for(channels, width)
    for copy in arrays:
        copy.wait()
    source = Stack(stack_0, 0, stages[0].high, steps[0], masks)
    for row in range(stages[0].high + 1):
        value = shards[row // shard_rows, line_of(row, shard_rows, odd)]
        source.put(row, value)
        if row in stages[0].keep:
            keep[row] = value
    place = len(stages[0].keep)
    sources = (source, source)
    for layer, refs in enumerate(((plain_1, turned_1), (plain_2, turned_2), ())):
        stage = stages[layer + 1]
        targets = tuple(Stack(ref, stage.early_low, stage.high, steps[layer + 1], masks) for ref in refs)

        def store(row, values):
            for target, value in zip(targets, values):
                target.put(row, value)
            if row in stage.keep:
                index = stage.keep.index(row)
                if not targets:
                    values = [mean_of(*values)]
                for copy, value in enumerate(values):
                    keep[place + copy * len(stage.keep) + index] = value

        block_two(weights, layer, stage, stage.early, range(stage.early_low, stage.high + 1), sources, store)
        place += len(stage.keep) * max(len(refs), 1)
        sources = targets


def two_late(across, keep, w_conv, bias_in, w_out, bias_out, out,
             shards, wide, kept, stack_0, plain_1, turned_1, plain_2, turned_2, stack_3,
             conv, proj, banded, turned, doubled, sems):
    shard_rows, channels, width = across.shape
    odd, edge = position()
    steps = two_steps()
    stages = plan(shard_rows, steps)
    arrays = fetch([(across, shards), (keep, kept)], sems, 2)
    weights = Weights(
        (w_conv, bias_in, w_out, bias_out, conv, proj, banded, turned, doubled, sems), DEPTH, DEPTH + 1, DEPTH, odd
    )
    masks = masks_for(channels, width)
    for copy in arrays:
        copy.wait()
    place = 0
    sources = None
    for layer, refs in enumerate(((stack_0,), (plain_1, turned_1), (plain_2, turned_2), (stack_3,))):
        stage = stages[layer]
        targets = tuple(Stack(ref, stage.low, stage.keep[-1], steps[layer], masks) for ref in refs)
        for target in targets:
            for index, row in enumerate(stage.keep):
                target.put(row, kept[place + index])
            place += len(stage.keep)
        if layer == 0:
            for row in range(stage.low, 0):
                targets[0].put(row, shards[line_of(row, shard_rows, odd)])
            targets = targets * 2
        else:
            def store(row, values):
                if layer == DEPTH:
                    values = [mean_of(*values)]
                for target, value in zip(targets, values):
                    if row < 0:
                        value = jnp.where(edge, jnp.zeros_like(value), value)
                    target.put(row, value)

            block_two(weights, layer - 1, stage, stage.late, range(stage.low, stage.early_low), sources, store)
        sources = targets

    stage = stages[DEPTH + 1]

    def store_last(row, value):
        picked = pl.ds(line_of(row, shard_rows, odd), channels, stride=shard_rows)
        for block in range(width // LANES):
            wide[block, picked, :] = value[:, block * LANES : (block + 1) * LANES]

    block_one(weights, DEPTH, stage, stage.late, range(stage.low, stage.high + 1), sources[0], store_last)
    whole = jnp.concatenate([wide[block] for block in range(width // LANES)], axis=1)
    out[...] = whole.reshape(channels, shard_rows, width).astype(BF16)


VMEM = pl.BlockSpec(memory_space=pltpu.VMEM)
HBM = pl.BlockSpec(memory_space=pltpu.HBM)
WEIGHT_SPECS = [HBM, VMEM, HBM, VMEM]


class Calls:
    def __init__(self, channels, shard_rows, width, inner, size):
        self.channels, self.shard_rows, self.width, self.inner, self.size = channels, shard_rows, width, inner, size
        self.params = pltpu.CompilerParams(vmem_limit_bytes=(10 + 6 * width // LANES) * 1024 * 1024)
        self.one = plan(shard_rows, dilations)
        self.two = plan(shard_rows, two_steps())

    def stack(self, low, high):
        return pltpu.VMEM((max(high - low + 1, 1), 3 * self.channels, self.width), BF16)

    def early(self, stage):
        return self.stack(stage.early_low, stage.high)

    def late(self, stage):
        return self.stack(stage.low, stage.keep[-1])

    def rows(self, count):
        return (count, self.channels, self.width)

    def weights(self, layers):
        inner, channels = self.inner, self.channels
        return [
            pltpu.VMEM((layers, 9, inner, channels), BF16),
            pltpu.VMEM((layers, inner, channels), BF16),
            pltpu.VMEM((layers, 2 * inner, 12 * channels), BF16),
            pltpu.VMEM((layers, 2 * inner, 12 * channels), BF16),
            pltpu.VMEM((layers, 2 * channels, 2 * inner), BF16),
            pltpu.SemaphoreType.DMA((4,)),
        ]

    def raw(self, shards):
        channels, rows, width = self.channels, self.shard_rows, self.width
        return [
            pltpu.VMEM((shards, channels, rows, width), BF16),
            pltpu.VMEM((shards, width // LANES, channels * rows, LANES), F32),
        ]

    def call(self, body, in_specs, shapes, scratch):
        shapes = [jax.ShapeDtypeStruct(shape, BF16) for shape in shapes]
        single = len(shapes) == 1
        return pl.pallas_call(
            body,
            out_shape=shapes[0] if single else shapes,
            in_specs=in_specs,
            out_specs=VMEM if single else [VMEM] * len(shapes),
            scratch_shapes=scratch,
            compiler_params=self.params,
            name=body.__name__,
        )

    def one_early(self, *args):
        kept = sum(len(stage.keep) for stage in self.one)
        scratch = self.raw(2) + [self.early(self.one[0]), self.early(self.one[1])] + self.weights(DEPTH - 1)
        return self.call(one_early, [HBM, HBM] + WEIGHT_SPECS, [self.rows(kept)], scratch)(*args)

    def one_late(self, *args):
        kept = sum(len(stage.keep) for stage in self.one)
        scratch = self.raw(1) + [pltpu.VMEM(self.rows(kept), BF16)]
        scratch += [self.late(stage) for stage in self.one[:DEPTH]] + self.weights(DEPTH)
        shapes = [self.rows(self.shard_rows), (self.size, self.channels // 2, LANES)]
        return self.call(one_late, [HBM, HBM] + WEIGHT_SPECS, shapes, scratch)(*args)

    def symmetrize(self, *args):
        scratch = [
            pltpu.VMEM((self.size, self.channels // 2, LANES), BF16),
            pltpu.VMEM(self.rows(self.shard_rows), BF16),
            pltpu.SemaphoreType.DMA((2,)),
        ]
        return self.call(symmetrize, [HBM, HBM], [self.rows(self.shard_rows)], scratch)(*args)

    def kept_two(self):
        copies = (1, 2, 2, 1, 0)
        return self.rows(sum(count * len(stage.keep) for count, stage in zip(copies, self.two)))

    def two_early(self, *args):
        scratch = [pltpu.VMEM((2,) + self.rows(self.shard_rows), BF16)]
        scratch += [self.early(self.two[index]) for index in (0, 1, 1, 2, 2)] + self.weights(DEPTH)
        return self.call(two_early, [HBM, HBM] + WEIGHT_SPECS, [self.kept_two()], scratch)(*args)

    def two_late(self, *args):
        channels, rows, width = self.channels, self.shard_rows, self.width
        scratch = [
            pltpu.VMEM(self.rows(rows), BF16),
            pltpu.VMEM((width // LANES, channels * rows, LANES), F32),
            pltpu.VMEM(self.kept_two(), BF16),
        ]
        scratch += [self.late(self.two[index]) for index in (0, 1, 1, 2, 2, 3)] + self.weights(DEPTH + 1)
        return self.call(two_late, [HBM, HBM] + WEIGHT_SPECS, [(channels, rows, width)], scratch)(*args)


def neighbours(array, axis):
    size = lax.axis_size(axis)
    inside = [(i, i ^ 1) for i in range(size)]
    edges = [(i, i + 1) for i in range(1, size - 1, 2)]
    edges = edges + [(j, i) for i, j in edges]
    across = lax.ppermute(array, axis, edges)
    beside = lax.ppermute(array, axis, inside)
    return across, beside


def on_device(features, w_conv, bias_in, w_out, bias_out):
    channels, shard_rows, width = features.shape
    calls = Calls(channels, shard_rows, width, w_conv.shape[2], lax.axis_size("row"))
    weights = (w_conv, bias_in, w_out.transpose(0, 2, 1), bias_out)

    across, beside = neighbours(features, "row")
    keep = calls.one_early(features, beside, *weights)
    field, tiles = calls.one_late(across, keep, *weights)
    received = lax.all_to_all(tiles, "row", split_axis=0, concat_axis=0, tiled=True)
    field = calls.symmetrize(received, field)
    across, beside = neighbours(field, "row")
    keep = calls.two_early(field, beside, *weights)
    return calls.two_late(across, keep, *weights)


def solution(mesh):
    in_specs = (P("groups", "row", None), P(), P(), P(), P())
    out_specs = P("groups", "row", None)
    return jax.shard_map(
        on_device, mesh=mesh, in_specs=in_specs, out_specs=out_specs, check_vma=False
    )
```

time: 121 us -> 47.5 us (0.39); the launches traced: 119 us -> 47.2 us
  starting transfers between devices: 33.4 us -> 7.49 us
  waiting for transfers between devices: 25.2 us -> 4.55 us
  blocking collectives: 35.3 us -> 16.6 us
  matrix products: 15.2 us -> 0 us
  Pallas kernels: 0 us -> 14.3 us
  local copies, waits for them, and re-layouts: 6.93 us -> 4.18 us
  other arithmetic: 2.28 us -> 0 us
    ppermute x14 -> x4, starting transfers between devices: 33.4 us -> 7.49 us  [the longest x2 6.77 us: neighbours(): across = lax.ppermute(array, axis, edges)]
    ppermute x14 -> x4, waiting for transfers between devices: 25.2 us -> 4.55 us  [the longest x2 4.54 us: neighbours(): across = lax.ppermute(array, axis, edges)]
    all_to_all x2 -> x1, blocking collectives: 35.3 us -> 16.6 us  [on_device(): lax.all_to_all(tiles, 'row', split_axis=0, concat_axis=0, tiled=True)]
    dot_general x63 -> x0, matrix products: 15.2 us -> none  [the longest x56 12.5 us: conv_rows(): jnp.einsum('hc,crm->hrm', w_conv[layer, row_tap * 3 + col_tap], window, p...]
    pallas_call x0 -> x5, Pallas kernels: none -> 14.3 us  [the longest x1 4.61 us: two_late(): self.call(two_late, [HBM, HBM] + WEIGHT_SPECS, [(channels, rows, width)],...]
    unnamed x7 -> x14, local copies, waits for them, and re-layouts: 1.64 us -> 4.18 us
    concatenate x7 -> x0, other arithmetic: 2.14 us -> none  [extended_2(): array = jnp.concatenate([before, array, after], axis=dim)]
    add x2 -> x0, local copies, waits for them, and re-layouts: 1.9 us -> none  [the longest x1 0.95 us: conv_rows(): total_sum + bias_in[layer][:, None, None]]
  transfers between devices with their start and end apart: 14 -> 4, of which waited for: 7 -> 1; matrix products, arithmetic and copies ran while one was open for 3% -> 0% of each run, Pallas kernels for 0% -> 12%
where the time goes in v3:
time: 47.5 us; the launch traced here: 47.2 us
  blocking collectives  16.6 us (35%)
  Pallas kernels  14.3 us (30%)
  starting transfers between devices  7.49 us (16%)
  waiting for transfers between devices  4.55 us (10%)
  local copies, waits for them, and re-layouts  4.18 us (9%)
    all_to_all x1, blocking collectives, on_device(): lax.all_to_all(tiles, 'row', split_axis=0, concat_axis=0, tiled=True)  16.6 us
    ppermute x2, starting transfers between devices, neighbours(): across = lax.ppermute(array, axis, edges)  6.77 us
    pallas_call x1, Pallas kernels, two_late(): self.call(two_late, [HBM, HBM] + WEIGHT_SPECS, [(channels, rows, width)],...  4.61 us
    ppermute x2, waiting for transfers between devices, neighbours(): across = lax.ppermute(array, axis, edges)  4.54 us
    unnamed x14, local copies, waits for them, and re-layouts  4.18 us
    pallas_call x1, Pallas kernels, one_late(): self.call(one_late, [HBM, HBM] + WEIGHT_SPECS, shapes, scratch)(*args)  3.58 us
    pallas_call x1, Pallas kernels, two_early(): self.call(two_early, [HBM, HBM] + WEIGHT_SPECS, [self.kept_two()], scratch)  3.25 us
    pallas_call x1, Pallas kernels, one_early(): self.call(one_early, [HBM, HBM] + WEIGHT_SPECS, [self.rows(kept)], scratch)  2.24 us
  transfers between devices with their start and end apart: 4, of which 1 were waited for; matrix products, arithmetic and copies ran while one was open for 0% of the time, Pallas kernels for 12%

profile of v3, /device:TPU:1, one launch (start us, length us, event | category | flops | bytes accessed | tf_op | source)
XLA Modules:
  0.0 47.2 jit_solution(12658469577379636943)
XLA Ops:
  0.0 0.1 collective-permute-start.1
  0.1 4.4 %collective-permute-start = (bf16[64,8,256]{2,1,0:T(8,128)(2,1)}, bf16[64,8,256]{2,1,0:T(8,128)(2,1)S(1)}, u32[]{:S(2)}, u32[]{:S(2)}) collective-permute-start(bf16[64,8,256]{2,1,0:T(8,128)(2,1)} %own.1), channel_id=1, source_target_pairs={{1,2},{3,4},{5,6},{7,8},{9,10},{11,12},{13,14},{15,16},{17,18},{19... | collective-permute-start | bytes 786440 | tf_op jit(solution)/shard_map/ppermute | solution.py:574
  4.5 0.0 collective-permute-done.1.beside
  4.5 0.0 copy-start
  4.5 1.0 %copy-done = bf16[7,9,32,64]{3,2,1,0:T(8,128)(2,1)S(1)} copy-done((bf16[7,9,32,64]{3,2,1,0:T(8,128)(2,1)S(1)}, bf16[7,9,32,64]{3,2,1,0:T(8,128)(2,1)}, u32[]{:S(2)}) %copy-start) | copy-done | bytes 258072
  5.6 0.0 copy-start.2
  5.6 0.8 %copy-done.2 = bf16[7,64,32]{1,2,0:T(8,128)(2,1)S(1)} copy-done((bf16[7,64,32]{1,2,0:T(8,128)(2,1)S(1)}, bf16[7,64,32]{1,2,0:T(8,128)(2,1)}, u32[]{:S(2)}) %copy-start.2) | copy-done | bytes 28696
  6.4 0.0 copy-start.4
  6.4 0.9 %copy-done.4 = bf16[64,8,256]{2,1,0:T(8,128)(2,1)S(1)} copy-done((bf16[64,8,256]{2,1,0:T(8,128)(2,1)S(1)}, bf16[64,8,256]{2,1,0:T(8,128)(2,1)}, u32[]{:S(2)}) %copy-start.4) | copy-done | bytes 262168
  7.3 0.0 copy-start.5
  7.3 0.7 %copy-done.5 = f32[7,32]{1,0:T(8,128)S(1)} copy-done((f32[7,32]{1,0:T(8,128)S(1)}, f32[7,32]{1,0:T(8,128)}, u32[]{:S(2)}) %copy-start.5) | copy-done | bytes 920
  8.0 0.0 copy-start.6
  8.0 0.7 %copy-done.6 = f32[7,64]{1,0:T(8,128)S(1)} copy-done((f32[7,64]{1,0:T(8,128)S(1)}, f32[7,64]{1,0:T(8,128)}, u32[]{:S(2)}) %copy-start.6) | copy-done | bytes 1816
  8.7 0.0 copy-start.1
  8.7 0.0 copy-start.3
  8.7 2.2 %one_early.1.keep = bf16[15,64,256]{2,1,0:T(8,128)(2,1)S(1)} custom-call(bf16[64,8,256]{2,1,0:T(8,128)(2,1)S(1)} %copy-done.4, bf16[64,8,256]{2,1,0:T(8,128)(2,1)S(1)} %collective-permute-done.1.beside, bf16[7,9,32,64]{3,2,1,0:T(8,128)(2,1)S(1)} %copy-done, f32[7,32]{1,0:T(8,128)S(1)} %copy-done.5, bf16[7,32,64]{2,1,0:T(8,128)(2,1)S(1)} %bitcast.1, ...), custom_call_target="tpu_custom_call" | custom-call | tf_op jit(solution)/shard_map/one_early/pallas_call | solution.py:532
  11.0 0.0 collective-permute-done.across
  11.0 0.0 copy-done.1
  11.0 0.0 copy-done.3
  11.0 3.6 %one_late.1 = (bf16[8,64,256]{2,1,0:T(8,128)(2,1)S(1)}, bf16[32,32,128]{2,1,0:T(8,128)(2,1)S(1)}) custom-call(bf16[64,8,256]{2,1,0:T(8,128)(2,1)S(1)} %collective-permute-done.across, bf16[15,64,256]{2,1,0:T(8,128)(2,1)S(1)} %one_early.1.keep, bf16[7,9,32,64]{3,2,1,0:T(8,128)(2,1)S(1)} %copy-done.1, f32[7,32]{1,0:T(8,128)S(1)} %copy-done.5, ...), custom_call_target="tpu_custom_call" | custom-call | tf_op jit(solution)/shard_map/one_late/pallas_call | solution.py:539
  14.6 16.6 %all_to_all.5.received = bf16[32,32,128]{2,1,0:T(8,128)(2,1)S(1)} all-to-all(bf16[32,32,128]{2,1,0:T(8,128)(2,1)S(1)} %get-tuple-element.7), channel_id=1, replica_groups=mesh['groups'=1,'row'=32] {'row'}, dimensions={0} | all-to-all | bytes 524288 | tf_op jit(solution)/shard_map/all_to_all | solution.py:587
  31.1 0.6 %symmetrize.1.own = bf16[8,64,256]{2,1,0:T(8,128)(2,1)S(1)} custom-call(bf16[32,32,128]{2,1,0:T(8,128)(2,1)S(1)} %all_to_all.5.received, bf16[8,64,256]{2,1,0:T(8,128)(2,1)S(1)} %get-tuple-element.8.field), custom_call_target="tpu_custom_call" | custom-call | tf_op jit(solution)/shard_map/symmetrize/pallas_call | solution.py:547
  31.7 0.7 %collective-permute-start.3 = (bf16[8,64,256]{2,1,0:T(8,128)(2,1)S(1)}, bf16[8,64,256]{2,1,0:T(8,128)(2,1)S(1)}, u32[]{:S(2)}, u32[]{:S(2)}) collective-permute-start(bf16[8,64,256]{2,1,0:T(8,128)(2,1)S(1)} %symmetrize.1.own), channel_id=1, source_target_pairs={{0,1},{1,0},{2,3},{3,2},{4,5},{5,4},{6,7},{7,6},{8,9},{9,8},{10,11... | collective-permute-start | bytes 786440 | tf_op jit(solution)/shard_map/ppermute | solution.py:575
  32.4 2.3 %collective-permute-start.2 = (bf16[8,64,256]{2,1,0:T(8,128)(2,1)S(1)}, bf16[8,64,256]{2,1,0:T(8,128)(2,1)S(1)}, u32[]{:S(2)}, u32[]{:S(2)}) collective-permute-start(bf16[8,64,256]{2,1,0:T(8,128)(2,1)S(1)} %symmetrize.1.own), channel_id=1, source_target_pairs={{1,2},{3,4},{5,6},{7,8},{9,10},{11,12},{13,14},{15,16},{17,18},{19... | collective-permute-start | bytes 786440 | tf_op jit(solution)/shard_map/ppermute | solution.py:574
  34.7 0.0 collective-permute-done.3.beside
  34.7 3.3 %two_early.1.keep = bf16[28,64,256]{2,1,0:T(8,128)(2,1)S(1)} custom-call(bf16[8,64,256]{2,1,0:T(8,128)(2,1)S(1)} %symmetrize.1.own, bf16[8,64,256]{2,1,0:T(8,128)(2,1)S(1)} %collective-permute-done.3.beside, bf16[7,9,32,64]{3,2,1,0:T(8,128)(2,1)S(1)} %copy-done.1, f32[7,32]{1,0:T(8,128)S(1)} %copy-done.5, bf16[7,32,64]{2,1,0:T(8,128)(2,1)S(1)} %bitcast.3, ...), custom_call_target="tpu_custom_call" | custom-call | tf_op jit(solution)/shard_map/two_early/pallas_call | solution.py:556
  38.0 4.5 %collective-permute-done.2.across = bf16[8,64,256]{2,1,0:T(8,128)(2,1)S(1)} collective-permute-done((bf16[8,64,256]{2,1,0:T(8,128)(2,1)S(1)}, bf16[8,64,256]{2,1,0:T(8,128)(2,1)S(1)}, u32[]{:S(2)}, u32[]{:S(2)}) %collective-permute-start.2) | collective-permute-done | bytes 262176 | tf_op jit(solution)/shard_map/ppermute | solution.py:574
  42.5 4.6 %two_late.1 = bf16[64,8,256]{2,1,0:T(8,128)(2,1)} custom-call(bf16[8,64,256]{2,1,0:T(8,128)(2,1)S(1)} %collective-permute-done.2.across, bf16[28,64,256]{2,1,0:T(8,128)(2,1)S(1)} %two_early.1.keep, bf16[7,9,32,64]{3,2,1,0:T(8,128)(2,1)S(1)} %copy-done.1, f32[7,32]{1,0:T(8,128)S(1)} %copy-done.5, bf16[7,32,64]{2,1,0:T(8,128)(2,1)S(1)} %bitcast.4, ...), custom_call_target="tpu_custom_call" | custom-call | tf_op jit(solution)/shard_map/two_late/pallas_call | solution.py:566
Async XLA Ops:
  0.0 4.5 %collective-permute-start.1 = (bf16[64,8,256]{2,1,0:T(8,128)(2,1)}, bf16[64,8,256]{2,1,0:T(8,128)(2,1)S(1)}, u32[]{:S(2)}, u32[]{:S(2)}) collective-permute-start(bf16[64,8,256]{2,1,0:T(8,128)(2,1)} %own.1), channel_id=1, source_target_pairs={{0,1},{1,0},{2,3},{3,2},{4,5},{5,4},{6,7},{7,6},{8,9},{9,8},{10,11... | collective-permute-start | bytes 786440 | tf_op jit(solution)/shard_map/ppermute | solution.py:575
  0.1 10.9 %collective-permute-start = (bf16[64,8,256]{2,1,0:T(8,128)(2,1)}, bf16[64,8,256]{2,1,0:T(8,128)(2,1)S(1)}, u32[]{:S(2)}, u32[]{:S(2)}) collective-permute-start(bf16[64,8,256]{2,1,0:T(8,128)(2,1)} %own.1), channel_id=1, source_target_pairs={{1,2},{3,4},{5,6},{7,8},{9,10},{11,12},{13,14},{15,16},{17,18},{19... | collective-permute-start | bytes 786440 | tf_op jit(solution)/shard_map/ppermute | solution.py:574
  4.5 1.0 %copy-start = (bf16[7,9,32,64]{3,2,1,0:T(8,128)(2,1)S(1)}, bf16[7,9,32,64]{3,2,1,0:T(8,128)(2,1)}, u32[]{:S(2)}) copy-start(bf16[7,9,32,64]{3,2,1,0:T(8,128)(2,1)} %w_conv.7) | copy-start | bytes 774148
  5.6 0.8 %copy-start.2 = (bf16[7,64,32]{1,2,0:T(8,128)(2,1)S(1)}, bf16[7,64,32]{1,2,0:T(8,128)(2,1)}, u32[]{:S(2)}) copy-start(bf16[7,64,32]{1,2,0:T(8,128)(2,1)} %param.8) | copy-start | bytes 86020
  6.4 0.9 %copy-start.4 = (bf16[64,8,256]{2,1,0:T(8,128)(2,1)S(1)}, bf16[64,8,256]{2,1,0:T(8,128)(2,1)}, u32[]{:S(2)}) copy-start(bf16[64,8,256]{2,1,0:T(8,128)(2,1)} %own.1) | copy-start | bytes 786436
  7.3 0.7 %copy-start.5 = (f32[7,32]{1,0:T(8,128)S(1)}, f32[7,32]{1,0:T(8,128)}, u32[]{:S(2)}) copy-start(f32[7,32]{1,0:T(8,128)} %bias_in.7) | copy-start | bytes 2692
  8.0 0.7 %copy-start.6 = (f32[7,64]{1,0:T(8,128)S(1)}, f32[7,64]{1,0:T(8,128)}, u32[]{:S(2)}) copy-start(f32[7,64]{1,0:T(8,128)} %bias_out.7) | copy-start | bytes 5380
  8.7 2.3 %copy-start.1 = (bf16[7,9,32,64]{3,2,1,0:T(8,128)(2,1)S(1)}, bf16[7,9,32,64]{3,2,1,0:T(8,128)(2,1)}, u32[]{:S(2)}) copy-start(bf16[7,9,32,64]{3,2,1,0:T(8,128)(2,1)} %w_conv.7) | copy-start | bytes 774148
  8.7 2.3 %copy-start.3 = (bf16[7,64,32]{1,2,0:T(8,128)(2,1)S(1)}, bf16[7,64,32]{1,2,0:T(8,128)(2,1)}, u32[]{:S(2)}) copy-start(bf16[7,64,32]{1,2,0:T(8,128)(2,1)} %param.8) | copy-start | bytes 86020
  31.7 3.0 %collective-permute-start.3 = (bf16[8,64,256]{2,1,0:T(8,128)(2,1)S(1)}, bf16[8,64,256]{2,1,0:T(8,128)(2,1)S(1)}, u32[]{:S(2)}, u32[]{:S(2)}) collective-permute-start(bf16[8,64,256]{2,1,0:T(8,128)(2,1)S(1)} %symmetrize.1.own), channel_id=1, source_target_pairs={{0,1},{1,0},{2,3},{3,2},{4,5},{5,4},{6,7},{7,6},{8,9},{9,8},{10,11... | collective-permute-start | bytes 786440 | tf_op jit(solution)/shard_map/ppermute | solution.py:575
  32.4 10.1 %collective-permute-start.2 = (bf16[8,64,256]{2,1,0:T(8,128)(2,1)S(1)}, bf16[8,64,256]{2,1,0:T(8,128)(2,1)S(1)}, u32[]{:S(2)}, u32[]{:S(2)}) collective-permute-start(bf16[8,64,256]{2,1,0:T(8,128)(2,1)S(1)} %symmetrize.1.own), channel_id=1, source_target_pairs={{1,2},{3,4},{5,6},{7,8},{9,10},{11,12},{13,14},{15,16},{17,18},{19... | collective-permute-start | bytes 786440 | tf_op jit(solution)/shard_map/ppermute | solution.py:574

commit v4 on v3

v4 whole, which is shorter than its diff:
```python
import jax
import jax.numpy as jnp
from jax import lax
from jax.experimental import pallas as pl
from jax.experimental.pallas import tpu as pltpu
from jax.sharding import PartitionSpec as P

SECTIONS = 2
DEPTH = 3

dilations = (1, 2, 4)
LANES = 128
LAG = 2
F32 = jnp.float32
BF16 = jnp.bfloat16


class Stage:
    def __init__(self, dilation, low, high, early_low, late, early):
        self.dilation, self.low, self.high, self.early_low = dilation, low, high, early_low
        self.late, self.early = late, early
        self.keep = ()


def cover(low, high, limit, dilation):
    covered, starts = set(), []
    for row in range(low, high + 1):
        if row in covered:
            continue
        start = row
        if row + dilation > limit and row - dilation >= low:
            start = row - dilation
        starts.append(start)
        covered |= {start, start + dilation}
    return starts, covered


def plan(shard_rows, steps):
    reach = sum(steps)
    ready = 0
    stages = [Stage(0, -reach, shard_rows - 1 + reach, 0, [], [])]
    for dilation in steps:
        reach, ready = reach - dilation, ready + dilation
        low, high = -reach, shard_rows - 1 + reach
        late, covered = cover(low, min(ready - 1, high), high, dilation)
        early_low = low
        while early_low in covered and early_low <= high:
            early_low += 1
        early = cover(early_low, high, high, dilation)[0] if early_low <= high else []
        stage = Stage(dilation, low, high, early_low, late, early)
        need = min(max(covered) + dilation, stages[-1].high)
        stages[-1].keep = tuple(range(stages[-1].early_low, need + 1))
        stages.append(stage)
    return stages


def column_masks(channels, width, dilation):
    column = lax.broadcasted_iota(jnp.int16, (channels, width), 1)
    return column >= jnp.int16(dilation), column < jnp.int16(width - dilation)


class Stack:
    def __init__(self, parts, top, dilation, masks):
        self.parts, self.top, self.dilation, self.masks = parts, top, dilation, masks[dilation]

    def find(self, row):
        for ref, base in self.parts:
            if row >= base:
                return ref, row - base
        raise ValueError(row)

    def put(self, row, value):
        channels, width = value.shape
        ref, index = self.find(row)
        zeros = jnp.zeros_like(value)
        ref[index, :channels, :] = jnp.where(self.masks[0], pltpu.roll(value, self.dilation, 1), zeros)
        ref[index, channels : 2 * channels, :] = value
        ref[index, 2 * channels :, :] = jnp.where(
            self.masks[1], pltpu.roll(value, width - self.dilation, 1), zeros
        )

    def get(self, row, place):
        ref, index = self.find(min(row, self.top))
        channels = ref.shape[1] // 3
        return ref[index, place * channels : (place + 1) * channels, :]

    def window(self, start):
        return jnp.concatenate(
            [self.get(start + (tap - 1) * self.dilation, place) for place in range(3) for tap in range(4)], axis=0
        )


def spread_conv(banded, slot, w_conv, layer, turned, odd):
    inner, channels = w_conv.shape[2], w_conv.shape[3]
    zeros = jnp.zeros((inner, channels), BF16)
    for col_tap in range(3):
        taps = []
        for row_tap in range(3):
            line = jnp.where(odd == 1, 2 - row_tap, row_tap)
            taps.append(w_conv[layer, col_tap * 3 + line if turned else line * 3 + col_tap])
        left = col_tap * 4 * channels
        banded[slot, :inner, left : left + 4 * channels] = jnp.concatenate(taps + [zeros], axis=1)
        banded[slot, inner:, left : left + 4 * channels] = jnp.concatenate([zeros] + taps, axis=1)


def spread_out(doubled, slot, w_out, layer):
    block = w_out[layer].astype(F32).T.astype(BF16)
    zeros = jnp.zeros_like(block)
    doubled[slot] = jnp.concatenate(
        [jnp.concatenate([block, zeros], axis=1), jnp.concatenate([zeros, block], axis=1)], axis=0
    )


def as_column(row, copies):
    size = row.shape[1]
    across = lax.broadcasted_iota(jnp.int32, (size, size), 1)
    down = lax.broadcasted_iota(jnp.int32, (size, size), 0)
    spread = jnp.where(across == down, jnp.broadcast_to(row, (size, size)), 0.0)
    column = jnp.sum(spread, axis=1, keepdims=True)
    return jnp.concatenate([column] * copies, axis=0)


def run_block(starts, rows, dilation, hidden_of, finish):
    waiting, done = [], set()

    def complete(start, hidden):
        steps = []
        for step, row in enumerate((start, start + dilation)):
            if row in rows and row not in done:
                steps.append((step, row))
                done.add(row)
        finish(start, hidden, steps)

    for start in starts:
        waiting.append((start, hidden_of(start)))
        if len(waiting) > LAG:
            complete(*waiting.pop(0))
    for item in waiting:
        complete(*item)


def conv_hidden(stack, start, kernel, bias):
    inner = jnp.dot(kernel, stack.window(start), preferred_element_type=F32)
    return jnp.maximum(inner + bias, 0.0).astype(BF16)


def two_rows(stack, start, hidden, kernel, bias):
    blended = jnp.dot(kernel, hidden, preferred_element_type=F32)
    residual = [stack.get(start + step * stack.dilation, 1).astype(F32) for step in range(2)]
    total = jnp.concatenate(residual, axis=0) + blended + bias
    channels = total.shape[0] // 2
    return total[:channels], total[channels:]


def fetch(pairs, sems):
    copies = [pltpu.make_async_copy(source, target, sems.at[i]) for i, (source, target) in enumerate(pairs)]
    for copy in copies:
        copy.start()
    return copies


def position():
    device = lax.axis_index("row")
    size = lax.axis_size("row")
    odd = device % 2
    edge = jnp.logical_or(device == 0, device == size - 1)
    return odd, edge


def line_of(row, shard_rows, odd):
    inside = row % shard_rows
    return jnp.where(odd == 1, shard_rows - 1 - inside, inside)


def prepare(w_conv, bias_in, w_out, bias_out, banded, turned, doubled, bias, bias_last, conv, proj, sems):
    odd, _ = position()
    for copy in fetch([(w_conv, conv), (w_out, proj)], sems):
        copy.wait()
    layers = w_conv.shape[0]
    for layer in range(layers):
        spread_conv(banded, layer, conv, layer, False, odd)
        spread_out(doubled, layer, proj, layer)
        bias[layer] = jnp.broadcast_to(as_column(bias_in[layer : layer + 1, :], 2), bias.shape[1:])
        bias_last[layer] = jnp.broadcast_to(as_column(bias_out[layer : layer + 1, :], 2), bias_last.shape[1:])
    for layer in range(turned.shape[0]):
        spread_conv(turned, layer, conv, layers - 1 - DEPTH + layer, True, odd)


class Weights:
    def __init__(self, refs, base, width):
        self.refs, self.base, self.blocks = refs, base, width // LANES

    def conv(self, layer):
        return self.refs[0][self.base + layer]

    def conv_turned(self, layer):
        return self.refs[1][layer]

    def out(self, layer):
        return self.refs[2][self.base + layer]

    def bias(self, layer):
        return jnp.concatenate([self.refs[3][self.base + layer]] * self.blocks, axis=1)

    def bias_out(self, layer):
        return jnp.concatenate([self.refs[4][self.base + layer]] * self.blocks, axis=1)


def block_one(weights, layer, stage, starts, rows, source, store):
    kernel, kernel_out = weights.conv(layer), weights.out(layer)
    bias, bias_out = weights.bias(layer), weights.bias_out(layer)

    def hidden_of(start):
        return conv_hidden(source, start, kernel, bias)

    def finish(start, hidden, steps):
        values = two_rows(source, start, hidden, kernel_out, bias_out)
        for step, row in steps:
            store(row, values[step])

    run_block(starts, rows, stage.dilation, hidden_of, finish)


def block_two(weights, layer, stage, starts, rows, sources, store):
    kernels = (weights.conv(layer), weights.conv_turned(layer))
    kernel_out, bias, bias_out = weights.out(layer), weights.bias(layer), weights.bias_out(layer)

    def hidden_of(start):
        if sources[0] is sources[1]:
            both = conv_hidden(
                sources[0], start, jnp.concatenate(kernels, axis=0), jnp.concatenate([bias, bias], axis=0)
            )
            half = both.shape[0] // 2
            return both[:half], both[half:]
        return tuple(conv_hidden(source, start, kernel, bias) for source, kernel in zip(sources, kernels))

    def finish(start, hiddens, steps):
        values = [
            two_rows(source, start, hidden, kernel_out, bias_out)
            for source, hidden in zip(sources, hiddens)
        ]
        for step, row in steps:
            store(row, [value[step].astype(BF16) for value in values])

    run_block(starts, rows, stage.dilation, hidden_of, finish)


def mean_of(first, second):
    return ((first.astype(F32) + second.astype(F32)) * 0.5).astype(BF16)


def masks_for(channels, width):
    return {dilation: column_masks(channels, width, dilation) for dilation in dilations}


def rows_of_raw(shards, wide, shard_rows, channels, width):
    for slot, shard in enumerate(shards):
        whole = shard[...].astype(F32).reshape(channels * shard_rows, width)
        for block in range(width // LANES):
            wide[slot, block] = whole[:, block * LANES : (block + 1) * LANES]


def raw_row(wide, slot, line, shard_rows, channels, width):
    picked = pl.ds(line, channels, stride=shard_rows)
    parts = [wide[slot, block, picked, :] for block in range(width // LANES)]
    return jnp.concatenate(parts, axis=1).astype(BF16)


def one_early(own, beside, *refs):
    weight_refs, (stack_0, stack_1, stack_2, wide) = refs[:5], refs[5:]
    channels, shard_rows, width = own.shape
    odd, _ = position()
    stages = plan(shard_rows, dilations)
    weights = Weights(weight_refs, 0, width)
    masks = masks_for(channels, width)
    rows_of_raw((own, beside), wide, shard_rows, channels, width)
    stacks = [
        Stack([(ref, stage.early_low)], stage.high, dilation, masks)
        for ref, stage, dilation in zip((stack_0, stack_1, stack_2), stages, dilations)
    ]
    for row in range(stages[0].high + 1):
        line = line_of(row, shard_rows, odd)
        stacks[0].put(row, raw_row(wide, row // shard_rows, line, shard_rows, channels, width))
    for layer in range(DEPTH - 1):
        stage = stages[layer + 1]

        def store(row, value):
            stacks[layer + 1].put(row, value.astype(BF16))

        block_one(weights, layer, stage, stage.early, range(stage.early_low, stage.high + 1), stacks[layer], store)


def chunks_turned(values, lines):
    values = list(values)
    chunk = lax.broadcasted_iota(jnp.int32, values[0].shape, 1) // lines
    for bit in range(3):
        step = 1 << bit
        clear = ((chunk >> bit) & 1) == 0
        for index in range(8):
            if index & step:
                continue
            first, second = values[index], values[index + step]
            values[index] = jnp.where(clear, first, pltpu.roll(second, lines * step, 1))
            values[index + step] = jnp.where(clear, pltpu.roll(first, LANES - lines * step, 1), second)
    return values


def one_late(across, kept_0, kept_1, kept_2, *refs):
    weight_refs, (out, tiles, stack_0, stack_1, stack_2, wide) = refs[:5], refs[5:]
    channels, shard_rows, width = across.shape
    odd, edge = position()
    stages = plan(shard_rows, dilations)
    weights = Weights(weight_refs, 0, width)
    masks = masks_for(channels, width)
    rows_of_raw((across,), wide, shard_rows, channels, width)
    stacks = [
        Stack([(early, stage.early_low), (late, stage.low)], stage.high, dilation, masks)
        for early, late, stage, dilation in zip(
            (kept_0, kept_1, kept_2), (stack_0, stack_1, stack_2), stages, dilations
        )
    ]
    for row in range(stages[0].low, 0):
        stacks[0].put(row, raw_row(wide, 0, line_of(row, shard_rows, odd), shard_rows, channels, width))
    for layer in range(DEPTH):
        stage = stages[layer + 1]

        def store(row, value):
            value = value.astype(BF16)
            if layer == DEPTH - 1:
                out[line_of(row, shard_rows, odd)] = value
                return
            if row < 0:
                value = jnp.where(edge, jnp.zeros_like(value), value)
            stacks[layer + 1].put(row, value)

        block_one(weights, layer, stage, stage.late, range(stage.low, stage.early_low), stacks[layer], store)

    half = channels // 2
    low_lanes = lax.broadcasted_iota(jnp.int32, (half, LANES), 1) < LANES // 2
    for block in range(width // LANES):
        values = [out[row, :, block * LANES : (block + 1) * LANES] for row in range(shard_rows)]
        for index, value in enumerate(chunks_turned(values, shard_rows)):
            top, bottom = value[:half], value[half:]
            device = block * 16 + index
            tiles[device] = jnp.where(low_lanes, top, pltpu.roll(bottom, LANES // 2, 1))
            tiles[device + 8] = jnp.where(low_lanes, pltpu.roll(top, LANES // 2, 1), bottom)


def symmetrize(tiles, own, out):
    shard_rows, channels, width = own.shape
    half = channels // 2
    low_lanes = lax.broadcasted_iota(jnp.int32, (half, LANES), 1) < LANES // 2
    lane_in = lax.broadcasted_iota(jnp.int32, (LANES, LANES), 0)
    lane_out = lax.broadcasted_iota(jnp.int32, (LANES, LANES), 1)
    size = shard_rows
    turned = (lane_out // (size * size)) * (size * size) + (lane_out % size) * size + (lane_out // size) % size
    swap = jnp.where(lane_in == turned, 1.0, 0.0).astype(BF16)
    for block in range(width // LANES):
        values = []
        for index in range(8):
            first, second = tiles[block * 16 + index], tiles[block * 16 + index + 8]
            top = jnp.where(low_lanes, first, pltpu.roll(second, LANES // 2, 1))
            bottom = jnp.where(low_lanes, pltpu.roll(first, LANES // 2, 1), second)
            values += [top, bottom]
        stacked = jnp.concatenate(values, axis=0)
        stacked = jnp.dot(stacked, swap, preferred_element_type=F32).astype(BF16)
        values = [stacked[index * channels : (index + 1) * channels] for index in range(8)]
        lanes = slice(block * LANES, (block + 1) * LANES)
        for row, value in enumerate(chunks_turned(values, shard_rows)):
            out[row, :, lanes] = mean_of(own[row, :, lanes], value)


def two_steps():
    return dilations + (dilations[0],)


LAYERS_OF = (0, 1, 1, 2, 2, 3)


def two_early(own, beside, *refs):
    weight_refs, stack_refs = refs[:5], refs[5:]
    shard_rows, channels, width = own.shape
    odd, _ = position()
    steps = two_steps()
    stages = plan(shard_rows, steps)
    weights = Weights(weight_refs, DEPTH, width)
    masks = masks_for(channels, width)
    stacks = [[], [], [], []]
    for ref, index in zip(stack_refs, LAYERS_OF):
        stacks[index].append(Stack([(ref, stages[index].early_low)], stages[index].high, steps[index], masks))
    for row in range(stages[0].high + 1):
        shard = (own, beside)[row // shard_rows]
        stacks[0][0].put(row, shard[line_of(row, shard_rows, odd)])
    sources = stacks[0] * 2
    for layer in range(DEPTH):
        stage = stages[layer + 1]

        def store(row, values):
            if layer == DEPTH - 1:
                values = [mean_of(*values)]
            for target, value in zip(stacks[layer + 1], values):
                target.put(row, value)

        block_two(weights, layer, stage, stage.early, range(stage.early_low, stage.high + 1), sources, store)
        sources = stacks[layer + 1]


def two_late(across, *refs):
    kept_refs, weight_refs, out, stack_refs, wide = refs[:6], refs[6:11], refs[11], refs[12:18], refs[18]
    shard_rows, channels, width = across.shape
    odd, edge = position()
    steps = two_steps()
    stages = plan(shard_rows, steps)
    weights = Weights(weight_refs, DEPTH, width)
    masks = masks_for(channels, width)
    stacks = [[], [], [], []]
    for early, late, index in zip(kept_refs, stack_refs, LAYERS_OF):
        stage = stages[index]
        stacks[index].append(Stack([(early, stage.early_low), (late, stage.low)], stage.high, steps[index], masks))
    for row in range(stages[0].low, 0):
        stacks[0][0].put(row, across[line_of(row, shard_rows, odd)])
    sources = stacks[0] * 2
    for layer in range(DEPTH):
        stage = stages[layer + 1]

        def store(row, values):
            if layer == DEPTH - 1:
                values = [mean_of(*values)]
            for target, value in zip(stacks[layer + 1], values):
                if row < 0:
                    value = jnp.where(edge, jnp.zeros_like(value), value)
                target.put(row, value)

        block_two(weights, layer, stage, stage.late, range(stage.low, stage.early_low), sources, store)
        sources = stacks[layer + 1]

    stage = stages[DEPTH + 1]

    def store_last(row, value):
        picked = pl.ds(line_of(row, shard_rows, odd), channels, stride=shard_rows)
        for block in range(width // LANES):
            wide[block, picked, :] = value[:, block * LANES : (block + 1) * LANES]

    block_one(weights, DEPTH, stage, stage.late, range(stage.low, stage.high + 1), sources[0], store_last)
    whole = jnp.concatenate([wide[block] for block in range(width // LANES)], axis=1)
    out[...] = whole.reshape(channels, shard_rows, width).astype(BF16)


VMEM = pl.BlockSpec(memory_space=pltpu.VMEM)
ANY = pl.BlockSpec(memory_space=pl.ANY)


class Calls:
    def __init__(self, channels, shard_rows, width, inner, size):
        self.channels, self.shard_rows, self.width, self.inner, self.size = channels, shard_rows, width, inner, size
        self.one = plan(shard_rows, dilations)
        self.two = plan(shard_rows, two_steps())

    def stack(self, low, high):
        return (max(high - low + 1, 1), 3 * self.channels, self.width)

    def early(self, stage):
        return self.stack(stage.early_low, stage.high)

    def late(self, stage):
        return pltpu.VMEM(self.stack(stage.low, stage.early_low - 1), BF16)

    def wide(self, *shards):
        return pltpu.VMEM(shards + (self.width // LANES, self.channels * self.shard_rows, LANES), F32)

    def call(self, body, args, shapes, scratch, specs=None):
        shapes = [shape if isinstance(shape, jax.ShapeDtypeStruct) else jax.ShapeDtypeStruct(shape, BF16) for shape in shapes]
        single = len(shapes) == 1
        return pl.pallas_call(
            body,
            out_shape=shapes[0] if single else shapes,
            in_specs=specs or [VMEM] * len(args),
            out_specs=VMEM if single else [VMEM] * len(shapes),
            scratch_shapes=scratch,
            compiler_params=pltpu.CompilerParams(vmem_limit_bytes=(10 + 6 * self.width // LANES) * 1024 * 1024),
            name=body.__name__,
        )(*args)

    def prepare(self, w_conv, bias_in, w_out, bias_out):
        layers, inner, channels = w_conv.shape[0], self.inner, self.channels
        shapes = [
            (layers, 2 * inner, 12 * channels),
            (DEPTH, 2 * inner, 12 * channels),
            (layers, 2 * channels, 2 * inner),
            jax.ShapeDtypeStruct((layers, 2 * inner, LANES), F32),
            jax.ShapeDtypeStruct((layers, 2 * channels, LANES), F32),
        ]
        scratch = [
            pltpu.VMEM(w_conv.shape, BF16), pltpu.VMEM(w_out.shape, BF16), pltpu.SemaphoreType.DMA((2,)),
        ]
        return self.call(
            prepare, (w_conv, bias_in, w_out, bias_out), shapes, scratch, [ANY, VMEM, ANY, VMEM]
        )

    def one_early(self, *args):
        return self.call(one_early, args, [self.early(stage) for stage in self.one[:DEPTH]], [self.wide(2)])

    def one_late(self, *args):
        shapes = [(self.shard_rows, self.channels, self.width), (self.size, self.channels // 2, LANES)]
        return self.call(one_late, args, shapes, [self.late(stage) for stage in self.one[:DEPTH]] + [self.wide(1)])

    def symmetrize(self, *args):
        return self.call(symmetrize, args, [(self.shard_rows, self.channels, self.width)], [])

    def two_early(self, *args):
        return self.call(two_early, args, [self.early(self.two[index]) for index in LAYERS_OF], [])

    def two_late(self, *args):
        scratch = [self.late(self.two[index]) for index in LAYERS_OF] + [self.wide()]
        return self.call(two_late, args, [(self.channels, self.shard_rows, self.width)], scratch)


def neighbours(array, axis):
    size = lax.axis_size(axis)
    inside = [(i, i ^ 1) for i in range(size)]
    edges = [(i, i + 1) for i in range(1, size - 1, 2)]
    edges = edges + [(j, i) for i, j in edges]
    across = lax.ppermute(array, axis, edges)
    beside = lax.ppermute(array, axis, inside)
    return across, beside


def on_device(features, w_conv, bias_in, w_out, bias_out):
    channels, shard_rows, width = features.shape
    calls = Calls(channels, shard_rows, width, w_conv.shape[2], lax.axis_size("row"))
    across, beside = neighbours(features, "row")
    weights = calls.prepare(w_conv, bias_in, w_out.transpose(0, 2, 1), bias_out)
    kept = calls.one_early(features, beside, *weights)
    field, tiles = calls.one_late(across, *kept, *weights)
    received = lax.all_to_all(tiles, "row", split_axis=0, concat_axis=0, tiled=True)
    field = calls.symmetrize(received, field)
    across, beside = neighbours(field, "row")
    kept = calls.two_early(field, beside, *weights)
    return calls.two_late(across, *kept, *weights)


def solution(mesh):
    in_specs = (P("groups", "row", None), P(), P(), P(), P())
    out_specs = P("groups", "row", None)
    return jax.shard_map(
        on_device, mesh=mesh, in_specs=in_specs, out_specs=out_specs, check_vma=False
    )
```

time: 47.5 us -> 45.5 us (0.958)
  Pallas kernels: 14.3 us -> 12.1 us
  waiting for transfers between devices: 4.55 us -> 5.24 us
  blocking collectives: 16.6 us -> 16 us
    pallas_call x5 -> x6, Pallas kernels: 14.3 us -> 12.1 us  [call(): pl.pallas_call(body, out_shape=shapes[0] if single else shapes, in_specs=...]
    ppermute x2, waiting for transfers between devices: 4.54 us -> 5.23 us  [neighbours(): across = lax.ppermute(array, axis, edges)]
    all_to_all x1, blocking collectives: 16.6 us -> 16 us  [on_device(): lax.all_to_all(tiles, 'row', split_axis=0, concat_axis=0, tiled=True)]
    unnamed x14 -> x10, local copies, waits for them, and re-layouts: 4.18 us -> 4.17 us
where the time goes in v4:
time: 45.5 us; the launch traced here: 45.1 us
  blocking collectives  16 us (35%)
  Pallas kernels  12.1 us (27%)
  starting transfers between devices  7.49 us (16%)
  waiting for transfers between devices  5.24 us (12%)
  local copies, waits for them, and re-layouts  4.17 us (9%)
    all_to_all x1, blocking collectives, on_device(): lax.all_to_all(tiles, 'row', split_axis=0, concat_axis=0, tiled=True)  16 us
    pallas_call x6, Pallas kernels, call(): pl.pallas_call(body, out_shape=shapes[0] if single else shapes, in_specs=...  12.1 us
    ppermute x2, starting transfers between devices, neighbours(): across = lax.ppermute(array, axis, edges)  6.77 us
    ppermute x2, waiting for transfers between devices, neighbours(): across = lax.ppermute(array, axis, edges)  5.23 us
    unnamed x10, local copies, waits for them, and re-layouts  4.17 us
  transfers between devices with their start and end apart: 4, of which 1 were waited for; matrix products, arithmetic and copies ran while one was open for 0% of the time, Pallas kernels for 12%

profile of v4, /device:TPU:1, one launch (start us, length us, event | category | flops | bytes accessed | tf_op | source)
XLA Modules:
  0.0 45.1 jit_solution(1996735652812751197)
XLA Ops:
  0.0 0.1 collective-permute-start.1
  0.1 4.4 %collective-permute-start = (bf16[64,8,256]{2,1,0:T(8,128)(2,1)}, bf16[64,8,256]{2,1,0:T(8,128)(2,1)S(1)}, u32[]{:S(2)}, u32[]{:S(2)}) collective-permute-start(bf16[64,8,256]{2,1,0:T(8,128)(2,1)} %own.1), channel_id=1, source_target_pairs={{1,2},{3,4},{5,6},{7,8},{9,10},{11,12},{13,14},{15,16},{17,18},{19... | collective-permute-start | bytes 786440 | tf_op jit(solution)/shard_map/ppermute | solution.py:523
  4.5 0.0 copy-start
  4.5 1.0 %copy-done = bf16[7,9,32,64]{3,2,1,0:T(8,128)(2,1)S(1)} copy-done((bf16[7,9,32,64]{3,2,1,0:T(8,128)(2,1)S(1)}, bf16[7,9,32,64]{3,2,1,0:T(8,128)(2,1)}, u32[]{:S(2)}) %copy-start) | copy-done | bytes 258072
  5.6 0.0 copy-start.2
  5.6 0.8 %copy-done.2 = bf16[7,64,32]{1,2,0:T(8,128)(2,1)S(1)} copy-done((bf16[7,64,32]{1,2,0:T(8,128)(2,1)S(1)}, bf16[7,64,32]{1,2,0:T(8,128)(2,1)}, u32[]{:S(2)}) %copy-start.2) | copy-done | bytes 28696
  6.4 0.0 copy-start.3
  6.4 0.7 %copy-done.3 = f32[7,32]{1,0:T(8,128)S(1)} copy-done((f32[7,32]{1,0:T(8,128)S(1)}, f32[7,32]{1,0:T(8,128)}, u32[]{:S(2)}) %copy-start.3) | copy-done | bytes 920
  7.1 0.0 copy-start.4
  7.1 0.7 %copy-done.4 = f32[7,64]{1,0:T(8,128)S(1)} copy-done((f32[7,64]{1,0:T(8,128)S(1)}, f32[7,64]{1,0:T(8,128)}, u32[]{:S(2)}) %copy-start.4) | copy-done | bytes 1816
  7.7 1.1 %prepare.1 = (bf16[7,64,768]{2,1,0:T(8,128)(2,1)S(1)}, bf16[3,64,768]{2,1,0:T(8,128)(2,1)S(1)}, bf16[7,128,64]{2,1,0:T(8,128)(2,1)S(1)}, f32[7,64,128]{2,1,0:T(8,128)S(1)}, f32[7,128,128]{2,1,0:T(8,128)S(1)}) custom-call(bf16[7,9,32,64]{3,2,1,0:T(8,128)(2,1)S(1)} %copy-done, f32[7,32]{1,0:T(8,128)S(1)} %copy-done.3, bf16[7,32,64]{2,1,0:T(8,128)(2,1)S(1)} %bitcast.1, ...), custom_call_target="tpu_custom_call" | custom-call | tf_op jit(solution)/shard_map/prepare/pallas_call | solution.py:474
  8.9 0.0 collective-permute-done.1.beside
  8.9 0.0 copy-start.1
  8.9 0.9 %copy-done.1 = bf16[64,8,256]{2,1,0:T(8,128)(2,1)S(1)} copy-done((bf16[64,8,256]{2,1,0:T(8,128)(2,1)S(1)}, bf16[64,8,256]{2,1,0:T(8,128)(2,1)}, u32[]{:S(2)}) %copy-start.1) | copy-done | bytes 262168
  9.9 1.7 %one_early.1 = (bf16[15,192,256]{2,1,0:T(8,128)(2,1)S(1)}, bf16[12,192,256]{2,1,0:T(8,128)(2,1)S(1)}, bf16[8,192,256]{2,1,0:T(8,128)(2,1)S(1)}) custom-call(bf16[64,8,256]{2,1,0:T(8,128)(2,1)S(1)} %copy-done.1, bf16[64,8,256]{2,1,0:T(8,128)(2,1)S(1)} %collective-permute-done.1.beside, bf16[7,64,768]{2,1,0:T(8,128)(2,1)S(1)} %get-tuple-element.21.refs_0_.refs_6_, ...), custom_call_target="tpu_custom_call" | custom-call | tf_op jit(solution)/shard_map/one_early/pallas_call | solution.py:474
  11.5 0.0 collective-permute-done.across
  11.5 2.4 %one_late.1 = (bf16[8,64,256]{2,1,0:T(8,128)(2,1)S(1)}, bf16[32,32,128]{2,1,0:T(8,128)(2,1)S(1)}) custom-call(bf16[64,8,256]{2,1,0:T(8,128)(2,1)S(1)} %collective-permute-done.across, bf16[15,192,256]{2,1,0:T(8,128)(2,1)S(1)} %get-tuple-element.26.kept_0, bf16[12,192,256]{2,1,0:T(8,128)(2,1)S(1)} %get-tuple-element.27.kept_1, ...), custom_call_target="tpu_custom_call" | custom-call | tf_op jit(solution)/shard_map/one_late/pallas_call | solution.py:474
  14.0 16.0 %all_to_all.5.tiles = bf16[32,32,128]{2,1,0:T(8,128)(2,1)S(1)} all-to-all(bf16[32,32,128]{2,1,0:T(8,128)(2,1)S(1)} %get-tuple-element.29), channel_id=1, replica_groups=mesh['groups'=1,'row'=32] {'row'}, dimensions={0} | all-to-all | bytes 524288 | tf_op jit(solution)/shard_map/all_to_all | solution.py:535
  30.0 0.5 %symmetrize.1.own = bf16[8,64,256]{2,1,0:T(8,128)(2,1)S(1)} custom-call(bf16[32,32,128]{2,1,0:T(8,128)(2,1)S(1)} %all_to_all.5.tiles, bf16[8,64,256]{2,1,0:T(8,128)(2,1)S(1)} %get-tuple-element.30.own), custom_call_target="tpu_custom_call" | custom-call | tf_op jit(solution)/shard_map/symmetrize/pallas_call | solution.py:474
  30.5 0.7 %collective-permute-start.3 = (bf16[8,64,256]{2,1,0:T(8,128)(2,1)S(1)}, bf16[8,64,256]{2,1,0:T(8,128)(2,1)S(1)}, u32[]{:S(2)}, u32[]{:S(2)}) collective-permute-start(bf16[8,64,256]{2,1,0:T(8,128)(2,1)S(1)} %symmetrize.1.own), channel_id=1, source_target_pairs={{0,1},{1,0},{2,3},{3,2},{4,5},{5,4},{6,7},{7,6},{8,9},{9,8},{10,11... | collective-permute-start | bytes 786440 | tf_op jit(solution)/shard_map/ppermute | solution.py:524
  31.2 2.3 %collective-permute-start.2 = (bf16[8,64,256]{2,1,0:T(8,128)(2,1)S(1)}, bf16[8,64,256]{2,1,0:T(8,128)(2,1)S(1)}, u32[]{:S(2)}, u32[]{:S(2)}) collective-permute-start(bf16[8,64,256]{2,1,0:T(8,128)(2,1)S(1)} %symmetrize.1.own), channel_id=1, source_target_pairs={{1,2},{3,4},{5,6},{7,8},{9,10},{11,12},{13,14},{15,16},{17,18},{19... | collective-permute-start | bytes 786440 | tf_op jit(solution)/shard_map/ppermute | solution.py:523
  33.5 0.0 collective-permute-done.3.beside
  33.5 2.6 %two_early.1 = (bf16[16,192,256]{2,1,0:T(8,128)(2,1)S(1)}, bf16[14,192,256]{2,1,0:T(8,128)(2,1)S(1)}, bf16[14,192,256]{2,1,0:T(8,128)(2,1)S(1)}, bf16[10,192,256...) custom-call(bf16[8,64,256]{2,1,0:T(8,128)(2,1)S(1)} %symmetrize.1.own, ...), custom_call_target="tpu_custom_call" | custom-call | tf_op jit(solution)/shard_map/two_early/pallas_call | solution.py:474
  36.1 5.2 %collective-permute-done.2.across = bf16[8,64,256]{2,1,0:T(8,128)(2,1)S(1)} collective-permute-done((bf16[8,64,256]{2,1,0:T(8,128)(2,1)S(1)}, bf16[8,64,256]{2,1,0:T(8,128)(2,1)S(1)}, u32[]{:S(2)}, u32[]{:S(2)}) %collective-permute-start.2) | collective-permute-done | bytes 262176 | tf_op jit(solution)/shard_map/ppermute | solution.py:523
  41.3 3.8 %two_late.1 = bf16[64,8,256]{2,1,0:T(8,128)(2,1)} custom-call(bf16[8,64,256]{2,1,0:T(8,128)(2,1)S(1)} %collective-permute-done.2.across, bf16[16,192,256]{2,1,0:T(8,128)(2,1)S(1)} %get-tuple-element.31.refs_0_, bf16[14,192,256]{2,1,0:T(8,128)(2,1)S(1)} %get-tuple-element.32.refs_1_, bf16[14,192,256]{2,1,0:T(8,128)(2,1)S(1)} %get-tuple-element.33.refs_2_, ...), custom_call_target="tpu_custom_call" | custom-call | tf_op jit(solution)/shard_map/two_late/pallas_call | solution.py:474
Async XLA Ops:
  0.0 8.9 %collective-permute-start.1 = (bf16[64,8,256]{2,1,0:T(8,128)(2,1)}, bf16[64,8,256]{2,1,0:T(8,128)(2,1)S(1)}, u32[]{:S(2)}, u32[]{:S(2)}) collective-permute-start(bf16[64,8,256]{2,1,0:T(8,128)(2,1)} %own.1), channel_id=1, source_target_pairs={{0,1},{1,0},{2,3},{3,2},{4,5},{5,4},{6,7},{7,6},{8,9},{9,8},{10,11... | collective-permute-start | bytes 786440 | tf_op jit(solution)/shard_map/ppermute | solution.py:524
  0.1 11.5 %collective-permute-start = (bf16[64,8,256]{2,1,0:T(8,128)(2,1)}, bf16[64,8,256]{2,1,0:T(8,128)(2,1)S(1)}, u32[]{:S(2)}, u32[]{:S(2)}) collective-permute-start(bf16[64,8,256]{2,1,0:T(8,128)(2,1)} %own.1), channel_id=1, source_target_pairs={{1,2},{3,4},{5,6},{7,8},{9,10},{11,12},{13,14},{15,16},{17,18},{19... | collective-permute-start | bytes 786440 | tf_op jit(solution)/shard_map/ppermute | solution.py:523
  4.5 1.0 %copy-start = (bf16[7,9,32,64]{3,2,1,0:T(8,128)(2,1)S(1)}, bf16[7,9,32,64]{3,2,1,0:T(8,128)(2,1)}, u32[]{:S(2)}) copy-start(bf16[7,9,32,64]{3,2,1,0:T(8,128)(2,1)} %w_conv.1) | copy-start | bytes 774148
  5.6 0.8 %copy-start.2 = (bf16[7,64,32]{1,2,0:T(8,128)(2,1)S(1)}, bf16[7,64,32]{1,2,0:T(8,128)(2,1)}, u32[]{:S(2)}) copy-start(bf16[7,64,32]{1,2,0:T(8,128)(2,1)} %param.8) | copy-start | bytes 86020
  6.4 0.7 %copy-start.3 = (f32[7,32]{1,0:T(8,128)S(1)}, f32[7,32]{1,0:T(8,128)}, u32[]{:S(2)}) copy-start(f32[7,32]{1,0:T(8,128)} %bias_in.1) | copy-start | bytes 2692
  7.1 0.7 %copy-start.4 = (f32[7,64]{1,0:T(8,128)S(1)}, f32[7,64]{1,0:T(8,128)}, u32[]{:S(2)}) copy-start(f32[7,64]{1,0:T(8,128)} %bias_out.1) | copy-start | bytes 5380
  8.9 1.0 %copy-start.1 = (bf16[64,8,256]{2,1,0:T(8,128)(2,1)S(1)}, bf16[64,8,256]{2,1,0:T(8,128)(2,1)}, u32[]{:S(2)}) copy-start(bf16[64,8,256]{2,1,0:T(8,128)(2,1)} %own.1) | copy-start | bytes 786436
  30.5 3.0 %collective-permute-start.3 = (bf16[8,64,256]{2,1,0:T(8,128)(2,1)S(1)}, bf16[8,64,256]{2,1,0:T(8,128)(2,1)S(1)}, u32[]{:S(2)}, u32[]{:S(2)}) collective-permute-start(bf16[8,64,256]{2,1,0:T(8,128)(2,1)S(1)} %symmetrize.1.own), channel_id=1, source_target_pairs={{0,1},{1,0},{2,3},{3,2},{4,5},{5,4},{6,7},{7,6},{8,9},{9,8},{10,11... | collective-permute-start | bytes 786440 | tf_op jit(solution)/shard_map/ppermute | solution.py:524
  31.2 10.1 %collective-permute-start.2 = (bf16[8,64,256]{2,1,0:T(8,128)(2,1)S(1)}, bf16[8,64,256]{2,1,0:T(8,128)(2,1)S(1)}, u32[]{:S(2)}, u32[]{:S(2)}) collective-permute-start(bf16[8,64,256]{2,1,0:T(8,128)(2,1)S(1)} %symmetrize.1.own), channel_id=1, source_target_pairs={{1,2},{3,4},{5,6},{7,8},{9,10},{11,12},{13,14},{15,16},{17,18},{19... | collective-permute-start | bytes 786440 | tf_op jit(solution)/shard_map/ppermute | solution.py:523

commit v5 on v4

--- a/solution.py
+++ b/solution.py
@@ -253,9 +253,9 @@
     return {dilation: column_masks(channels, width, dilation) for dilation in dilations}
 
 
-def rows_of_raw(shards, wide, shard_rows, channels, width):
-    for slot, shard in enumerate(shards):
-        whole = shard[...].astype(F32).reshape(channels * shard_rows, width)
+def rows_of_raw(shards, count, wide, shard_rows, channels, width):
+    for slot in range(count):
+        whole = shards[slot][...].astype(F32).reshape(channels * shard_rows, width)
         for block in range(width // LANES):
             wide[slot, block] = whole[:, block * LANES : (block + 1) * LANES]
 
@@ -266,21 +266,22 @@
     return jnp.concatenate(parts, axis=1).astype(BF16)
 
 
-def one_early(own, beside, *refs):
+def one_early(chip, *refs):
     weight_refs, (stack_0, stack_1, stack_2, wide) = refs[:5], refs[5:]
-    channels, shard_rows, width = own.shape
+    _, channels, shard_rows, width = chip.shape
     odd, _ = position()
     stages = plan(shard_rows, dilations)
     weights = Weights(weight_refs, 0, width)
     masks = masks_for(channels, width)
-    rows_of_raw((own, beside), wide, shard_rows, channels, width)
+    rows_of_raw(chip, 2, wide, shard_rows, channels, width)
     stacks = [
         Stack([(ref, stage.early_low)], stage.high, dilation, masks)
         for ref, stage, dilation in zip((stack_0, stack_1, stack_2), stages, dilations)
     ]
     for row in range(stages[0].high + 1):
         line = line_of(row, shard_rows, odd)
-        stacks[0].put(row, raw_row(wide, row // shard_rows, line, shard_rows, channels, width))
+        slot = jnp.where(odd == 1, 1 - row // shard_rows, row // shard_rows)
+        stacks[0].put(row, raw_row(wide, slot, line, shard_rows, channels, width))
     for layer in range(DEPTH - 1):
         stage = stages[layer + 1]
 
@@ -312,7 +313,7 @@
     stages = plan(shard_rows, dilations)
     weights = Weights(weight_refs, 0, width)
     masks = masks_for(channels, width)
-    rows_of_raw((across,), wide, shard_rows, channels, width)
+    rows_of_raw([across], 1, wide, shard_rows, channels, width)
     stacks = [
         Stack([(early, stage.early_low), (late, stage.low)], stage.high, dilation, masks)
         for early, late, stage, dilation in zip(
@@ -377,9 +378,9 @@
 LAYERS_OF = (0, 1, 1, 2, 2, 3)
 
 
-def two_early(own, beside, *refs):
+def two_early(chip, *refs):
     weight_refs, stack_refs = refs[:5], refs[5:]
-    shard_rows, channels, width = own.shape
+    _, shard_rows, channels, width = chip.shape
     odd, _ = position()
     steps = two_steps()
     stages = plan(shard_rows, steps)
@@ -389,8 +390,8 @@
     for ref, index in zip(stack_refs, LAYERS_OF):
         stacks[index].append(Stack([(ref, stages[index].early_low)], stages[index].high, steps[index], masks))
     for row in range(stages[0].high + 1):
-        shard = (own, beside)[row // shard_rows]
-        stacks[0][0].put(row, shard[line_of(row, shard_rows, odd)])
+        slot = jnp.where(odd == 1, 1 - row // shard_rows, row // shard_rows)
+        stacks[0][0].put(row, chip[slot, line_of(row, shard_rows, odd)])
     sources = stacks[0] * 2
     for layer in range(DEPTH):
         stage = stages[layer + 1]
@@ -517,25 +518,24 @@
 
 def neighbours(array, axis):
     size = lax.axis_size(axis)
-    inside = [(i, i ^ 1) for i in range(size)]
     edges = [(i, i + 1) for i in range(1, size - 1, 2)]
     edges = edges + [(j, i) for i, j in edges]
     across = lax.ppermute(array, axis, edges)
-    beside = lax.ppermute(array, axis, inside)
-    return across, beside
+    chip = lax.all_gather(array, axis, axis_index_groups=[[i, i + 1] for i in range(0, size, 2)])
+    return across, chip
 
 
 def on_device(features, w_conv, bias_in, w_out, bias_out):
     channels, shard_rows, width = features.shape
     calls = Calls(channels, shard_rows, width, w_conv.shape[2], lax.axis_size("row"))
-    across, beside = neighbours(features, "row")
+    across, chip = neighbours(features, "row")
     weights = calls.prepare(w_conv, bias_in, w_out.transpose(0, 2, 1), bias_out)
-    kept = calls.one_early(features, beside, *weights)
+    kept = calls.one_early(chip, *weights)
     field, tiles = calls.one_late(across, *kept, *weights)
     received = lax.all_to_all(tiles, "row", split_axis=0, concat_axis=0, tiled=True)
     field = calls.symmetrize(received, field)
-    across, beside = neighbours(field, "row")
-    kept = calls.two_early(field, beside, *weights)
+    across, chip = neighbours(field, "row")
+    kept = calls.two_early(chip, *weights)
     return calls.two_late(across, *kept, *weights)
 
 

time: 45.5 us -> 45.2 us (level)
  blocking collectives: 16 us -> 19.5 us
  waiting for transfers between devices: 5.24 us -> 3.17 us
  local copies, waits for them, and re-layouts: 4.17 us -> 3.22 us
  starting transfers between devices: 7.49 us -> 6.86 us
    all_gather x0 -> x2, blocking collectives: none -> 4.57 us  [neighbours(): lax.all_gather(array, axis, axis_index_groups=[[i, i + 1] for i in range(...]
    ppermute x2, waiting for transfers between devices: 5.23 us -> 3.17 us  [neighbours(): across = lax.ppermute(array, axis, edges)]
    all_to_all x1, blocking collectives: 16 us -> 14.9 us  [on_device(): lax.all_to_all(tiles, 'row', split_axis=0, concat_axis=0, tiled=True)]
    unnamed x10 -> x8, local copies, waits for them, and re-layouts: 4.17 us -> 3.22 us
    ppermute x2 -> x0, starting transfers between devices: 0.72 us -> none  [neighbours(): beside = lax.ppermute(array, axis, inside)]
  transfers between devices with their start and end apart: 4 -> 2, of which waited for: 1 -> 1; matrix products, arithmetic and copies ran while one was open for 0% -> 0% of each run, Pallas kernels for 12% -> 12%
where the time goes in v5:
time: 45.2 us; the launch traced here: 44.9 us
  blocking collectives  19.5 us (43%)
  Pallas kernels  12.1 us (27%)
  starting transfers between devices  6.86 us (15%)
  local copies, waits for them, and re-layouts  3.22 us (7%)
  waiting for transfers between devices  3.17 us (7%)
    all_to_all x1, blocking collectives, on_device(): lax.all_to_all(tiles, 'row', split_axis=0, concat_axis=0, tiled=True)  14.9 us
    pallas_call x6, Pallas kernels, call(): pl.pallas_call(body, out_shape=shapes[0] if single else shapes, in_specs=...  12.1 us
    ppermute x2, starting transfers between devices, neighbours(): across = lax.ppermute(array, axis, edges)  6.86 us
    all_gather x2, blocking collectives, neighbours(): lax.all_gather(array, axis, axis_index_groups=[[i, i + 1] for i in range(...  4.57 us
    unnamed x8, local copies, waits for them, and re-layouts  3.22 us
    ppermute x2, waiting for transfers between devices, neighbours(): across = lax.ppermute(array, axis, edges)  3.17 us
  transfers between devices with their start and end apart: 2, of which 1 were waited for; matrix products, arithmetic and copies ran while one was open for 0% of the time, Pallas kernels for 12%

profile of v5, /device:TPU:1, one launch (start us, length us, event | category | flops | bytes accessed | tf_op | source)
XLA Modules:
  0.0 44.9 jit_solution(13421837741891089423)
XLA Ops:
  0.0 4.5 %collective-permute-start = (bf16[64,8,256]{2,1,0:T(8,128)(2,1)}, bf16[64,8,256]{2,1,0:T(8,128)(2,1)S(1)}, u32[]{:S(2)}, u32[]{:S(2)}) collective-permute-start(bf16[64,8,256]{2,1,0:T(8,128)(2,1)} %param.5), channel_id=1, source_target_pairs={{1,2},{3,4},{5,6},{7,8},{9,10},{11,12},{13,14},{15,16},{17,18},{19... | collective-permute-start | bytes 786440 | tf_op jit(solution)/shard_map/ppermute | solution.py:523
  4.5 0.0 copy-start
  4.5 1.0 %copy-done = bf16[7,9,32,64]{3,2,1,0:T(8,128)(2,1)S(1)} copy-done((bf16[7,9,32,64]{3,2,1,0:T(8,128)(2,1)S(1)}, bf16[7,9,32,64]{3,2,1,0:T(8,128)(2,1)}, u32[]{:S(2)}) %copy-start) | copy-done | bytes 258072
  5.5 0.0 copy-start.1
  5.5 0.8 %copy-done.1 = bf16[7,64,32]{1,2,0:T(8,128)(2,1)S(1)} copy-done((bf16[7,64,32]{1,2,0:T(8,128)(2,1)S(1)}, bf16[7,64,32]{1,2,0:T(8,128)(2,1)}, u32[]{:S(2)}) %copy-start.1) | copy-done | bytes 28696
  6.4 0.0 copy-start.2
  6.4 0.7 %copy-done.2 = f32[7,32]{1,0:T(8,128)S(1)} copy-done((f32[7,32]{1,0:T(8,128)S(1)}, f32[7,32]{1,0:T(8,128)}, u32[]{:S(2)}) %copy-start.2) | copy-done | bytes 920
  7.1 0.0 copy-start.3
  7.1 0.7 %copy-done.3 = f32[7,64]{1,0:T(8,128)S(1)} copy-done((f32[7,64]{1,0:T(8,128)S(1)}, f32[7,64]{1,0:T(8,128)}, u32[]{:S(2)}) %copy-start.3) | copy-done | bytes 1816
  7.7 1.1 %prepare.1 = (bf16[7,64,768]{2,1,0:T(8,128)(2,1)S(1)}, bf16[3,64,768]{2,1,0:T(8,128)(2,1)S(1)}, bf16[7,128,64]{2,1,0:T(8,128)(2,1)S(1)}, f32[7,64,128]{2,1,0:T(8,128)S(1)}, f32[7,128,128]{2,1,0:T(8,128)S(1)}) custom-call(bf16[7,9,32,64]{3,2,1,0:T(8,128)(2,1)S(1)} %copy-done, f32[7,32]{1,0:T(8,128)S(1)} %copy-done.2, bf16[7,32,64]{2,1,0:T(8,128)(2,1)S(1)} %bitcast.5, ...), custom_call_target="tpu_custom_call" | custom-call | tf_op jit(solution)/shard_map/prepare/pallas_call | solution.py:475
  8.9 2.4 %all-gather = bf16[128,8,256]{2,1,0:T(8,128)(2,1)S(1)} all-gather(bf16[64,8,256]{2,1,0:T(8,128)(2,1)} %param.5), channel_id=2, replica_groups={{0,1},{2,3},{4,5},{6,7},{8,9},{10,11},{12,13},{14,15},{16,17},{18,19},{..., dimensions={0}, use_global_device_ids=true | all-gather | bytes 786432 | tf_op jit(solution)/shard_map/all_gather | solution.py:524
  11.3 1.6 %one_early.1 = (bf16[15,192,256]{2,1,0:T(8,128)(2,1)S(1)}, bf16[12,192,256]{2,1,0:T(8,128)(2,1)S(1)}, bf16[8,192,256]{2,1,0:T(8,128)(2,1)S(1)}) custom-call(bf16[2,64,8,256]{3,2,1,0:T(8,128)(2,1)S(1)} %bitcast.4, bf16[7,64,768]{2,1,0:T(8,128)(2,1)S(1)} %get-tuple-element.21.refs_0_.refs_6_, bf16[3,64,768]{2,1,0:T(8,128)(2,1)S(1)} %get-tuple-element.22.refs_1_.refs_7_, ...), custom_call_target="tpu_custom_call" | custom-call | tf_op jit(solution)/shard_map/one_early/pallas_call | solution.py:475
  12.9 0.0 collective-permute-done.across
  12.9 2.4 %one_late.1 = (bf16[8,64,256]{2,1,0:T(8,128)(2,1)S(1)}, bf16[32,32,128]{2,1,0:T(8,128)(2,1)S(1)}) custom-call(bf16[64,8,256]{2,1,0:T(8,128)(2,1)S(1)} %collective-permute-done.across, bf16[15,192,256]{2,1,0:T(8,128)(2,1)S(1)} %get-tuple-element.26.kept_0, bf16[12,192,256]{2,1,0:T(8,128)(2,1)S(1)} %get-tuple-element.27.kept_1, ...), custom_call_target="tpu_custom_call" | custom-call | tf_op jit(solution)/shard_map/one_late/pallas_call | solution.py:475
  15.4 14.9 %all_to_all.5.tiles = bf16[32,32,128]{2,1,0:T(8,128)(2,1)S(1)} all-to-all(bf16[32,32,128]{2,1,0:T(8,128)(2,1)S(1)} %get-tuple-element.29), channel_id=1, replica_groups=mesh['groups'=1,'row'=32] {'row'}, dimensions={0} | all-to-all | bytes 524288 | tf_op jit(solution)/shard_map/all_to_all | solution.py:535
  30.2 0.5 %symmetrize.1 = bf16[8,64,256]{2,1,0:T(8,128)(2,1)S(1)} custom-call(bf16[32,32,128]{2,1,0:T(8,128)(2,1)S(1)} %all_to_all.5.tiles, bf16[8,64,256]{2,1,0:T(8,128)(2,1)S(1)} %get-tuple-element.30.own), custom_call_target="tpu_custom_call" | custom-call | tf_op jit(solution)/shard_map/symmetrize/pallas_call | solution.py:475
  30.8 2.4 %collective-permute-start.1 = (bf16[8,64,256]{2,1,0:T(8,128)(2,1)S(1)}, bf16[8,64,256]{2,1,0:T(8,128)(2,1)S(1)}, u32[]{:S(2)}, u32[]{:S(2)}) collective-permute-start(bf16[8,64,256]{2,1,0:T(8,128)(2,1)S(1)} %symmetrize.1), channel_id=1, source_target_pairs={{1,2},{3,4},{5,6},{7,8},{9,10},{11,12},{13,14},{15,16},{17,18},{19... | collective-permute-start | bytes 786440 | tf_op jit(solution)/shard_map/ppermute | solution.py:523
  33.1 2.2 %all-gather.1 = bf16[16,64,256]{2,1,0:T(8,128)(2,1)S(1)} all-gather(bf16[8,64,256]{2,1,0:T(8,128)(2,1)S(1)} %symmetrize.1), channel_id=3, replica_groups={{0,1},{2,3},{4,5},{6,7},{8,9},{10,11},{12,13},{14,15},{16,17},{18,19},{..., dimensions={0}, use_global_device_ids=true | all-gather | bytes 786432 | tf_op jit(solution)/shard_map/all_gather | solution.py:524
  35.3 2.5 %two_early.1 = (bf16[16,192,256]{2,1,0:T(8,128)(2,1)S(1)}, bf16[14,192,256]{2,1,0:T(8,128)(2,1)S(1)}, bf16[14,192,256]{2,1,0:T(8,128)(2,1)S(1)}, bf16[10,192,256...) custom-call(bf16[2,8,64,256]{3,2,1,0:T(8,128)(2,1)S(1)} %bitcast.3, ...), custom_call_target="tpu_custom_call" | custom-call | tf_op jit(solution)/shard_map/two_early/pallas_call | solution.py:475
  37.9 3.2 %collective-permute-done.1.across = bf16[8,64,256]{2,1,0:T(8,128)(2,1)S(1)} collective-permute-done((bf16[8,64,256]{2,1,0:T(8,128)(2,1)S(1)}, bf16[8,64,256]{2,1,0:T(8,128)(2,1)S(1)}, u32[]{:S(2)}, u32[]{:S(2)}) %collective-permute-start.1) | collective-permute-done | bytes 262176 | tf_op jit(solution)/shard_map/ppermute | solution.py:523
  41.0 3.8 %two_late.1 = bf16[64,8,256]{2,1,0:T(8,128)(2,1)} custom-call(bf16[8,64,256]{2,1,0:T(8,128)(2,1)S(1)} %collective-permute-done.1.across, bf16[16,192,256]{2,1,0:T(8,128)(2,1)S(1)} %get-tuple-element.31.refs_0_, bf16[14,192,256]{2,1,0:T(8,128)(2,1)S(1)} %get-tuple-element.32.refs_1_, bf16[14,192,256]{2,1,0:T(8,128)(2,1)S(1)} %get-tuple-element.33.refs_2_, ...), custom_call_target="tpu_custom_call" | custom-call | tf_op jit(solution)/shard_map/two_late/pallas_call | solution.py:475
Async XLA Ops:
  0.0 12.9 %collective-permute-start = (bf16[64,8,256]{2,1,0:T(8,128)(2,1)}, bf16[64,8,256]{2,1,0:T(8,128)(2,1)S(1)}, u32[]{:S(2)}, u32[]{:S(2)}) collective-permute-start(bf16[64,8,256]{2,1,0:T(8,128)(2,1)} %param.5), channel_id=1, source_target_pairs={{1,2},{3,4},{5,6},{7,8},{9,10},{11,12},{13,14},{15,16},{17,18},{19... | collective-permute-start | bytes 786440 | tf_op jit(solution)/shard_map/ppermute | solution.py:523
  4.5 1.0 %copy-start = (bf16[7,9,32,64]{3,2,1,0:T(8,128)(2,1)S(1)}, bf16[7,9,32,64]{3,2,1,0:T(8,128)(2,1)}, u32[]{:S(2)}) copy-start(bf16[7,9,32,64]{3,2,1,0:T(8,128)(2,1)} %w_conv.1) | copy-start | bytes 774148
  5.5 0.8 %copy-start.1 = (bf16[7,64,32]{1,2,0:T(8,128)(2,1)S(1)}, bf16[7,64,32]{1,2,0:T(8,128)(2,1)}, u32[]{:S(2)}) copy-start(bf16[7,64,32]{1,2,0:T(8,128)(2,1)} %param.8) | copy-start | bytes 86020
  6.4 0.7 %copy-start.2 = (f32[7,32]{1,0:T(8,128)S(1)}, f32[7,32]{1,0:T(8,128)}, u32[]{:S(2)}) copy-start(f32[7,32]{1,0:T(8,128)} %bias_in.1) | copy-start | bytes 2692
  7.1 0.7 %copy-start.3 = (f32[7,64]{1,0:T(8,128)S(1)}, f32[7,64]{1,0:T(8,128)}, u32[]{:S(2)}) copy-start(f32[7,64]{1,0:T(8,128)} %bias_out.1) | copy-start | bytes 5380
  30.8 10.3 %collective-permute-start.1 = (bf16[8,64,256]{2,1,0:T(8,128)(2,1)S(1)}, bf16[8,64,256]{2,1,0:T(8,128)(2,1)S(1)}, u32[]{:S(2)}, u32[]{:S(2)}) collective-permute-start(bf16[8,64,256]{2,1,0:T(8,128)(2,1)S(1)} %symmetrize.1), channel_id=1, source_target_pairs={{1,2},{3,4},{5,6},{7,8},{9,10},{11,12},{13,14},{15,16},{17,18},{19... | collective-permute-start | bytes 786440 | tf_op jit(solution)/shard_map/ppermute | solution.py:523

commit v6 on v5

--- a/solution.py
+++ b/solution.py
@@ -172,10 +172,13 @@
     return jnp.where(odd == 1, shard_rows - 1 - inside, inside)
 
 
-def prepare(w_conv, bias_in, w_out, bias_out, banded, turned, doubled, bias, bias_last, conv, proj, sems):
+def prepare(w_conv, bias_in, w_out, bias_out, banded, turned, doubled, bias, bias_last,
+            conv, proj, first_bias, last_bias, sems):
     odd, _ = position()
-    for copy in fetch([(w_conv, conv), (w_out, proj)], sems):
+    pairs = [(w_conv, conv), (w_out, proj), (bias_in, first_bias), (bias_out, last_bias)]
+    for copy in fetch(pairs, sems):
         copy.wait()
+    bias_in, bias_out = first_bias, last_bias
     layers = w_conv.shape[0]
     for layer in range(layers):
         spread_conv(banded, layer, conv, layer, False, odd)
@@ -448,7 +451,7 @@
 
 
 VMEM = pl.BlockSpec(memory_space=pltpu.VMEM)
-ANY = pl.BlockSpec(memory_space=pl.ANY)
+HBM = pl.BlockSpec(memory_space=pltpu.HBM)
 
 
 class Calls:
@@ -492,10 +495,12 @@
             jax.ShapeDtypeStruct((layers, 2 * channels, LANES), F32),
         ]
         scratch = [
-            pltpu.VMEM(w_conv.shape, BF16), pltpu.VMEM(w_out.shape, BF16), pltpu.SemaphoreType.DMA((2,)),
+            pltpu.VMEM(w_conv.shape, BF16), pltpu.VMEM(w_out.shape, BF16),
+            pltpu.VMEM(bias_in.shape, F32), pltpu.VMEM(bias_out.shape, F32), pltpu.SemaphoreType.DMA((4,)),
         ]
+        args = [pltpu.with_memory_space_constraint(arg, pltpu.HBM) for arg in (w_conv, bias_in, w_out, bias_out)]
         return self.call(
-            prepare, (w_conv, bias_in, w_out, bias_out), shapes, scratch, [ANY, VMEM, ANY, VMEM]
+            prepare, args, shapes, scratch, [HBM] * 4
         )
 
     def one_early(self, *args):

time: 45.2 us -> 45.1 us (level)
  local copies, waits for them, and re-layouts: 3.22 us -> 0 us
  blocking collectives: 19.5 us -> 21.5 us
  Pallas kernels: 12.1 us -> 12.7 us
  waiting for transfers between devices: 3.17 us -> 3.75 us
    unnamed x8 -> x0, local copies, waits for them, and re-layouts: 3.22 us -> none
    all_to_all x1, blocking collectives: 14.9 us -> 16.9 us  [on_device(): lax.all_to_all(tiles, 'row', split_axis=0, concat_axis=0, tiled=True)]
    pallas_call x6, Pallas kernels: 12.1 us -> 12.7 us  [call(): pl.pallas_call(body, out_shape=shapes[0] if single else shapes, in_specs=...]
    ppermute x2, waiting for transfers between devices: 3.17 us -> 3.75 us  [neighbours(): across = lax.ppermute(array, axis, edges)]
  transfers between devices with their start and end apart: 2 -> 2, of which waited for: 1 -> 2; matrix products, arithmetic and copies ran while one was open for 0% -> 0% of each run, Pallas kernels for 12% -> 13%
where the time goes in v6:
time: 45.1 us; the launch traced here: 44.8 us
  blocking collectives  21.5 us (48%)
  Pallas kernels  12.7 us (28%)
  starting transfers between devices  6.86 us (15%)
  waiting for transfers between devices  3.75 us (8%)
    all_to_all x1, blocking collectives, on_device(): lax.all_to_all(tiles, 'row', split_axis=0, concat_axis=0, tiled=True)  16.9 us
    pallas_call x6, Pallas kernels, call(): pl.pallas_call(body, out_shape=shapes[0] if single else shapes, in_specs=...  12.7 us
    ppermute x2, starting transfers between devices, neighbours(): across = lax.ppermute(array, axis, edges)  6.86 us
    all_gather x2, blocking collectives, neighbours(): lax.all_gather(array, axis, axis_index_groups=[[i, i + 1] for i in range(...  4.57 us
    ppermute x2, waiting for transfers between devices, neighbours(): across = lax.ppermute(array, axis, edges)  3.75 us
  transfers between devices with their start and end apart: 2, of which 2 were waited for; matrix products, arithmetic and copies ran while one was open for 0% of the time, Pallas kernels for 13%

profile of v6, /device:TPU:1, one launch (start us, length us, event | category | flops | bytes accessed | tf_op | source)
XLA Modules:
  0.0 44.8 jit_solution(3671560789604686401)
XLA Ops:
  0.0 4.5 %collective-permute-start = (bf16[64,8,256]{2,1,0:T(8,128)(2,1)}, bf16[64,8,256]{2,1,0:T(8,128)(2,1)S(1)}, u32[]{:S(2)}, u32[]{:S(2)}) collective-permute-start(bf16[64,8,256]{2,1,0:T(8,128)(2,1)} %param.5), channel_id=1, source_target_pairs={{1,2},{3,4},{5,6},{7,8},{9,10},{11,12},{13,14},{15,16},{17,18},{19... | collective-permute-start | bytes 786440 | tf_op jit(solution)/shard_map/ppermute | solution.py:528
  4.5 1.8 %prepare.1 = (bf16[7,64,768]{2,1,0:T(8,128)(2,1)S(1)}, bf16[3,64,768]{2,1,0:T(8,128)(2,1)S(1)}, bf16[7,128,64]{2,1,0:T(8,128)(2,1)S(1)}, f32[7,64,128]{2,1,0:T(8,128)S(1)}, f32[7,128,128]{2,1,0:T(8,128)S(1)}) custom-call(bf16[7,9,32,64]{3,2,1,0:T(8,128)(2,1)} %w_conv.1, f32[7,32]{1,0:T(8,128)} %bias_in.1, bf16[7,32,64]{2,1,0:T(8,128)(2,1)} %bitcast.5, ...), custom_call_target="tpu_custom_call" | custom-call | tf_op jit(solution)/shard_map/prepare/pallas_call | solution.py:478
  6.3 2.4 %all-gather = bf16[128,8,256]{2,1,0:T(8,128)(2,1)S(1)} all-gather(bf16[64,8,256]{2,1,0:T(8,128)(2,1)} %param.5), channel_id=2, replica_groups={{0,1},{2,3},{4,5},{6,7},{8,9},{10,11},{12,13},{14,15},{16,17},{18,19},{..., dimensions={0}, use_global_device_ids=true | all-gather | bytes 786432 | tf_op jit(solution)/shard_map/all_gather | solution.py:529
  8.7 1.6 %one_early.1 = (bf16[15,192,256]{2,1,0:T(8,128)(2,1)S(1)}, bf16[12,192,256]{2,1,0:T(8,128)(2,1)S(1)}, bf16[8,192,256]{2,1,0:T(8,128)(2,1)S(1)}) custom-call(bf16[2,64,8,256]{3,2,1,0:T(8,128)(2,1)S(1)} %bitcast.4, bf16[7,64,768]{2,1,0:T(8,128)(2,1)S(1)} %get-tuple-element.21.refs_0_.refs_6_, bf16[3,64,768]{2,1,0:T(8,128)(2,1)S(1)} %get-tuple-element.22.refs_1_.refs_7_, ...), custom_call_target="tpu_custom_call" | custom-call | tf_op jit(solution)/shard_map/one_early/pallas_call | solution.py:478
  10.3 0.6 %collective-permute-done.across = bf16[64,8,256]{2,1,0:T(8,128)(2,1)S(1)} collective-permute-done((bf16[64,8,256]{2,1,0:T(8,128)(2,1)}, bf16[64,8,256]{2,1,0:T(8,128)(2,1)S(1)}, u32[]{:S(2)}, u32[]{:S(2)}) %collective-permute-start) | collective-permute-done | bytes 262176 | tf_op jit(solution)/shard_map/ppermute | solution.py:528
  10.9 2.4 %one_late.1 = (bf16[8,64,256]{2,1,0:T(8,128)(2,1)S(1)}, bf16[32,32,128]{2,1,0:T(8,128)(2,1)S(1)}) custom-call(bf16[64,8,256]{2,1,0:T(8,128)(2,1)S(1)} %collective-permute-done.across, bf16[15,192,256]{2,1,0:T(8,128)(2,1)S(1)} %get-tuple-element.26.kept_0, bf16[12,192,256]{2,1,0:T(8,128)(2,1)S(1)} %get-tuple-element.27.kept_1, ...), custom_call_target="tpu_custom_call" | custom-call | tf_op jit(solution)/shard_map/one_late/pallas_call | solution.py:478
  13.4 16.9 %all_to_all.5.tiles = bf16[32,32,128]{2,1,0:T(8,128)(2,1)S(1)} all-to-all(bf16[32,32,128]{2,1,0:T(8,128)(2,1)S(1)} %get-tuple-element.29), channel_id=1, replica_groups=mesh['groups'=1,'row'=32] {'row'}, dimensions={0} | all-to-all | bytes 524288 | tf_op jit(solution)/shard_map/all_to_all | solution.py:540
  30.2 0.5 %symmetrize.1 = bf16[8,64,256]{2,1,0:T(8,128)(2,1)S(1)} custom-call(bf16[32,32,128]{2,1,0:T(8,128)(2,1)S(1)} %all_to_all.5.tiles, bf16[8,64,256]{2,1,0:T(8,128)(2,1)S(1)} %get-tuple-element.30.own), custom_call_target="tpu_custom_call" | custom-call | tf_op jit(solution)/shard_map/symmetrize/pallas_call | solution.py:478
  30.8 2.4 %collective-permute-start.1 = (bf16[8,64,256]{2,1,0:T(8,128)(2,1)S(1)}, bf16[8,64,256]{2,1,0:T(8,128)(2,1)S(1)}, u32[]{:S(2)}, u32[]{:S(2)}) collective-permute-start(bf16[8,64,256]{2,1,0:T(8,128)(2,1)S(1)} %symmetrize.1), channel_id=1, source_target_pairs={{1,2},{3,4},{5,6},{7,8},{9,10},{11,12},{13,14},{15,16},{17,18},{19... | collective-permute-start | bytes 786440 | tf_op jit(solution)/shard_map/ppermute | solution.py:528
  33.1 2.2 %all-gather.1 = bf16[16,64,256]{2,1,0:T(8,128)(2,1)S(1)} all-gather(bf16[8,64,256]{2,1,0:T(8,128)(2,1)S(1)} %symmetrize.1), channel_id=3, replica_groups={{0,1},{2,3},{4,5},{6,7},{8,9},{10,11},{12,13},{14,15},{16,17},{18,19},{..., dimensions={0}, use_global_device_ids=true | all-gather | bytes 786432 | tf_op jit(solution)/shard_map/all_gather | solution.py:529
  35.3 2.5 %two_early.1 = (bf16[16,192,256]{2,1,0:T(8,128)(2,1)S(1)}, bf16[14,192,256]{2,1,0:T(8,128)(2,1)S(1)}, bf16[14,192,256]{2,1,0:T(8,128)(2,1)S(1)}, bf16[10,192,256...) custom-call(bf16[2,8,64,256]{3,2,1,0:T(8,128)(2,1)S(1)} %bitcast.3, ...), custom_call_target="tpu_custom_call" | custom-call | tf_op jit(solution)/shard_map/two_early/pallas_call | solution.py:478
  37.9 3.2 %collective-permute-done.1.across = bf16[8,64,256]{2,1,0:T(8,128)(2,1)S(1)} collective-permute-done((bf16[8,64,256]{2,1,0:T(8,128)(2,1)S(1)}, bf16[8,64,256]{2,1,0:T(8,128)(2,1)S(1)}, u32[]{:S(2)}, u32[]{:S(2)}) %collective-permute-start.1) | collective-permute-done | bytes 262176 | tf_op jit(solution)/shard_map/ppermute | solution.py:528
  41.0 3.8 %two_late.1 = bf16[64,8,256]{2,1,0:T(8,128)(2,1)} custom-call(bf16[8,64,256]{2,1,0:T(8,128)(2,1)S(1)} %collective-permute-done.1.across, bf16[16,192,256]{2,1,0:T(8,128)(2,1)S(1)} %get-tuple-element.31.refs_0_, bf16[14,192,256]{2,1,0:T(8,128)(2,1)S(1)} %get-tuple-element.32.refs_1_, bf16[14,192,256]{2,1,0:T(8,128)(2,1)S(1)} %get-tuple-element.33.refs_2_, ...), custom_call_target="tpu_custom_call" | custom-call | tf_op jit(solution)/shard_map/two_late/pallas_call | solution.py:478
Async XLA Ops:
  0.0 10.9 %collective-permute-start = (bf16[64,8,256]{2,1,0:T(8,128)(2,1)}, bf16[64,8,256]{2,1,0:T(8,128)(2,1)S(1)}, u32[]{:S(2)}, u32[]{:S(2)}) collective-permute-start(bf16[64,8,256]{2,1,0:T(8,128)(2,1)} %param.5), channel_id=1, source_target_pairs={{1,2},{3,4},{5,6},{7,8},{9,10},{11,12},{13,14},{15,16},{17,18},{19... | collective-permute-start | bytes 786440 | tf_op jit(solution)/shard_map/ppermute | solution.py:528
  30.8 10.3 %collective-permute-start.1 = (bf16[8,64,256]{2,1,0:T(8,128)(2,1)S(1)}, bf16[8,64,256]{2,1,0:T(8,128)(2,1)S(1)}, u32[]{:S(2)}, u32[]{:S(2)}) collective-permute-start(bf16[8,64,256]{2,1,0:T(8,128)(2,1)S(1)} %symmetrize.1), channel_id=1, source_target_pairs={{1,2},{3,4},{5,6},{7,8},{9,10},{11,12},{13,14},{15,16},{17,18},{19... | collective-permute-start | bytes 786440 | tf_op jit(solution)/shard_map/ppermute | solution.py:528

commit v7 on v6

--- a/solution.py
+++ b/solution.py
@@ -10,7 +10,7 @@
 
 dilations = (1, 2, 4)
 LANES = 128
-LAG = 2
+LAG = 3
 F32 = jnp.float32
 BF16 = jnp.bfloat16
 
@@ -22,16 +22,24 @@
         self.keep = ()
 
 
+def group_of(dilation):
+    return 4 if dilation < dilations[-1] else 2
+
+
 def cover(low, high, limit, dilation):
     covered, starts = set(), []
+    count = group_of(dilation)
     for row in range(low, high + 1):
         if row in covered:
             continue
         start = row
-        if row + dilation > limit and row - dilation >= low:
-            start = row - dilation
+        for back in range(count):
+            candidate = row - back * dilation
+            if candidate >= low and candidate + (count - 1) * dilation <= limit:
+                start = candidate
+                break
         starts.append(start)
-        covered |= {start, start + dilation}
+        covered |= {start + step * dilation for step in range(count)}
     return starts, covered
 
 
@@ -86,21 +94,30 @@
 
     def window(self, start):
         return jnp.concatenate(
-            [self.get(start + (tap - 1) * self.dilation, place) for place in range(3) for tap in range(4)], axis=0
+            [
+                self.get(start + (tap - 1) * self.dilation, place)
+                for place in range(3)
+                for tap in range(group_of(self.dilation) + 2)
+            ],
+            axis=0,
         )
 
 
 def spread_conv(banded, slot, w_conv, layer, turned, odd):
     inner, channels = w_conv.shape[2], w_conv.shape[3]
+    count = banded.shape[1] // inner
     zeros = jnp.zeros((inner, channels), BF16)
     for col_tap in range(3):
         taps = []
         for row_tap in range(3):
             line = jnp.where(odd == 1, 2 - row_tap, row_tap)
             taps.append(w_conv[layer, col_tap * 3 + line if turned else line * 3 + col_tap])
-        left = col_tap * 4 * channels
-        banded[slot, :inner, left : left + 4 * channels] = jnp.concatenate(taps + [zeros], axis=1)
-        banded[slot, inner:, left : left + 4 * channels] = jnp.concatenate([zeros] + taps, axis=1)
+        left = col_tap * (count + 2) * channels
+        for row in range(count):
+            parts = [zeros] * row + taps + [zeros] * (count - 1 - row)
+            banded[slot, row * inner : (row + 1) * inner, left : left + (count + 2) * channels] = jnp.concatenate(
+                parts, axis=1
+            )
 
 
 def spread_out(doubled, slot, w_out, layer):
@@ -125,7 +142,8 @@
 
     def complete(start, hidden):
         steps = []
-        for step, row in enumerate((start, start + dilation)):
+        for step in range(group_of(dilation)):
+            row = start + step * dilation
             if row in rows and row not in done:
                 steps.append((step, row))
                 done.add(row)
@@ -144,12 +162,16 @@
     return jnp.maximum(inner + bias, 0.0).astype(BF16)
 
 
-def two_rows(stack, start, hidden, kernel, bias):
-    blended = jnp.dot(kernel, hidden, preferred_element_type=F32)
-    residual = [stack.get(start + step * stack.dilation, 1).astype(F32) for step in range(2)]
-    total = jnp.concatenate(residual, axis=0) + blended + bias
-    channels = total.shape[0] // 2
-    return total[:channels], total[channels:]
+def group_rows(stack, start, hidden, kernel, bias):
+    half = kernel.shape[1]
+    values = []
+    for pair in range(hidden.shape[0] // half):
+        blended = jnp.dot(kernel, hidden[pair * half : (pair + 1) * half], preferred_element_type=F32)
+        residual = [stack.get(start + (2 * pair + step) * stack.dilation, 1).astype(F32) for step in range(2)]
+        total = jnp.concatenate(residual, axis=0) + blended + bias
+        channels = total.shape[0] // 2
+        values += [total[:channels], total[channels:]]
+    return values
 
 
 def fetch(pairs, sems):
@@ -172,21 +194,30 @@
     return jnp.where(odd == 1, shard_rows - 1 - inside, inside)
 
 
-def prepare(w_conv, bias_in, w_out, bias_out, banded, turned, doubled, bias, bias_last,
+def layer_steps():
+    return dilations * SECTIONS + (dilations[0],)
+
+
+def slot_of(steps, layer):
+    return sum(1 for step in steps[:layer] if group_of(step) == group_of(steps[layer]))
+
+
+def prepare(w_conv, bias_in, w_out, bias_out, small, large, small_turned, large_turned, doubled, bias, bias_last,
             conv, proj, first_bias, last_bias, sems):
     odd, _ = position()
     pairs = [(w_conv, conv), (w_out, proj), (bias_in, first_bias), (bias_out, last_bias)]
     for copy in fetch(pairs, sems):
         copy.wait()
-    bias_in, bias_out = first_bias, last_bias
-    layers = w_conv.shape[0]
-    for layer in range(layers):
-        spread_conv(banded, layer, conv, layer, False, odd)
+    steps = layer_steps()
+    base = len(steps) - 1 - DEPTH
+    for layer, step in enumerate(steps):
+        spread_conv(small if group_of(step) == 2 else large, slot_of(steps, layer), conv, layer, False, odd)
         spread_out(doubled, layer, proj, layer)
-        bias[layer] = jnp.broadcast_to(as_column(bias_in[layer : layer + 1, :], 2), bias.shape[1:])
-        bias_last[layer] = jnp.broadcast_to(as_column(bias_out[layer : layer + 1, :], 2), bias_last.shape[1:])
-    for layer in range(turned.shape[0]):
-        spread_conv(turned, layer, conv, layers - 1 - DEPTH + layer, True, odd)
+        bias[layer] = jnp.broadcast_to(as_column(first_bias[layer : layer + 1, :], 4), bias.shape[1:])
+        bias_last[layer] = jnp.broadcast_to(as_column(last_bias[layer : layer + 1, :], 2), bias_last.shape[1:])
+    for layer, step in enumerate(dilations):
+        place = small_turned if group_of(step) == 2 else large_turned
+        spread_conv(place, slot_of(dilations, layer), conv, base + layer, True, odd)
 
 
 class Weights:
@@ -194,19 +225,23 @@
         self.refs, self.base, self.blocks = refs, base, width // LANES
 
     def conv(self, layer):
-        return self.refs[0][self.base + layer]
+        steps = layer_steps()
+        layer = self.base + layer
+        return self.refs[0 if group_of(steps[layer]) == 2 else 1][slot_of(steps, layer)]
 
     def conv_turned(self, layer):
-        return self.refs[1][layer]
+        return self.refs[2 if group_of(dilations[layer]) == 2 else 3][slot_of(dilations, layer)]
 
     def out(self, layer):
-        return self.refs[2][self.base + layer]
+        return self.refs[4][self.base + layer]
 
     def bias(self, layer):
-        return jnp.concatenate([self.refs[3][self.base + layer]] * self.blocks, axis=1)
+        inner = self.refs[5].shape[1] // 4
+        rows = group_of(layer_steps()[self.base + layer]) * inner
+        return jnp.concatenate([self.refs[5][self.base + layer, :rows]] * self.blocks, axis=1)
 
     def bias_out(self, layer):
-        return jnp.concatenate([self.refs[4][self.base + layer]] * self.blocks, axis=1)
+        return jnp.concatenate([self.refs[6][self.base + layer]] * self.blocks, axis=1)
 
 
 def block_one(weights, layer, stage, starts, rows, source, store):
@@ -217,7 +252,7 @@
         return conv_hidden(source, start, kernel, bias)
 
     def finish(start, hidden, steps):
-        values = two_rows(source, start, hidden, kernel_out, bias_out)
+        values = group_rows(source, start, hidden, kernel_out, bias_out)
         for step, row in steps:
             store(row, values[step])
 
@@ -239,7 +274,7 @@
 
     def finish(start, hiddens, steps):
         values = [
-            two_rows(source, start, hidden, kernel_out, bias_out)
+            group_rows(source, start, hidden, kernel_out, bias_out)
             for source, hidden in zip(sources, hiddens)
         ]
         for step, row in steps:
@@ -270,7 +305,7 @@
 
 
 def one_early(chip, *refs):
-    weight_refs, (stack_0, stack_1, stack_2, wide) = refs[:5], refs[5:]
+    weight_refs, (stack_0, stack_1, stack_2, wide) = refs[:7], refs[7:]
     _, channels, shard_rows, width = chip.shape
     odd, _ = position()
     stages = plan(shard_rows, dilations)
@@ -310,7 +345,7 @@
 
 
 def one_late(across, kept_0, kept_1, kept_2, *refs):
-    weight_refs, (out, tiles, stack_0, stack_1, stack_2, wide) = refs[:5], refs[5:]
+    weight_refs, (out, tiles, stack_0, stack_1, stack_2, wide) = refs[:7], refs[7:]
     channels, shard_rows, width = across.shape
     odd, edge = position()
     stages = plan(shard_rows, dilations)
@@ -382,7 +417,7 @@
 
 
 def two_early(chip, *refs):
-    weight_refs, stack_refs = refs[:5], refs[5:]
+    weight_refs, stack_refs = refs[:7], refs[7:]
     _, shard_rows, channels, width = chip.shape
     odd, _ = position()
     steps = two_steps()
@@ -410,7 +445,7 @@
 
 
 def two_late(across, *refs):
-    kept_refs, weight_refs, out, stack_refs, wide = refs[:6], refs[6:11], refs[11], refs[12:18], refs[18]
+    kept_refs, weight_refs, out, stack_refs, wide = refs[:6], refs[6:13], refs[13], refs[14:20], refs[20]
     shard_rows, channels, width = across.shape
     odd, edge = position()
     steps = two_steps()
@@ -487,11 +522,14 @@
 
     def prepare(self, w_conv, bias_in, w_out, bias_out):
         layers, inner, channels = w_conv.shape[0], self.inner, self.channels
+
+        def banded(steps, count):
+            return (sum(1 for step in steps if group_of(step) == count), count * inner, 3 * (count + 2) * channels)
+
         shapes = [
-            (layers, 2 * inner, 12 * channels),
-            (DEPTH, 2 * inner, 12 * channels),
+            banded(layer_steps(), 2), banded(layer_steps(), 4), banded(dilations, 2), banded(dilations, 4),
             (layers, 2 * channels, 2 * inner),
-            jax.ShapeDtypeStruct((layers, 2 * inner, LANES), F32),
+            jax.ShapeDtypeStruct((layers, 4 * inner, LANES), F32),
             jax.ShapeDtypeStruct((layers, 2 * channels, LANES), F32),
         ]
         scratch = [

time: 45.1 us -> 44.6 us (0.989)
  transfers between devices with their start and end apart: 2 -> 2, of which waited for: 2 -> 2; matrix products, arithmetic and copies ran while one was open for 0% -> 0% of each run, Pallas kernels for 13% -> 14%
where the time goes in v7:
time: 44.6 us; the launch traced here: 44.5 us
  blocking collectives  21.5 us (48%)
  Pallas kernels  12.7 us (28%)
  starting transfers between devices  6.86 us (15%)
  waiting for transfers between devices  3.33 us (7%)
    all_to_all x1, blocking collectives, on_device(): lax.all_to_all(tiles, 'row', split_axis=0, concat_axis=0, tiled=True)  16.9 us
    pallas_call x6, Pallas kernels, call(): pl.pallas_call(body, out_shape=shapes[0] if single else shapes, in_specs=...  12.7 us
    ppermute x2, starting transfers between devices, neighbours(): across = lax.ppermute(array, axis, edges)  6.86 us
    all_gather x2, blocking collectives, neighbours(): lax.all_gather(array, axis, axis_index_groups=[[i, i + 1] for i in range(...  4.57 us
    ppermute x2, waiting for transfers between devices, neighbours(): across = lax.ppermute(array, axis, edges)  3.33 us
  transfers between devices with their start and end apart: 2, of which 2 were waited for; matrix products, arithmetic and copies ran while one was open for 0% of the time, Pallas kernels for 14%

profile of v7, /device:TPU:1, one launch (start us, length us, event | category | flops | bytes accessed | tf_op | source)
XLA Modules:
  0.0 44.5 jit_solution(4916282033054951313)
XLA Ops:
  0.0 4.5 %collective-permute-start = (bf16[64,8,256]{2,1,0:T(8,128)(2,1)}, bf16[64,8,256]{2,1,0:T(8,128)(2,1)S(1)}, u32[]{:S(2)}, u32[]{:S(2)}) collective-permute-start(bf16[64,8,256]{2,1,0:T(8,128)(2,1)} %param.5), channel_id=1, source_target_pairs={{1,2},{3,4},{5,6},{7,8},{9,10},{11,12},{13,14},{15,16},{17,18},{19... | collective-permute-start | bytes 786440 | tf_op jit(solution)/shard_map/ppermute | solution.py:566
  4.5 1.8 %prepare.1 = (bf16[2,64,768]{2,1,0:T(8,128)(2,1)S(1)}, bf16[5,128,1152]{2,1,0:T(8,128)(2,1)S(1)}, bf16[1,64,768]{2,1,0:T(8,128)(2,1)S(1)}, bf16[2,128,1152]{2,1,...) custom-call(bf16[7,9,32,64]{3,2,1,0:T(8,128)(2,1)} %w_conv.1, ...), custom_call_target="tpu_custom_call" | custom-call | tf_op jit(solution)/shard_map/prepare/pallas_call | solution.py:513
  6.3 2.4 %all-gather = bf16[128,8,256]{2,1,0:T(8,128)(2,1)S(1)} all-gather(bf16[64,8,256]{2,1,0:T(8,128)(2,1)} %param.5), channel_id=2, replica_groups={{0,1},{2,3},{4,5},{6,7},{8,9},{10,11},{12,13},{14,15},{16,17},{18,19},{..., dimensions={0}, use_global_device_ids=true | all-gather | bytes 786432 | tf_op jit(solution)/shard_map/all_gather | solution.py:567
  8.7 1.6 %one_early.1 = (bf16[15,192,256]{2,1,0:T(8,128)(2,1)S(1)}, bf16[12,192,256]{2,1,0:T(8,128)(2,1)S(1)}, bf16[8,192,256]{2,1,0:T(8,128)(2,1)S(1)}) custom-call(bf16[2,64,8,256]{3,2,1,0:T(8,128)(2,1)S(1)} %bitcast.4, bf16[2,64,768]{2,1,0:T(8,128)(2,1)S(1)} %get-tuple-element.23.refs_0_.refs_6_, bf16[5,128,1152]{2,1,0:T(8,128)(2,1)S(1)} %get-tuple-element.24.refs_1_.refs_7_, ...), custom_call_target="tpu_custom_call" | custom-call | tf_op jit(solution)/shard_map/one_early/pallas_call | solution.py:513
  10.3 0.6 %collective-permute-done.across = bf16[64,8,256]{2,1,0:T(8,128)(2,1)S(1)} collective-permute-done((bf16[64,8,256]{2,1,0:T(8,128)(2,1)}, bf16[64,8,256]{2,1,0:T(8,128)(2,1)S(1)}, u32[]{:S(2)}, u32[]{:S(2)}) %collective-permute-start) | collective-permute-done | bytes 262176 | tf_op jit(solution)/shard_map/ppermute | solution.py:566
  10.9 2.2 %one_late.1 = (bf16[8,64,256]{2,1,0:T(8,128)(2,1)S(1)}, bf16[32,32,128]{2,1,0:T(8,128)(2,1)S(1)}) custom-call(bf16[64,8,256]{2,1,0:T(8,128)(2,1)S(1)} %collective-permute-done.across, bf16[15,192,256]{2,1,0:T(8,128)(2,1)S(1)} %get-tuple-element.30.kept_0, bf16[12,192,256]{2,1,0:T(8,128)(2,1)S(1)} %get-tuple-element.31.kept_1, ...), custom_call_target="tpu_custom_call" | custom-call | tf_op jit(solution)/shard_map/one_late/pallas_call | solution.py:513
  13.2 16.9 %all_to_all.5.tiles = bf16[32,32,128]{2,1,0:T(8,128)(2,1)S(1)} all-to-all(bf16[32,32,128]{2,1,0:T(8,128)(2,1)S(1)} %get-tuple-element.33), channel_id=1, replica_groups=mesh['groups'=1,'row'=32] {'row'}, dimensions={0} | all-to-all | bytes 524288 | tf_op jit(solution)/shard_map/all_to_all | solution.py:578
  30.1 0.5 %symmetrize.1 = bf16[8,64,256]{2,1,0:T(8,128)(2,1)S(1)} custom-call(bf16[32,32,128]{2,1,0:T(8,128)(2,1)S(1)} %all_to_all.5.tiles, bf16[8,64,256]{2,1,0:T(8,128)(2,1)S(1)} %get-tuple-element.34.own), custom_call_target="tpu_custom_call" | custom-call | tf_op jit(solution)/shard_map/symmetrize/pallas_call | solution.py:513
  30.6 2.4 %collective-permute-start.1 = (bf16[8,64,256]{2,1,0:T(8,128)(2,1)S(1)}, bf16[8,64,256]{2,1,0:T(8,128)(2,1)S(1)}, u32[]{:S(2)}, u32[]{:S(2)}) collective-permute-start(bf16[8,64,256]{2,1,0:T(8,128)(2,1)S(1)} %symmetrize.1), channel_id=1, source_target_pairs={{1,2},{3,4},{5,6},{7,8},{9,10},{11,12},{13,14},{15,16},{17,18},{19... | collective-permute-start | bytes 786440 | tf_op jit(solution)/shard_map/ppermute | solution.py:566
  32.9 2.2 %all-gather.1 = bf16[16,64,256]{2,1,0:T(8,128)(2,1)S(1)} all-gather(bf16[8,64,256]{2,1,0:T(8,128)(2,1)S(1)} %symmetrize.1), channel_id=3, replica_groups={{0,1},{2,3},{4,5},{6,7},{8,9},{10,11},{12,13},{14,15},{16,17},{18,19},{..., dimensions={0}, use_global_device_ids=true | all-gather | bytes 786432 | tf_op jit(solution)/shard_map/all_gather | solution.py:567
  35.1 3.0 %two_early.1 = (bf16[16,192,256]{2,1,0:T(8,128)(2,1)S(1)}, bf16[14,192,256]{2,1,0:T(8,128)(2,1)S(1)}, bf16[14,192,256]{2,1,0:T(8,128)(2,1)S(1)}, bf16[10,192,256...) custom-call(bf16[2,8,64,256]{3,2,1,0:T(8,128)(2,1)S(1)} %bitcast.3, ...), custom_call_target="tpu_custom_call" | custom-call | tf_op jit(solution)/shard_map/two_early/pallas_call | solution.py:513
  38.1 2.7 %collective-permute-done.1.across = bf16[8,64,256]{2,1,0:T(8,128)(2,1)S(1)} collective-permute-done((bf16[8,64,256]{2,1,0:T(8,128)(2,1)S(1)}, bf16[8,64,256]{2,1,0:T(8,128)(2,1)S(1)}, u32[]{:S(2)}, u32[]{:S(2)}) %collective-permute-start.1) | collective-permute-done | bytes 262176 | tf_op jit(solution)/shard_map/ppermute | solution.py:566
  40.8 3.6 %two_late.1 = bf16[64,8,256]{2,1,0:T(8,128)(2,1)} custom-call(bf16[8,64,256]{2,1,0:T(8,128)(2,1)S(1)} %collective-permute-done.1.across, bf16[16,192,256]{2,1,0:T(8,128)(2,1)S(1)} %get-tuple-element.35.refs_0_, bf16[14,192,256]{2,1,0:T(8,128)(2,1)S(1)} %get-tuple-element.36.refs_1_, bf16[14,192,256]{2,1,0:T(8,128)(2,1)S(1)} %get-tuple-element.37.refs_2_, ...), custom_call_target="tpu_custom_call" | custom-call | tf_op jit(solution)/shard_map/two_late/pallas_call | solution.py:513
Async XLA Ops:
  0.0 10.9 %collective-permute-start = (bf16[64,8,256]{2,1,0:T(8,128)(2,1)}, bf16[64,8,256]{2,1,0:T(8,128)(2,1)S(1)}, u32[]{:S(2)}, u32[]{:S(2)}) collective-permute-start(bf16[64,8,256]{2,1,0:T(8,128)(2,1)} %param.5), channel_id=1, source_target_pairs={{1,2},{3,4},{5,6},{7,8},{9,10},{11,12},{13,14},{15,16},{17,18},{19... | collective-permute-start | bytes 786440 | tf_op jit(solution)/shard_map/ppermute | solution.py:566
  30.6 10.3 %collective-permute-start.1 = (bf16[8,64,256]{2,1,0:T(8,128)(2,1)S(1)}, bf16[8,64,256]{2,1,0:T(8,128)(2,1)S(1)}, u32[]{:S(2)}, u32[]{:S(2)}) collective-permute-start(bf16[8,64,256]{2,1,0:T(8,128)(2,1)S(1)} %symmetrize.1), channel_id=1, source_target_pairs={{1,2},{3,4},{5,6},{7,8},{9,10},{11,12},{13,14},{15,16},{17,18},{19... | collective-permute-start | bytes 786440 | tf_op jit(solution)/shard_map/ppermute | solution.py:566

commit v8 on v7

--- a/solution.py
+++ b/solution.py
@@ -92,32 +92,41 @@
         channels = ref.shape[1] // 3
         return ref[index, place * channels : (place + 1) * channels, :]
 
-    def window(self, start):
-        return jnp.concatenate(
-            [
-                self.get(start + (tap - 1) * self.dilation, place)
-                for place in range(3)
-                for tap in range(group_of(self.dilation) + 2)
-            ],
-            axis=0,
-        )
+    def window(self, start, taps):
+        slabs = []
+        for tap in taps:
+            ref, index = self.find(min(start + (tap - 1) * self.dilation, self.top))
+            slabs.append(ref[index])
+        return jnp.concatenate(slabs, axis=0)
+
+
+def late_groups(stages, layer):
+    stage, source = stages[layer + 1], stages[layer]
+    count = group_of(stage.dilation) + 2
+    groups = {}
+    place = 0
+    for start in stage.late:
+        first = 0
+        while first < count and start + (first - 1) * stage.dilation < source.early_low:
+            first += 1
+        first = min(first + first % 2, count)
+        groups[start] = (first, place)
+        place += first < count
+    return groups, place
 
 
 def spread_conv(banded, slot, w_conv, layer, turned, odd):
     inner, channels = w_conv.shape[2], w_conv.shape[3]
     count = banded.shape[1] // inner
     zeros = jnp.zeros((inner, channels), BF16)
-    for col_tap in range(3):
-        taps = []
-        for row_tap in range(3):
-            line = jnp.where(odd == 1, 2 - row_tap, row_tap)
+    taps = []
+    for row_tap in range(3):
+        line = jnp.where(odd == 1, 2 - row_tap, row_tap)
+        for col_tap in range(3):
             taps.append(w_conv[layer, col_tap * 3 + line if turned else line * 3 + col_tap])
-        left = col_tap * (count + 2) * channels
-        for row in range(count):
-            parts = [zeros] * row + taps + [zeros] * (count - 1 - row)
-            banded[slot, row * inner : (row + 1) * inner, left : left + (count + 2) * channels] = jnp.concatenate(
-                parts, axis=1
-            )
+    for row in range(count):
+        parts = [zeros] * (3 * row) + taps + [zeros] * (3 * (count - 1 - row))
+        banded[slot, row * inner : (row + 1) * inner, :] = jnp.concatenate(parts, axis=1)
 
 
 def spread_out(doubled, slot, w_out, layer):
@@ -157,9 +166,26 @@
         complete(*item)
 
 
-def conv_hidden(stack, start, kernel, bias):
-    inner = jnp.dot(kernel, stack.window(start), preferred_element_type=F32)
-    return jnp.maximum(inner + bias, 0.0).astype(BF16)
+def conv_sum(stack, start, kernel, bias, taps):
+    slab = stack.parts[0][0].shape[1]
+    columns = slice(taps[0] * slab, (taps[-1] + 1) * slab)
+    return jnp.dot(kernel[:, columns], stack.window(start, taps), preferred_element_type=F32) + bias
+
+
+def conv_hidden(stack, start, kernel, bias, groups=None, sums=None):
+    count = group_of(stack.dilation) + 2
+    first, place = groups[start] if groups else (count, 0)
+    if first < count:
+        bias = sums[place]
+    inner = conv_sum(stack, start, kernel, bias, range(first))
+    return jnp.maximum(inner, 0.0).astype(BF16)
+
+
+def early_sums(stack, kernel, bias, groups, sums):
+    count = group_of(stack.dilation) + 2
+    for start, (first, place) in groups.items():
+        if first < count:
+            sums[place] = conv_sum(stack, start, kernel, bias, range(first, count))
 
 
 def group_rows(stack, start, hidden, kernel, bias):
@@ -244,12 +270,12 @@
         return jnp.concatenate([self.refs[6][self.base + layer]] * self.blocks, axis=1)
 
 
-def block_one(weights, layer, stage, starts, rows, source, store):
+def block_one(weights, layer, stage, starts, rows, source, store, groups=None, sums=None):
     kernel, kernel_out = weights.conv(layer), weights.out(layer)
     bias, bias_out = weights.bias(layer), weights.bias_out(layer)
 
     def hidden_of(start):
-        return conv_hidden(source, start, kernel, bias)
+        return conv_hidden(source, start, kernel, bias, groups, sums)
 
     def finish(start, hidden, steps):
         values = group_rows(source, start, hidden, kernel_out, bias_out)
@@ -259,18 +285,22 @@
     run_block(starts, rows, stage.dilation, hidden_of, finish)
 
 
-def block_two(weights, layer, stage, starts, rows, sources, store):
+def block_two(weights, layer, stage, starts, rows, sources, store, groups=None, sums=(None, None)):
     kernels = (weights.conv(layer), weights.conv_turned(layer))
     kernel_out, bias, bias_out = weights.out(layer), weights.bias(layer), weights.bias_out(layer)
 
     def hidden_of(start):
         if sources[0] is sources[1]:
             both = conv_hidden(
-                sources[0], start, jnp.concatenate(kernels, axis=0), jnp.concatenate([bias, bias], axis=0)
+                sources[0], start, jnp.concatenate(kernels, axis=0), jnp.concatenate([bias, bias], axis=0),
+                groups, sums[0],
             )
             half = both.shape[0] // 2
             return both[:half], both[half:]
-        return tuple(conv_hidden(source, start, kernel, bias) for source, kernel in zip(sources, kernels))
+        return tuple(
+            conv_hidden(source, start, kernel, bias, groups, part)
+            for source, kernel, part in zip(sources, kernels, sums)
+        )
 
     def finish(start, hiddens, steps):
         values = [
@@ -305,7 +335,7 @@
 
 
 def one_early(chip, *refs):
-    weight_refs, (stack_0, stack_1, stack_2, wide) = refs[:7], refs[7:]
+    weight_refs, (stack_0, stack_1, stack_2), sums, wide = refs[:7], refs[7:10], refs[10:13], refs[13]
     _, channels, shard_rows, width = chip.shape
     odd, _ = position()
     stages = plan(shard_rows, dilations)
@@ -327,6 +357,9 @@
             stacks[layer + 1].put(row, value.astype(BF16))
 
         block_one(weights, layer, stage, stage.early, range(stage.early_low, stage.high + 1), stacks[layer], store)
+    for layer in range(DEPTH):
+        groups, _ = late_groups(stages, layer)
+        early_sums(stacks[layer], weights.conv(layer), weights.bias(layer), groups, sums[layer])
 
 
 def chunks_turned(values, lines):
@@ -345,7 +378,7 @@
 
 
 def one_late(across, kept_0, kept_1, kept_2, *refs):
-    weight_refs, (out, tiles, stack_0, stack_1, stack_2, wide) = refs[:7], refs[7:]
+    sums, weight_refs, (out, tiles, stack_0, stack_1, stack_2, wide) = refs[:3], refs[3:10], refs[10:]
     channels, shard_rows, width = across.shape
     odd, edge = position()
     stages = plan(shard_rows, dilations)
@@ -372,7 +405,9 @@
                 value = jnp.where(edge, jnp.zeros_like(value), value)
             stacks[layer + 1].put(row, value)
 
-        block_one(weights, layer, stage, stage.late, range(stage.low, stage.early_low), stacks[layer], store)
+        groups, _ = late_groups(stages, layer)
+        rows = range(stage.low, stage.early_low)
+        block_one(weights, layer, stage, stage.late, rows, stacks[layer], store, groups, sums[layer])
 
     half = channels // 2
     low_lanes = lax.broadcasted_iota(jnp.int32, (half, LANES), 1) < LANES // 2
@@ -414,10 +449,11 @@
 
 
 LAYERS_OF = (0, 1, 1, 2, 2, 3)
+SUMS_OF = (0, 1, 1, 2, 2, 3)
 
 
 def two_early(chip, *refs):
-    weight_refs, stack_refs = refs[:7], refs[7:]
+    weight_refs, stack_refs, sums = refs[:7], refs[7:13], refs[13:]
     _, shard_rows, channels, width = chip.shape
     odd, _ = position()
     steps = two_steps()
@@ -442,10 +478,19 @@
 
         block_two(weights, layer, stage, stage.early, range(stage.early_low, stage.high + 1), sources, store)
         sources = stacks[layer + 1]
+    for ref, layer, turn in zip(sums, SUMS_OF, (0, 0, 1, 0, 1, 0)):
+        groups, _ = late_groups(stages, layer)
+        kernel = weights.conv_turned(layer) if turn else weights.conv(layer)
+        bias = weights.bias(layer)
+        if layer == 0:
+            kernel = jnp.concatenate([kernel, weights.conv_turned(layer)], axis=0)
+            bias = jnp.concatenate([bias, bias], axis=0)
+        early_sums(stacks[layer][turn], kernel, bias, groups, ref)
 
 
 def two_late(across, *refs):
-    kept_refs, weight_refs, out, stack_refs, wide = refs[:6], refs[6:13], refs[13], refs[14:20], refs[20]
+    kept_refs, sums, weight_refs = refs[:6], refs[6:12], refs[12:19]
+    out, stack_refs, wide = refs[19], refs[20:26], refs[26]
     shard_rows, channels, width = across.shape
     odd, edge = position()
     steps = two_steps()
@@ -470,7 +515,12 @@
                     value = jnp.where(edge, jnp.zeros_like(value), value)
                 target.put(row, value)
 
-        block_two(weights, layer, stage, stage.late, range(stage.low, stage.early_low), sources, store)
+        groups, _ = late_groups(stages, layer)
+        parts = [ref for ref, place in zip(sums, SUMS_OF) if place == layer]
+        block_two(
+            weights, layer, stage, stage.late, range(stage.low, stage.early_low), sources, store, groups,
+            parts if len(parts) == 2 else parts * 2,
+        )
         sources = stacks[layer + 1]
 
     stage = stages[DEPTH + 1]
@@ -480,7 +530,9 @@
         for block in range(width // LANES):
             wide[block, picked, :] = value[:, block * LANES : (block + 1) * LANES]
 
-    block_one(weights, DEPTH, stage, stage.late, range(stage.low, stage.high + 1), sources[0], store_last)
+    groups, _ = late_groups(stages, DEPTH)
+    rows = range(stage.low, stage.high + 1)
+    block_one(weights, DEPTH, stage, stage.late, rows, sources[0], store_last, groups, sums[-1])
     whole = jnp.concatenate([wide[block] for block in range(width // LANES)], axis=1)
     out[...] = whole.reshape(channels, shard_rows, width).astype(BF16)
 
@@ -503,6 +555,10 @@
 
     def late(self, stage):
         return pltpu.VMEM(self.stack(stage.low, stage.early_low - 1), BF16)
+
+    def sums(self, stages, layer, copies=1):
+        rows = copies * group_of(stages[layer + 1].dilation) * self.inner
+        return jax.ShapeDtypeStruct((max(late_groups(stages, layer)[1], 1), rows, self.width), F32)
 
     def wide(self, *shards):
         return pltpu.VMEM(shards + (self.width // LANES, self.channels * self.shard_rows, LANES), F32)
@@ -542,7 +598,9 @@
         )
 
     def one_early(self, *args):
-        return self.call(one_early, args, [self.early(stage) for stage in self.one[:DEPTH]], [self.wide(2)])
+        shapes = [self.early(stage) for stage in self.one[:DEPTH]]
+        shapes += [self.sums(self.one, layer) for layer in range(DEPTH)]
+        return self.call(one_early, args, shapes, [self.wide(2)])
 
     def one_late(self, *args):
         shapes = [(self.shard_rows, self.channels, self.width), (self.size, self.channels // 2, LANES)]
@@ -552,7 +610,9 @@
         return self.call(symmetrize, args, [(self.shard_rows, self.channels, self.width)], [])
 
     def two_early(self, *args):
-        return self.call(two_early, args, [self.early(self.two[index]) for index in LAYERS_OF], [])
+        shapes = [self.early(self.two[index]) for index in LAYERS_OF]
+        shapes += [self.sums(self.two, layer, 2 if layer == 0 else 1) for layer in SUMS_OF]
+        return self.call(two_early, args, shapes, [])
 
     def two_late(self, *args):
         scratch = [self.late(self.two[index]) for index in LAYERS_OF] + [self.wide()]

time: 44.6 us -> 44 us (0.987)
  transfers between devices with their start and end apart: 2 -> 2, of which waited for: 2 -> 2; matrix products, arithmetic and copies ran while one was open for 0% -> 0% of each run, Pallas kernels for 14% -> 15%
where the time goes in v8:
time: 44 us; the launch traced here: 43.8 us
  blocking collectives  21.5 us (49%)
  Pallas kernels  12.3 us (28%)
  starting transfers between devices  6.86 us (16%)
  waiting for transfers between devices  3.05 us (7%)
    all_to_all x1, blocking collectives, on_device(): lax.all_to_all(tiles, 'row', split_axis=0, concat_axis=0, tiled=True)  16.9 us
    pallas_call x6, Pallas kernels, call(): pl.pallas_call(body, out_shape=shapes[0] if single else shapes, in_specs=...  12.3 us
    ppermute x2, starting transfers between devices, neighbours(): across = lax.ppermute(array, axis, edges)  6.86 us
    all_gather x2, blocking collectives, neighbours(): lax.all_gather(array, axis, axis_index_groups=[[i, i + 1] for i in range(...  4.57 us
    ppermute x2, waiting for transfers between devices, neighbours(): across = lax.ppermute(array, axis, edges)  3.05 us
  transfers between devices with their start and end apart: 2, of which 2 were waited for; matrix products, arithmetic and copies ran while one was open for 0% of the time, Pallas kernels for 15%

profile of v8, /device:TPU:1, one launch (start us, length us, event | category | flops | bytes accessed | tf_op | source)
XLA Modules:
  0.0 43.8 jit_solution(8429052374194100279)
XLA Ops:
  0.0 4.5 %collective-permute-start = (bf16[64,8,256]{2,1,0:T(8,128)(2,1)}, bf16[64,8,256]{2,1,0:T(8,128)(2,1)S(1)}, u32[]{:S(2)}, u32[]{:S(2)}) collective-permute-start(bf16[64,8,256]{2,1,0:T(8,128)(2,1)} %param.5), channel_id=1, source_target_pairs={{1,2},{3,4},{5,6},{7,8},{9,10},{11,12},{13,14},{15,16},{17,18},{19... | collective-permute-start | bytes 786440 | tf_op jit(solution)/shard_map/ppermute | solution.py:626
  4.5 1.8 %prepare.1 = (bf16[2,64,768]{2,1,0:T(8,128)(2,1)S(1)}, bf16[5,128,1152]{2,1,0:T(8,128)(2,1)S(1)}, bf16[1,64,768]{2,1,0:T(8,128)(2,1)S(1)}, bf16[2,128,1152]{2,1,...) custom-call(bf16[7,9,32,64]{3,2,1,0:T(8,128)(2,1)} %w_conv.1, ...), custom_call_target="tpu_custom_call" | custom-call | tf_op jit(solution)/shard_map/prepare/pallas_call | solution.py:569
  6.3 2.4 %all-gather = bf16[128,8,256]{2,1,0:T(8,128)(2,1)S(1)} all-gather(bf16[64,8,256]{2,1,0:T(8,128)(2,1)} %param.5), channel_id=2, replica_groups={{0,1},{2,3},{4,5},{6,7},{8,9},{10,11},{12,13},{14,15},{16,17},{18,19},{..., dimensions={0}, use_global_device_ids=true | all-gather | bytes 786432 | tf_op jit(solution)/shard_map/all_gather | solution.py:627
  8.7 1.7 %one_early.1 = (bf16[15,192,256]{2,1,0:T(8,128)(2,1)S(1)}, bf16[12,192,256]{2,1,0:T(8,128)(2,1)S(1)}, bf16[8,192,256]{2,1,0:T(8,128)(2,1)S(1)}, f32[1,128,256]{2...) custom-call(bf16[2,64,8,256]{3,2,1,0:T(8,128)(2,1)S(1)} %bitcast.4, ...), custom_call_target="tpu_custom_call" | custom-call | tf_op jit(solution)/shard_map/one_early/pallas_call | solution.py:569
  10.4 0.5 %collective-permute-done.across = bf16[64,8,256]{2,1,0:T(8,128)(2,1)S(1)} collective-permute-done((bf16[64,8,256]{2,1,0:T(8,128)(2,1)}, bf16[64,8,256]{2,1,0:T(8,128)(2,1)S(1)}, u32[]{:S(2)}, u32[]{:S(2)}) %collective-permute-start) | collective-permute-done | bytes 262176 | tf_op jit(solution)/shard_map/ppermute | solution.py:626
  10.9 2.0 %one_late.1 = (bf16[8,64,256]{2,1,0:T(8,128)(2,1)S(1)}, bf16[32,32,128]{2,1,0:T(8,128)(2,1)S(1)}) custom-call(bf16[64,8,256]{2,1,0:T(8,128)(2,1)S(1)} %collective-permute-done.across, bf16[15,192,256]{2,1,0:T(8,128)(2,1)S(1)} %get-tuple-element.39.kept_0, bf16[12,192,256]{2,1,0:T(8,128)(2,1)S(1)} %get-tuple-element.40.kept_1, ...), custom_call_target="tpu_custom_call" | custom-call | tf_op jit(solution)/shard_map/one_late/pallas_call | solution.py:569
  12.9 16.9 %all_to_all.5.tiles = bf16[32,32,128]{2,1,0:T(8,128)(2,1)S(1)} all-to-all(bf16[32,32,128]{2,1,0:T(8,128)(2,1)S(1)} %get-tuple-element.45), channel_id=1, replica_groups=mesh['groups'=1,'row'=32] {'row'}, dimensions={0} | all-to-all | bytes 524288 | tf_op jit(solution)/shard_map/all_to_all | solution.py:638
  29.8 0.5 %symmetrize.1 = bf16[8,64,256]{2,1,0:T(8,128)(2,1)S(1)} custom-call(bf16[32,32,128]{2,1,0:T(8,128)(2,1)S(1)} %all_to_all.5.tiles, bf16[8,64,256]{2,1,0:T(8,128)(2,1)S(1)} %get-tuple-element.46.own), custom_call_target="tpu_custom_call" | custom-call | tf_op jit(solution)/shard_map/symmetrize/pallas_call | solution.py:569
  30.3 2.4 %collective-permute-start.1 = (bf16[8,64,256]{2,1,0:T(8,128)(2,1)S(1)}, bf16[8,64,256]{2,1,0:T(8,128)(2,1)S(1)}, u32[]{:S(2)}, u32[]{:S(2)}) collective-permute-start(bf16[8,64,256]{2,1,0:T(8,128)(2,1)S(1)} %symmetrize.1), channel_id=1, source_target_pairs={{1,2},{3,4},{5,6},{7,8},{9,10},{11,12},{13,14},{15,16},{17,18},{19... | collective-permute-start | bytes 786440 | tf_op jit(solution)/shard_map/ppermute | solution.py:626
  32.7 2.2 %all-gather.1 = bf16[16,64,256]{2,1,0:T(8,128)(2,1)S(1)} all-gather(bf16[8,64,256]{2,1,0:T(8,128)(2,1)S(1)} %symmetrize.1), channel_id=3, replica_groups={{0,1},{2,3},{4,5},{6,7},{8,9},{10,11},{12,13},{14,15},{16,17},{18,19},{..., dimensions={0}, use_global_device_ids=true | all-gather | bytes 786432 | tf_op jit(solution)/shard_map/all_gather | solution.py:627
  34.9 3.2 %two_early.1 = (bf16[16,192,256]{2,1,0:T(8,128)(2,1)S(1)}, bf16[14,192,256]{2,1,0:T(8,128)(2,1)S(1)}, bf16[14,192,256]{2,1,0:T(8,128)(2,1)S(1)}, bf16[10,192,256...) custom-call(bf16[2,8,64,256]{3,2,1,0:T(8,128)(2,1)S(1)} %bitcast.3, ...), custom_call_target="tpu_custom_call" | custom-call | tf_op jit(solution)/shard_map/two_early/pallas_call | solution.py:569
  38.1 2.5 %collective-permute-done.1.across = bf16[8,64,256]{2,1,0:T(8,128)(2,1)S(1)} collective-permute-done((bf16[8,64,256]{2,1,0:T(8,128)(2,1)S(1)}, bf16[8,64,256]{2,1,0:T(8,128)(2,1)S(1)}, u32[]{:S(2)}, u32[]{:S(2)}) %collective-permute-start.1) | collective-permute-done | bytes 262176 | tf_op jit(solution)/shard_map/ppermute | solution.py:626
  40.6 3.2 %two_late.1 = bf16[64,8,256]{2,1,0:T(8,128)(2,1)} custom-call(bf16[8,64,256]{2,1,0:T(8,128)(2,1)S(1)} %collective-permute-done.1.across, bf16[16,192,256]{2,1,0:T(8,128)(2,1)S(1)} %get-tuple-element.47.refs_0_, bf16[14,192,256]{2,1,0:T(8,128)(2,1)S(1)} %get-tuple-element.48.refs_1_, bf16[14,192,256]{2,1,0:T(8,128)(2,1)S(1)} %get-tuple-element.49.refs_2_, ...), custom_call_target="tpu_custom_call" | custom-call | tf_op jit(solution)/shard_map/two_late/pallas_call | solution.py:569
Async XLA Ops:
  0.0 10.9 %collective-permute-start = (bf16[64,8,256]{2,1,0:T(8,128)(2,1)}, bf16[64,8,256]{2,1,0:T(8,128)(2,1)S(1)}, u32[]{:S(2)}, u32[]{:S(2)}) collective-permute-start(bf16[64,8,256]{2,1,0:T(8,128)(2,1)} %param.5), channel_id=1, source_target_pairs={{1,2},{3,4},{5,6},{7,8},{9,10},{11,12},{13,14},{15,16},{17,18},{19... | collective-permute-start | bytes 786440 | tf_op jit(solution)/shard_map/ppermute | solution.py:626
  30.3 10.3 %collective-permute-start.1 = (bf16[8,64,256]{2,1,0:T(8,128)(2,1)S(1)}, bf16[8,64,256]{2,1,0:T(8,128)(2,1)S(1)}, u32[]{:S(2)}, u32[]{:S(2)}) collective-permute-start(bf16[8,64,256]{2,1,0:T(8,128)(2,1)S(1)} %symmetrize.1), channel_id=1, source_target_pairs={{1,2},{3,4},{5,6},{7,8},{9,10},{11,12},{13,14},{15,16},{17,18},{19... | collective-permute-start | bytes 786440 | tf_op jit(solution)/shard_map/ppermute | solution.py:626

commit v9 on v8

--- a/solution.py
+++ b/solution.py
@@ -23,7 +23,7 @@
 
 
 def group_of(dilation):
-    return 4 if dilation < dilations[-1] else 2
+    return 4 if dilation == dilations[1] else 2
 
 
 def cover(low, high, limit, dilation):

time: 44 us -> 43.7 us (level)
  Pallas kernels: 12.3 us -> 11.7 us
    pallas_call x6, Pallas kernels: 12.3 us -> 11.7 us  [call(): pl.pallas_call(body, out_shape=shapes[0] if single else shapes, in_specs=...]
  transfers between devices with their start and end apart: 2 -> 2, of which waited for: 2 -> 2; matrix products, arithmetic and copies ran while one was open for 0% -> 0% of each run, Pallas kernels for 15% -> 14%
where the time goes in v9:
time: 43.7 us; the launch traced here: 43.5 us
  blocking collectives  21.5 us (49%)
  Pallas kernels  11.7 us (27%)
  starting transfers between devices  6.86 us (16%)
  waiting for transfers between devices  3.48 us (8%)
    all_to_all x1, blocking collectives, on_device(): lax.all_to_all(tiles, 'row', split_axis=0, concat_axis=0, tiled=True)  16.9 us
    pallas_call x6, Pallas kernels, call(): pl.pallas_call(body, out_shape=shapes[0] if single else shapes, in_specs=...  11.7 us
    ppermute x2, starting transfers between devices, neighbours(): across = lax.ppermute(array, axis, edges)  6.86 us
    all_gather x2, blocking collectives, neighbours(): lax.all_gather(array, axis, axis_index_groups=[[i, i + 1] for i in range(...  4.57 us
    ppermute x2, waiting for transfers between devices, neighbours(): across = lax.ppermute(array, axis, edges)  3.48 us
  transfers between devices with their start and end apart: 2, of which 2 were waited for; matrix products, arithmetic and copies ran while one was open for 0% of the time, Pallas kernels for 14%

profile of v9, /device:TPU:1, one launch (start us, length us, event | category | flops | bytes accessed | tf_op | source)
XLA Modules:
  0.0 43.5 jit_solution(3613749749597922932)
XLA Ops:
  0.0 4.5 %collective-permute-start = (bf16[64,8,256]{2,1,0:T(8,128)(2,1)}, bf16[64,8,256]{2,1,0:T(8,128)(2,1)S(1)}, u32[]{:S(2)}, u32[]{:S(2)}) collective-permute-start(bf16[64,8,256]{2,1,0:T(8,128)(2,1)} %param.5), channel_id=1, source_target_pairs={{1,2},{3,4},{5,6},{7,8},{9,10},{11,12},{13,14},{15,16},{17,18},{19... | collective-permute-start | bytes 786440 | tf_op jit(solution)/shard_map/ppermute | solution.py:626
  4.5 1.8 %prepare.1 = (bf16[5,64,768]{2,1,0:T(8,128)(2,1)S(1)}, bf16[2,128,1152]{2,1,0:T(8,128)(2,1)S(1)}, bf16[2,64,768]{2,1,0:T(8,128)(2,1)S(1)}, bf16[1,128,1152]{2,1,...) custom-call(bf16[7,9,32,64]{3,2,1,0:T(8,128)(2,1)} %w_conv.1, ...), custom_call_target="tpu_custom_call" | custom-call | tf_op jit(solution)/shard_map/prepare/pallas_call | solution.py:569
  6.3 2.4 %all-gather = bf16[128,8,256]{2,1,0:T(8,128)(2,1)S(1)} all-gather(bf16[64,8,256]{2,1,0:T(8,128)(2,1)} %param.5), channel_id=2, replica_groups={{0,1},{2,3},{4,5},{6,7},{8,9},{10,11},{12,13},{14,15},{16,17},{18,19},{..., dimensions={0}, use_global_device_ids=true | all-gather | bytes 786432 | tf_op jit(solution)/shard_map/all_gather | solution.py:627
  8.7 1.6 %one_early.1 = (bf16[15,192,256]{2,1,0:T(8,128)(2,1)S(1)}, bf16[12,192,256]{2,1,0:T(8,128)(2,1)S(1)}, bf16[8,192,256]{2,1,0:T(8,128)(2,1)S(1)}, f32[1,64,256]{2,...) custom-call(bf16[2,64,8,256]{3,2,1,0:T(8,128)(2,1)S(1)} %bitcast.4, ...), custom_call_target="tpu_custom_call" | custom-call | tf_op jit(solution)/shard_map/one_early/pallas_call | solution.py:569
  10.4 0.6 %collective-permute-done.across = bf16[64,8,256]{2,1,0:T(8,128)(2,1)S(1)} collective-permute-done((bf16[64,8,256]{2,1,0:T(8,128)(2,1)}, bf16[64,8,256]{2,1,0:T(8,128)(2,1)S(1)}, u32[]{:S(2)}, u32[]{:S(2)}) %collective-permute-start) | collective-permute-done | bytes 262176 | tf_op jit(solution)/shard_map/ppermute | solution.py:626
  10.9 2.0 %one_late.1 = (bf16[8,64,256]{2,1,0:T(8,128)(2,1)S(1)}, bf16[32,32,128]{2,1,0:T(8,128)(2,1)S(1)}) custom-call(bf16[64,8,256]{2,1,0:T(8,128)(2,1)S(1)} %collective-permute-done.across, bf16[15,192,256]{2,1,0:T(8,128)(2,1)S(1)} %get-tuple-element.39.kept_0, bf16[12,192,256]{2,1,0:T(8,128)(2,1)S(1)} %get-tuple-element.40.kept_1, ...), custom_call_target="tpu_custom_call" | custom-call | tf_op jit(solution)/shard_map/one_late/pallas_call | solution.py:569
  12.9 16.9 %all_to_all.5.tiles = bf16[32,32,128]{2,1,0:T(8,128)(2,1)S(1)} all-to-all(bf16[32,32,128]{2,1,0:T(8,128)(2,1)S(1)} %get-tuple-element.45), channel_id=1, replica_groups=mesh['groups'=1,'row'=32] {'row'}, dimensions={0} | all-to-all | bytes 524288 | tf_op jit(solution)/shard_map/all_to_all | solution.py:638
  29.8 0.5 %symmetrize.1 = bf16[8,64,256]{2,1,0:T(8,128)(2,1)S(1)} custom-call(bf16[32,32,128]{2,1,0:T(8,128)(2,1)S(1)} %all_to_all.5.tiles, bf16[8,64,256]{2,1,0:T(8,128)(2,1)S(1)} %get-tuple-element.46.own), custom_call_target="tpu_custom_call" | custom-call | tf_op jit(solution)/shard_map/symmetrize/pallas_call | solution.py:569
  30.3 2.4 %collective-permute-start.1 = (bf16[8,64,256]{2,1,0:T(8,128)(2,1)S(1)}, bf16[8,64,256]{2,1,0:T(8,128)(2,1)S(1)}, u32[]{:S(2)}, u32[]{:S(2)}) collective-permute-start(bf16[8,64,256]{2,1,0:T(8,128)(2,1)S(1)} %symmetrize.1), channel_id=1, source_target_pairs={{1,2},{3,4},{5,6},{7,8},{9,10},{11,12},{13,14},{15,16},{17,18},{19... | collective-permute-start | bytes 786440 | tf_op jit(solution)/shard_map/ppermute | solution.py:626
  32.7 2.2 %all-gather.1 = bf16[16,64,256]{2,1,0:T(8,128)(2,1)S(1)} all-gather(bf16[8,64,256]{2,1,0:T(8,128)(2,1)S(1)} %symmetrize.1), channel_id=3, replica_groups={{0,1},{2,3},{4,5},{6,7},{8,9},{10,11},{12,13},{14,15},{16,17},{18,19},{..., dimensions={0}, use_global_device_ids=true | all-gather | bytes 786432 | tf_op jit(solution)/shard_map/all_gather | solution.py:627
  34.9 2.8 %two_early.1 = (bf16[16,192,256]{2,1,0:T(8,128)(2,1)S(1)}, bf16[14,192,256]{2,1,0:T(8,128)(2,1)S(1)}, bf16[14,192,256]{2,1,0:T(8,128)(2,1)S(1)}, bf16[10,192,256...) custom-call(bf16[2,8,64,256]{3,2,1,0:T(8,128)(2,1)S(1)} %bitcast.3, ...), custom_call_target="tpu_custom_call" | custom-call | tf_op jit(solution)/shard_map/two_early/pallas_call | solution.py:569
  37.7 2.9 %collective-permute-done.1.across = bf16[8,64,256]{2,1,0:T(8,128)(2,1)S(1)} collective-permute-done((bf16[8,64,256]{2,1,0:T(8,128)(2,1)S(1)}, bf16[8,64,256]{2,1,0:T(8,128)(2,1)S(1)}, u32[]{:S(2)}, u32[]{:S(2)}) %collective-permute-start.1) | collective-permute-done | bytes 262176 | tf_op jit(solution)/shard_map/ppermute | solution.py:626
  40.6 2.9 %two_late.1 = bf16[64,8,256]{2,1,0:T(8,128)(2,1)} custom-call(bf16[8,64,256]{2,1,0:T(8,128)(2,1)S(1)} %collective-permute-done.1.across, bf16[16,192,256]{2,1,0:T(8,128)(2,1)S(1)} %get-tuple-element.47.refs_0_, bf16[14,192,256]{2,1,0:T(8,128)(2,1)S(1)} %get-tuple-element.48.refs_1_, bf16[14,192,256]{2,1,0:T(8,128)(2,1)S(1)} %get-tuple-element.49.refs_2_, ...), custom_call_target="tpu_custom_call" | custom-call | tf_op jit(solution)/shard_map/two_late/pallas_call | solution.py:569
Async XLA Ops:
  0.0 10.9 %collective-permute-start = (bf16[64,8,256]{2,1,0:T(8,128)(2,1)}, bf16[64,8,256]{2,1,0:T(8,128)(2,1)S(1)}, u32[]{:S(2)}, u32[]{:S(2)}) collective-permute-start(bf16[64,8,256]{2,1,0:T(8,128)(2,1)} %param.5), channel_id=1, source_target_pairs={{1,2},{3,4},{5,6},{7,8},{9,10},{11,12},{13,14},{15,16},{17,18},{19... | collective-permute-start | bytes 786440 | tf_op jit(solution)/shard_map/ppermute | solution.py:626
  30.3 10.3 %collective-permute-start.1 = (bf16[8,64,256]{2,1,0:T(8,128)(2,1)S(1)}, bf16[8,64,256]{2,1,0:T(8,128)(2,1)S(1)}, u32[]{:S(2)}, u32[]{:S(2)}) collective-permute-start(bf16[8,64,256]{2,1,0:T(8,128)(2,1)S(1)} %symmetrize.1), channel_id=1, source_target_pairs={{1,2},{3,4},{5,6},{7,8},{9,10},{11,12},{13,14},{15,16},{17,18},{19... | collective-permute-start | bytes 786440 | tf_op jit(solution)/shard_map/ppermute | solution.py:626

commit v10 on v9

--- a/solution.py
+++ b/solution.py
@@ -129,14 +129,6 @@
         banded[slot, row * inner : (row + 1) * inner, :] = jnp.concatenate(parts, axis=1)
 
 
-def spread_out(doubled, slot, w_out, layer):
-    block = w_out[layer].astype(F32).T.astype(BF16)
-    zeros = jnp.zeros_like(block)
-    doubled[slot] = jnp.concatenate(
-        [jnp.concatenate([block, zeros], axis=1), jnp.concatenate([zeros, block], axis=1)], axis=0
-    )
-
-
 def as_column(row, copies):
     size = row.shape[1]
     across = lax.broadcasted_iota(jnp.int32, (size, size), 1)
@@ -189,14 +181,11 @@
 
 
 def group_rows(stack, start, hidden, kernel, bias):
-    half = kernel.shape[1]
+    inner = kernel.shape[1]
     values = []
-    for pair in range(hidden.shape[0] // half):
-        blended = jnp.dot(kernel, hidden[pair * half : (pair + 1) * half], preferred_element_type=F32)
-        residual = [stack.get(start + (2 * pair + step) * stack.dilation, 1).astype(F32) for step in range(2)]
-        total = jnp.concatenate(residual, axis=0) + blended + bias
-        channels = total.shape[0] // 2
-        values += [total[:channels], total[channels:]]
+    for step in range(hidden.shape[0] // inner):
+        blended = jnp.dot(kernel, hidden[step * inner : (step + 1) * inner], preferred_element_type=F32)
+        values.append(stack.get(start + step * stack.dilation, 1).astype(F32) + blended + bias)
     return values
 
 
@@ -228,7 +217,7 @@
     return sum(1 for step in steps[:layer] if group_of(step) == group_of(steps[layer]))
 
 
-def prepare(w_conv, bias_in, w_out, bias_out, small, large, small_turned, large_turned, doubled, bias, bias_last,
+def prepare(w_conv, bias_in, w_out, bias_out, small, large, small_turned, large_turned, project, bias, bias_last,
             conv, proj, first_bias, last_bias, sems):
     odd, _ = position()
     pairs = [(w_conv, conv), (w_out, proj), (bias_in, first_bias), (bias_out, last_bias)]
@@ -238,9 +227,9 @@
     base = len(steps) - 1 - DEPTH
     for layer, step in enumerate(steps):
         spread_conv(small if group_of(step) == 2 else large, slot_of(steps, layer), conv, layer, False, odd)
-        spread_out(doubled, layer, proj, layer)
+        project[layer] = proj[layer].astype(F32).T.astype(BF16)
         bias[layer] = jnp.broadcast_to(as_column(first_bias[layer : layer + 1, :], 4), bias.shape[1:])
-        bias_last[layer] = jnp.broadcast_to(as_column(last_bias[layer : layer + 1, :], 2), bias_last.shape[1:])
+        bias_last[layer] = jnp.broadcast_to(as_column(last_bias[layer : layer + 1, :], 1), bias_last.shape[1:])
     for layer, step in enumerate(dilations):
         place = small_turned if group_of(step) == 2 else large_turned
         spread_conv(place, slot_of(dilations, layer), conv, base + layer, True, odd)
@@ -584,9 +573,9 @@
 
         shapes = [
             banded(layer_steps(), 2), banded(layer_steps(), 4), banded(dilations, 2), banded(dilations, 4),
-            (layers, 2 * channels, 2 * inner),
+            (layers, channels, inner),
             jax.ShapeDtypeStruct((layers, 4 * inner, LANES), F32),
-            jax.ShapeDtypeStruct((layers, 2 * channels, LANES), F32),
+            jax.ShapeDtypeStruct((layers, channels, LANES), F32),
         ]
         scratch = [
             pltpu.VMEM(w_conv.shape, BF16), pltpu.VMEM(w_out.shape, BF16),

time: 43.7 us -> 43.6 us (level)
  transfers between devices with their start and end apart: 2 -> 2, of which waited for: 2 -> 2; matrix products, arithmetic and copies ran while one was open for 0% -> 0% of each run, Pallas kernels for 14% -> 15%
where the time goes in v10:
time: 43.6 us; the launch traced here: 43.4 us
  blocking collectives  21.5 us (49%)
  Pallas kernels  11.7 us (27%)
  starting transfers between devices  6.86 us (16%)
  waiting for transfers between devices  3.34 us (8%)
    all_to_all x1, blocking collectives, on_device(): lax.all_to_all(tiles, 'row', split_axis=0, concat_axis=0, tiled=True)  16.9 us
    pallas_call x6, Pallas kernels, call(): pl.pallas_call(body, out_shape=shapes[0] if single else shapes, in_specs=...  11.7 us
    ppermute x2, starting transfers between devices, neighbours(): across = lax.ppermute(array, axis, edges)  6.86 us
    all_gather x2, blocking collectives, neighbours(): lax.all_gather(array, axis, axis_index_groups=[[i, i + 1] for i in range(...  4.57 us
    ppermute x2, waiting for transfers between devices, neighbours(): across = lax.ppermute(array, axis, edges)  3.34 us
  transfers between devices with their start and end apart: 2, of which 2 were waited for; matrix products, arithmetic and copies ran while one was open for 0% of the time, Pallas kernels for 15%

profile of v10, /device:TPU:1, one launch (start us, length us, event | category | flops | bytes accessed | tf_op | source)
XLA Modules:
  0.0 43.4 jit_solution(2309217526966913267)
XLA Ops:
  0.0 4.5 %collective-permute-start = (bf16[64,8,256]{2,1,0:T(8,128)(2,1)}, bf16[64,8,256]{2,1,0:T(8,128)(2,1)S(1)}, u32[]{:S(2)}, u32[]{:S(2)}) collective-permute-start(bf16[64,8,256]{2,1,0:T(8,128)(2,1)} %param.5), channel_id=1, source_target_pairs={{1,2},{3,4},{5,6},{7,8},{9,10},{11,12},{13,14},{15,16},{17,18},{19... | collective-permute-start | bytes 786440 | tf_op jit(solution)/shard_map/ppermute | solution.py:615
  4.5 1.8 %prepare.1 = (bf16[5,64,768]{2,1,0:T(8,128)(2,1)S(1)}, bf16[2,128,1152]{2,1,0:T(8,128)(2,1)S(1)}, bf16[2,64,768]{2,1,0:T(8,128)(2,1)S(1)}, bf16[1,128,1152]{2,1,...) custom-call(bf16[7,9,32,64]{3,2,1,0:T(8,128)(2,1)} %w_conv.1, ...), custom_call_target="tpu_custom_call" | custom-call | tf_op jit(solution)/shard_map/prepare/pallas_call | solution.py:558
  6.3 2.4 %all-gather = bf16[128,8,256]{2,1,0:T(8,128)(2,1)S(1)} all-gather(bf16[64,8,256]{2,1,0:T(8,128)(2,1)} %param.5), channel_id=2, replica_groups={{0,1},{2,3},{4,5},{6,7},{8,9},{10,11},{12,13},{14,15},{16,17},{18,19},{..., dimensions={0}, use_global_device_ids=true | all-gather | bytes 786432 | tf_op jit(solution)/shard_map/all_gather | solution.py:616
  8.7 1.8 %one_early.1 = (bf16[15,192,256]{2,1,0:T(8,128)(2,1)S(1)}, bf16[12,192,256]{2,1,0:T(8,128)(2,1)S(1)}, bf16[8,192,256]{2,1,0:T(8,128)(2,1)S(1)}, f32[1,64,256]{2,...) custom-call(bf16[2,64,8,256]{3,2,1,0:T(8,128)(2,1)S(1)} %bitcast.4, ...), custom_call_target="tpu_custom_call" | custom-call | tf_op jit(solution)/shard_map/one_early/pallas_call | solution.py:558
  10.4 0.5 %collective-permute-done.across = bf16[64,8,256]{2,1,0:T(8,128)(2,1)S(1)} collective-permute-done((bf16[64,8,256]{2,1,0:T(8,128)(2,1)}, bf16[64,8,256]{2,1,0:T(8,128)(2,1)S(1)}, u32[]{:S(2)}, u32[]{:S(2)}) %collective-permute-start) | collective-permute-done | bytes 262176 | tf_op jit(solution)/shard_map/ppermute | solution.py:615
  10.9 1.9 %one_late.1 = (bf16[8,64,256]{2,1,0:T(8,128)(2,1)S(1)}, bf16[32,32,128]{2,1,0:T(8,128)(2,1)S(1)}) custom-call(bf16[64,8,256]{2,1,0:T(8,128)(2,1)S(1)} %collective-permute-done.across, bf16[15,192,256]{2,1,0:T(8,128)(2,1)S(1)} %get-tuple-element.39.kept_0, bf16[12,192,256]{2,1,0:T(8,128)(2,1)S(1)} %get-tuple-element.40.kept_1, ...), custom_call_target="tpu_custom_call" | custom-call | tf_op jit(solution)/shard_map/one_late/pallas_call | solution.py:558
  12.9 16.9 %all_to_all.5.tiles = bf16[32,32,128]{2,1,0:T(8,128)(2,1)S(1)} all-to-all(bf16[32,32,128]{2,1,0:T(8,128)(2,1)S(1)} %get-tuple-element.45), channel_id=1, replica_groups=mesh['groups'=1,'row'=32] {'row'}, dimensions={0} | all-to-all | bytes 524288 | tf_op jit(solution)/shard_map/all_to_all | solution.py:627
  29.8 0.5 %symmetrize.1 = bf16[8,64,256]{2,1,0:T(8,128)(2,1)S(1)} custom-call(bf16[32,32,128]{2,1,0:T(8,128)(2,1)S(1)} %all_to_all.5.tiles, bf16[8,64,256]{2,1,0:T(8,128)(2,1)S(1)} %get-tuple-element.46.own), custom_call_target="tpu_custom_call" | custom-call | tf_op jit(solution)/shard_map/symmetrize/pallas_call | solution.py:558
  30.3 2.4 %collective-permute-start.1 = (bf16[8,64,256]{2,1,0:T(8,128)(2,1)S(1)}, bf16[8,64,256]{2,1,0:T(8,128)(2,1)S(1)}, u32[]{:S(2)}, u32[]{:S(2)}) collective-permute-start(bf16[8,64,256]{2,1,0:T(8,128)(2,1)S(1)} %symmetrize.1), channel_id=1, source_target_pairs={{1,2},{3,4},{5,6},{7,8},{9,10},{11,12},{13,14},{15,16},{17,18},{19... | collective-permute-start | bytes 786440 | tf_op jit(solution)/shard_map/ppermute | solution.py:615
  32.7 2.2 %all-gather.1 = bf16[16,64,256]{2,1,0:T(8,128)(2,1)S(1)} all-gather(bf16[8,64,256]{2,1,0:T(8,128)(2,1)S(1)} %symmetrize.1), channel_id=3, replica_groups={{0,1},{2,3},{4,5},{6,7},{8,9},{10,11},{12,13},{14,15},{16,17},{18,19},{..., dimensions={0}, use_global_device_ids=true | all-gather | bytes 786432 | tf_op jit(solution)/shard_map/all_gather | solution.py:616
  34.8 2.8 %two_early.1 = (bf16[16,192,256]{2,1,0:T(8,128)(2,1)S(1)}, bf16[14,192,256]{2,1,0:T(8,128)(2,1)S(1)}, bf16[14,192,256]{2,1,0:T(8,128)(2,1)S(1)}, bf16[10,192,256...) custom-call(bf16[2,8,64,256]{3,2,1,0:T(8,128)(2,1)S(1)} %bitcast.3, ...), custom_call_target="tpu_custom_call" | custom-call | tf_op jit(solution)/shard_map/two_early/pallas_call | solution.py:558
  37.7 2.9 %collective-permute-done.1.across = bf16[8,64,256]{2,1,0:T(8,128)(2,1)S(1)} collective-permute-done((bf16[8,64,256]{2,1,0:T(8,128)(2,1)S(1)}, bf16[8,64,256]{2,1,0:T(8,128)(2,1)S(1)}, u32[]{:S(2)}, u32[]{:S(2)}) %collective-permute-start.1) | collective-permute-done | bytes 262176 | tf_op jit(solution)/shard_map/ppermute | solution.py:615
  40.6 2.8 %two_late.1 = bf16[64,8,256]{2,1,0:T(8,128)(2,1)} custom-call(bf16[8,64,256]{2,1,0:T(8,128)(2,1)S(1)} %collective-permute-done.1.across, bf16[16,192,256]{2,1,0:T(8,128)(2,1)S(1)} %get-tuple-element.47.refs_0_, bf16[14,192,256]{2,1,0:T(8,128)(2,1)S(1)} %get-tuple-element.48.refs_1_, bf16[14,192,256]{2,1,0:T(8,128)(2,1)S(1)} %get-tuple-element.49.refs_2_, ...), custom_call_target="tpu_custom_call" | custom-call | tf_op jit(solution)/shard_map/two_late/pallas_call | solution.py:558
Async XLA Ops:
  0.0 10.9 %collective-permute-start = (bf16[64,8,256]{2,1,0:T(8,128)(2,1)}, bf16[64,8,256]{2,1,0:T(8,128)(2,1)S(1)}, u32[]{:S(2)}, u32[]{:S(2)}) collective-permute-start(bf16[64,8,256]{2,1,0:T(8,128)(2,1)} %param.5), channel_id=1, source_target_pairs={{1,2},{3,4},{5,6},{7,8},{9,10},{11,12},{13,14},{15,16},{17,18},{19... | collective-permute-start | bytes 786440 | tf_op jit(solution)/shard_map/ppermute | solution.py:615
  30.3 10.3 %collective-permute-start.1 = (bf16[8,64,256]{2,1,0:T(8,128)(2,1)S(1)}, bf16[8,64,256]{2,1,0:T(8,128)(2,1)S(1)}, u32[]{:S(2)}, u32[]{:S(2)}) collective-permute-start(bf16[8,64,256]{2,1,0:T(8,128)(2,1)S(1)} %symmetrize.1), channel_id=1, source_target_pairs={{1,2},{3,4},{5,6},{7,8},{9,10},{11,12},{13,14},{15,16},{17,18},{19... | collective-permute-start | bytes 786440 | tf_op jit(solution)/shard_map/ppermute | solution.py:615

commit v11 on v10

--- a/solution.py
+++ b/solution.py
@@ -11,6 +11,7 @@
 dilations = (1, 2, 4)
 LANES = 128
 LAG = 3
+PARTS = 4
 F32 = jnp.float32
 BF16 = jnp.bfloat16
 
@@ -479,7 +480,7 @@
 
 def two_late(across, *refs):
     kept_refs, sums, weight_refs = refs[:6], refs[6:12], refs[12:19]
-    out, stack_refs, wide = refs[19], refs[20:26], refs[26]
+    out, stack_refs, (wide, buffer, sems) = refs[19], refs[20:26], refs[26:]
     shard_rows, channels, width = across.shape
     odd, edge = position()
     steps = two_steps()
@@ -522,8 +523,17 @@
     groups, _ = late_groups(stages, DEPTH)
     rows = range(stage.low, stage.high + 1)
     block_one(weights, DEPTH, stage, stage.late, rows, sources[0], store_last, groups, sums[-1])
-    whole = jnp.concatenate([wide[block] for block in range(width // LANES)], axis=1)
-    out[...] = whole.reshape(channels, shard_rows, width).astype(BF16)
+    copies = []
+    part = channels // PARTS
+    for index in range(PARTS):
+        lines = slice(index * part * shard_rows, (index + 1) * part * shard_rows)
+        whole = jnp.concatenate([wide[block, lines, :] for block in range(width // LANES)], axis=1)
+        buffer[index * part : (index + 1) * part] = whole.reshape(part, shard_rows, width).astype(BF16)
+        place = pl.ds(index * part, part)
+        copies.append(pltpu.make_async_copy(buffer.at[place], out.at[place], sems.at[index]))
+        copies[-1].start()
+    for copy in copies:
+        copy.wait()
 
 
 VMEM = pl.BlockSpec(memory_space=pltpu.VMEM)
@@ -552,14 +562,14 @@
     def wide(self, *shards):
         return pltpu.VMEM(shards + (self.width // LANES, self.channels * self.shard_rows, LANES), F32)
 
-    def call(self, body, args, shapes, scratch, specs=None):
+    def call(self, body, args, shapes, scratch, specs=None, out_spec=VMEM):
         shapes = [shape if isinstance(shape, jax.ShapeDtypeStruct) else jax.ShapeDtypeStruct(shape, BF16) for shape in shapes]
         single = len(shapes) == 1
         return pl.pallas_call(
             body,
             out_shape=shapes[0] if single else shapes,
             in_specs=specs or [VMEM] * len(args),
-            out_specs=VMEM if single else [VMEM] * len(shapes),
+            out_specs=out_spec if single else [VMEM] * len(shapes),
             scratch_shapes=scratch,
             compiler_params=pltpu.CompilerParams(vmem_limit_bytes=(10 + 6 * self.width // LANES) * 1024 * 1024),
             name=body.__name__,
@@ -605,7 +615,9 @@
 
     def two_late(self, *args):
         scratch = [self.late(self.two[index]) for index in LAYERS_OF] + [self.wide()]
-        return self.call(two_late, args, [(self.channels, self.shard_rows, self.width)], scratch)
+        shape = (self.channels, self.shard_rows, self.width)
+        scratch += [pltpu.VMEM(shape, BF16), pltpu.SemaphoreType.DMA((PARTS,))]
+        return self.call(two_late, args, [shape], scratch, None, HBM)
 
 
 def neighbours(array, axis):

time: 43.6 us -> 43.6 us (level)
  no operation moved by 1% of the time
where the time goes in v11:
time: 43.6 us; the launch traced here: 43.4 us
  blocking collectives  21.5 us (49%)
  Pallas kernels  11.7 us (27%)
  starting transfers between devices  6.86 us (16%)
  waiting for transfers between devices  3.34 us (8%)
    all_to_all x1, blocking collectives, on_device(): lax.all_to_all(tiles, 'row', split_axis=0, concat_axis=0, tiled=True)  16.9 us
    pallas_call x6, Pallas kernels, call(): pl.pallas_call(body, out_shape=shapes[0] if single else shapes, in_specs=...  11.7 us
    ppermute x2, starting transfers between devices, neighbours(): across = lax.ppermute(array, axis, edges)  6.86 us
    all_gather x2, blocking collectives, neighbours(): lax.all_gather(array, axis, axis_index_groups=[[i, i + 1] for i in range(...  4.57 us
    ppermute x2, waiting for transfers between devices, neighbours(): across = lax.ppermute(array, axis, edges)  3.34 us
  transfers between devices with their start and end apart: 2, of which 2 were waited for; matrix products, arithmetic and copies ran while one was open for 0% of the time, Pallas kernels for 15%

profile of v11, /device:TPU:1, one launch (start us, length us, event | category | flops | bytes accessed | tf_op | source)
XLA Modules:
  0.0 43.4 jit_solution(18408360090983960223)
XLA Ops:
  0.0 4.5 %collective-permute-start = (bf16[64,8,256]{2,1,0:T(8,128)(2,1)}, bf16[64,8,256]{2,1,0:T(8,128)(2,1)S(1)}, u32[]{:S(2)}, u32[]{:S(2)}) collective-permute-start(bf16[64,8,256]{2,1,0:T(8,128)(2,1)} %param.5), channel_id=1, source_target_pairs={{1,2},{3,4},{5,6},{7,8},{9,10},{11,12},{13,14},{15,16},{17,18},{19... | collective-permute-start | bytes 786440 | tf_op jit(solution)/shard_map/ppermute | solution.py:627
  4.5 1.8 %prepare.1 = (bf16[5,64,768]{2,1,0:T(8,128)(2,1)S(1)}, bf16[2,128,1152]{2,1,0:T(8,128)(2,1)S(1)}, bf16[2,64,768]{2,1,0:T(8,128)(2,1)S(1)}, bf16[1,128,1152]{2,1,...) custom-call(bf16[7,9,32,64]{3,2,1,0:T(8,128)(2,1)} %w_conv.1, ...), custom_call_target="tpu_custom_call" | custom-call | tf_op jit(solution)/shard_map/prepare/pallas_call | solution.py:568
  6.3 2.4 %all-gather = bf16[128,8,256]{2,1,0:T(8,128)(2,1)S(1)} all-gather(bf16[64,8,256]{2,1,0:T(8,128)(2,1)} %param.5), channel_id=2, replica_groups={{0,1},{2,3},{4,5},{6,7},{8,9},{10,11},{12,13},{14,15},{16,17},{18,19},{..., dimensions={0}, use_global_device_ids=true | all-gather | bytes 786432 | tf_op jit(solution)/shard_map/all_gather | solution.py:628
  8.7 1.8 %one_early.1 = (bf16[15,192,256]{2,1,0:T(8,128)(2,1)S(1)}, bf16[12,192,256]{2,1,0:T(8,128)(2,1)S(1)}, bf16[8,192,256]{2,1,0:T(8,128)(2,1)S(1)}, f32[1,64,256]{2,...) custom-call(bf16[2,64,8,256]{3,2,1,0:T(8,128)(2,1)S(1)} %bitcast.4, ...), custom_call_target="tpu_custom_call" | custom-call | tf_op jit(solution)/shard_map/one_early/pallas_call | solution.py:568
  10.4 0.5 %collective-permute-done.across = bf16[64,8,256]{2,1,0:T(8,128)(2,1)S(1)} collective-permute-done((bf16[64,8,256]{2,1,0:T(8,128)(2,1)}, bf16[64,8,256]{2,1,0:T(8,128)(2,1)S(1)}, u32[]{:S(2)}, u32[]{:S(2)}) %collective-permute-start) | collective-permute-done | bytes 262176 | tf_op jit(solution)/shard_map/ppermute | solution.py:627
  10.9 1.9 %one_late.1 = (bf16[8,64,256]{2,1,0:T(8,128)(2,1)S(1)}, bf16[32,32,128]{2,1,0:T(8,128)(2,1)S(1)}) custom-call(bf16[64,8,256]{2,1,0:T(8,128)(2,1)S(1)} %collective-permute-done.across, bf16[15,192,256]{2,1,0:T(8,128)(2,1)S(1)} %get-tuple-element.39.kept_0, bf16[12,192,256]{2,1,0:T(8,128)(2,1)S(1)} %get-tuple-element.40.kept_1, ...), custom_call_target="tpu_custom_call" | custom-call | tf_op jit(solution)/shard_map/one_late/pallas_call | solution.py:568
  12.9 16.9 %all_to_all.5.tiles = bf16[32,32,128]{2,1,0:T(8,128)(2,1)S(1)} all-to-all(bf16[32,32,128]{2,1,0:T(8,128)(2,1)S(1)} %get-tuple-element.45), channel_id=1, replica_groups=mesh['groups'=1,'row'=32] {'row'}, dimensions={0} | all-to-all | bytes 524288 | tf_op jit(solution)/shard_map/all_to_all | solution.py:639
  29.8 0.5 %symmetrize.1 = bf16[8,64,256]{2,1,0:T(8,128)(2,1)S(1)} custom-call(bf16[32,32,128]{2,1,0:T(8,128)(2,1)S(1)} %all_to_all.5.tiles, bf16[8,64,256]{2,1,0:T(8,128)(2,1)S(1)} %get-tuple-element.46.own), custom_call_target="tpu_custom_call" | custom-call | tf_op jit(solution)/shard_map/symmetrize/pallas_call | solution.py:568
  30.3 2.4 %collective-permute-start.1 = (bf16[8,64,256]{2,1,0:T(8,128)(2,1)S(1)}, bf16[8,64,256]{2,1,0:T(8,128)(2,1)S(1)}, u32[]{:S(2)}, u32[]{:S(2)}) collective-permute-start(bf16[8,64,256]{2,1,0:T(8,128)(2,1)S(1)} %symmetrize.1), channel_id=1, source_target_pairs={{1,2},{3,4},{5,6},{7,8},{9,10},{11,12},{13,14},{15,16},{17,18},{19... | collective-permute-start | bytes 786440 | tf_op jit(solution)/shard_map/ppermute | solution.py:627
  32.7 2.2 %all-gather.1 = bf16[16,64,256]{2,1,0:T(8,128)(2,1)S(1)} all-gather(bf16[8,64,256]{2,1,0:T(8,128)(2,1)S(1)} %symmetrize.1), channel_id=3, replica_groups={{0,1},{2,3},{4,5},{6,7},{8,9},{10,11},{12,13},{14,15},{16,17},{18,19},{..., dimensions={0}, use_global_device_ids=true | all-gather | bytes 786432 | tf_op jit(solution)/shard_map/all_gather | solution.py:628
  34.8 2.8 %two_early.1 = (bf16[16,192,256]{2,1,0:T(8,128)(2,1)S(1)}, bf16[14,192,256]{2,1,0:T(8,128)(2,1)S(1)}, bf16[14,192,256]{2,1,0:T(8,128)(2,1)S(1)}, bf16[10,192,256...) custom-call(bf16[2,8,64,256]{3,2,1,0:T(8,128)(2,1)S(1)} %bitcast.3, ...), custom_call_target="tpu_custom_call" | custom-call | tf_op jit(solution)/shard_map/two_early/pallas_call | solution.py:568
  37.7 2.9 %collective-permute-done.1.across = bf16[8,64,256]{2,1,0:T(8,128)(2,1)S(1)} collective-permute-done((bf16[8,64,256]{2,1,0:T(8,128)(2,1)S(1)}, bf16[8,64,256]{2,1,0:T(8,128)(2,1)S(1)}, u32[]{:S(2)}, u32[]{:S(2)}) %collective-permute-start.1) | collective-permute-done | bytes 262176 | tf_op jit(solution)/shard_map/ppermute | solution.py:627
  40.6 2.8 %two_late.1 = bf16[64,8,256]{2,1,0:T(8,128)(2,1)} custom-call(bf16[8,64,256]{2,1,0:T(8,128)(2,1)S(1)} %collective-permute-done.1.across, bf16[16,192,256]{2,1,0:T(8,128)(2,1)S(1)} %get-tuple-element.47.refs_0_, bf16[14,192,256]{2,1,0:T(8,128)(2,1)S(1)} %get-tuple-element.48.refs_1_, bf16[14,192,256]{2,1,0:T(8,128)(2,1)S(1)} %get-tuple-element.49.refs_2_, ...), custom_call_target="tpu_custom_call" | custom-call | tf_op jit(solution)/shard_map/two_late/pallas_call | solution.py:568
Async XLA Ops:
  0.0 10.9 %collective-permute-start = (bf16[64,8,256]{2,1,0:T(8,128)(2,1)}, bf16[64,8,256]{2,1,0:T(8,128)(2,1)S(1)}, u32[]{:S(2)}, u32[]{:S(2)}) collective-permute-start(bf16[64,8,256]{2,1,0:T(8,128)(2,1)} %param.5), channel_id=1, source_target_pairs={{1,2},{3,4},{5,6},{7,8},{9,10},{11,12},{13,14},{15,16},{17,18},{19... | collective-permute-start | bytes 786440 | tf_op jit(solution)/shard_map/ppermute | solution.py:627
  30.3 10.3 %collective-permute-start.1 = (bf16[8,64,256]{2,1,0:T(8,128)(2,1)S(1)}, bf16[8,64,256]{2,1,0:T(8,128)(2,1)S(1)}, u32[]{:S(2)}, u32[]{:S(2)}) collective-permute-start(bf16[8,64,256]{2,1,0:T(8,128)(2,1)S(1)} %symmetrize.1), channel_id=1, source_target_pairs={{1,2},{3,4},{5,6},{7,8},{9,10},{11,12},{13,14},{15,16},{17,18},{19... | collective-permute-start | bytes 786440 | tf_op jit(solution)/shard_map/ppermute | solution.py:627

commit v12 on v10

--- a/solution.py
+++ b/solution.py
@@ -353,10 +353,10 @@
 
 def chunks_turned(values, lines):
     values = list(values)
-    chunk = lax.broadcasted_iota(jnp.int32, values[0].shape, 1) // lines
+    lane = lax.broadcasted_iota(jnp.int16, values[0].shape, 1)
     for bit in range(3):
         step = 1 << bit
-        clear = ((chunk >> bit) & 1) == 0
+        clear = (lane & jnp.int16(lines * step)) == jnp.int16(0)
         for index in range(8):
             if index & step:
                 continue
@@ -399,7 +399,7 @@
         block_one(weights, layer, stage, stage.late, rows, stacks[layer], store, groups, sums[layer])
 
     half = channels // 2
-    low_lanes = lax.broadcasted_iota(jnp.int32, (half, LANES), 1) < LANES // 2
+    low_lanes = lax.broadcasted_iota(jnp.int16, (half, LANES), 1) < jnp.int16(LANES // 2)
     for block in range(width // LANES):
         values = [out[row, :, block * LANES : (block + 1) * LANES] for row in range(shard_rows)]
         for index, value in enumerate(chunks_turned(values, shard_rows)):
@@ -412,7 +412,7 @@
 def symmetrize(tiles, own, out):
     shard_rows, channels, width = own.shape
     half = channels // 2
-    low_lanes = lax.broadcasted_iota(jnp.int32, (half, LANES), 1) < LANES // 2
+    low_lanes = lax.broadcasted_iota(jnp.int16, (half, LANES), 1) < jnp.int16(LANES // 2)
     lane_in = lax.broadcasted_iota(jnp.int32, (LANES, LANES), 0)
     lane_out = lax.broadcasted_iota(jnp.int32, (LANES, LANES), 1)
     size = shard_rows

time: 43.6 us -> 43.6 us (level)
  no operation moved by 1% of the time
where the time goes in v12:
time: 43.6 us; the launch traced here: 43.4 us
  blocking collectives  21.5 us (49%)
  Pallas kernels  11.7 us (27%)
  starting transfers between devices  6.86 us (16%)
  waiting for transfers between devices  3.33 us (8%)
    all_to_all x1, blocking collectives, on_device(): lax.all_to_all(tiles, 'row', split_axis=0, concat_axis=0, tiled=True)  16.9 us
    pallas_call x6, Pallas kernels, call(): pl.pallas_call(body, out_shape=shapes[0] if single else shapes, in_specs=...  11.7 us
    ppermute x2, starting transfers between devices, neighbours(): across = lax.ppermute(array, axis, edges)  6.86 us
    all_gather x2, blocking collectives, neighbours(): lax.all_gather(array, axis, axis_index_groups=[[i, i + 1] for i in range(...  4.57 us
    ppermute x2, waiting for transfers between devices, neighbours(): across = lax.ppermute(array, axis, edges)  3.33 us
  transfers between devices with their start and end apart: 2, of which 2 were waited for; matrix products, arithmetic and copies ran while one was open for 0% of the time, Pallas kernels for 15%

profile of v12, /device:TPU:1, one launch (start us, length us, event | category | flops | bytes accessed | tf_op | source)
XLA Modules:
  0.0 43.4 jit_solution(11675395825274145018)
XLA Ops:
  0.0 4.5 %collective-permute-start = (bf16[64,8,256]{2,1,0:T(8,128)(2,1)}, bf16[64,8,256]{2,1,0:T(8,128)(2,1)S(1)}, u32[]{:S(2)}, u32[]{:S(2)}) collective-permute-start(bf16[64,8,256]{2,1,0:T(8,128)(2,1)} %param.5), channel_id=1, source_target_pairs={{1,2},{3,4},{5,6},{7,8},{9,10},{11,12},{13,14},{15,16},{17,18},{19... | collective-permute-start | bytes 786440 | tf_op jit(solution)/shard_map/ppermute | solution.py:615
  4.5 1.8 %prepare.1 = (bf16[5,64,768]{2,1,0:T(8,128)(2,1)S(1)}, bf16[2,128,1152]{2,1,0:T(8,128)(2,1)S(1)}, bf16[2,64,768]{2,1,0:T(8,128)(2,1)S(1)}, bf16[1,128,1152]{2,1,...) custom-call(bf16[7,9,32,64]{3,2,1,0:T(8,128)(2,1)} %w_conv.1, ...), custom_call_target="tpu_custom_call" | custom-call | tf_op jit(solution)/shard_map/prepare/pallas_call | solution.py:558
  6.3 2.4 %all-gather = bf16[128,8,256]{2,1,0:T(8,128)(2,1)S(1)} all-gather(bf16[64,8,256]{2,1,0:T(8,128)(2,1)} %param.5), channel_id=2, replica_groups={{0,1},{2,3},{4,5},{6,7},{8,9},{10,11},{12,13},{14,15},{16,17},{18,19},{..., dimensions={0}, use_global_device_ids=true | all-gather | bytes 786432 | tf_op jit(solution)/shard_map/all_gather | solution.py:616
  8.7 1.8 %one_early.1 = (bf16[15,192,256]{2,1,0:T(8,128)(2,1)S(1)}, bf16[12,192,256]{2,1,0:T(8,128)(2,1)S(1)}, bf16[8,192,256]{2,1,0:T(8,128)(2,1)S(1)}, f32[1,64,256]{2,...) custom-call(bf16[2,64,8,256]{3,2,1,0:T(8,128)(2,1)S(1)} %bitcast.4, ...), custom_call_target="tpu_custom_call" | custom-call | tf_op jit(solution)/shard_map/one_early/pallas_call | solution.py:558
  10.4 0.5 %collective-permute-done.across = bf16[64,8,256]{2,1,0:T(8,128)(2,1)S(1)} collective-permute-done((bf16[64,8,256]{2,1,0:T(8,128)(2,1)}, bf16[64,8,256]{2,1,0:T(8,128)(2,1)S(1)}, u32[]{:S(2)}, u32[]{:S(2)}) %collective-permute-start) | collective-permute-done | bytes 262176 | tf_op jit(solution)/shard_map/ppermute | solution.py:615
  10.9 1.9 %one_late.1 = (bf16[8,64,256]{2,1,0:T(8,128)(2,1)S(1)}, bf16[32,32,128]{2,1,0:T(8,128)(2,1)S(1)}) custom-call(bf16[64,8,256]{2,1,0:T(8,128)(2,1)S(1)} %collective-permute-done.across, bf16[15,192,256]{2,1,0:T(8,128)(2,1)S(1)} %get-tuple-element.39.kept_0, bf16[12,192,256]{2,1,0:T(8,128)(2,1)S(1)} %get-tuple-element.40.kept_1, ...), custom_call_target="tpu_custom_call" | custom-call | tf_op jit(solution)/shard_map/one_late/pallas_call | solution.py:558
  12.9 16.9 %all_to_all.5.tiles = bf16[32,32,128]{2,1,0:T(8,128)(2,1)S(1)} all-to-all(bf16[32,32,128]{2,1,0:T(8,128)(2,1)S(1)} %get-tuple-element.45), channel_id=1, replica_groups=mesh['groups'=1,'row'=32] {'row'}, dimensions={0} | all-to-all | bytes 524288 | tf_op jit(solution)/shard_map/all_to_all | solution.py:627
  29.8 0.5 %symmetrize.1 = bf16[8,64,256]{2,1,0:T(8,128)(2,1)S(1)} custom-call(bf16[32,32,128]{2,1,0:T(8,128)(2,1)S(1)} %all_to_all.5.tiles, bf16[8,64,256]{2,1,0:T(8,128)(2,1)S(1)} %get-tuple-element.46.own), custom_call_target="tpu_custom_call" | custom-call | tf_op jit(solution)/shard_map/symmetrize/pallas_call | solution.py:558
  30.3 2.4 %collective-permute-start.1 = (bf16[8,64,256]{2,1,0:T(8,128)(2,1)S(1)}, bf16[8,64,256]{2,1,0:T(8,128)(2,1)S(1)}, u32[]{:S(2)}, u32[]{:S(2)}) collective-permute-start(bf16[8,64,256]{2,1,0:T(8,128)(2,1)S(1)} %symmetrize.1), channel_id=1, source_target_pairs={{1,2},{3,4},{5,6},{7,8},{9,10},{11,12},{13,14},{15,16},{17,18},{19... | collective-permute-start | bytes 786440 | tf_op jit(solution)/shard_map/ppermute | solution.py:615
  32.7 2.2 %all-gather.1 = bf16[16,64,256]{2,1,0:T(8,128)(2,1)S(1)} all-gather(bf16[8,64,256]{2,1,0:T(8,128)(2,1)S(1)} %symmetrize.1), channel_id=3, replica_groups={{0,1},{2,3},{4,5},{6,7},{8,9},{10,11},{12,13},{14,15},{16,17},{18,19},{..., dimensions={0}, use_global_device_ids=true | all-gather | bytes 786432 | tf_op jit(solution)/shard_map/all_gather | solution.py:616
  34.8 2.9 %two_early.1 = (bf16[16,192,256]{2,1,0:T(8,128)(2,1)S(1)}, bf16[14,192,256]{2,1,0:T(8,128)(2,1)S(1)}, bf16[14,192,256]{2,1,0:T(8,128)(2,1)S(1)}, bf16[10,192,256...) custom-call(bf16[2,8,64,256]{3,2,1,0:T(8,128)(2,1)S(1)} %bitcast.3, ...), custom_call_target="tpu_custom_call" | custom-call | tf_op jit(solution)/shard_map/two_early/pallas_call | solution.py:558
  37.7 2.9 %collective-permute-done.1.across = bf16[8,64,256]{2,1,0:T(8,128)(2,1)S(1)} collective-permute-done((bf16[8,64,256]{2,1,0:T(8,128)(2,1)S(1)}, bf16[8,64,256]{2,1,0:T(8,128)(2,1)S(1)}, u32[]{:S(2)}, u32[]{:S(2)}) %collective-permute-start.1) | collective-permute-done | bytes 262176 | tf_op jit(solution)/shard_map/ppermute | solution.py:615
  40.5 2.8 %two_late.1 = bf16[64,8,256]{2,1,0:T(8,128)(2,1)} custom-call(bf16[8,64,256]{2,1,0:T(8,128)(2,1)S(1)} %collective-permute-done.1.across, bf16[16,192,256]{2,1,0:T(8,128)(2,1)S(1)} %get-tuple-element.47.refs_0_, bf16[14,192,256]{2,1,0:T(8,128)(2,1)S(1)} %get-tuple-element.48.refs_1_, bf16[14,192,256]{2,1,0:T(8,128)(2,1)S(1)} %get-tuple-element.49.refs_2_, ...), custom_call_target="tpu_custom_call" | custom-call | tf_op jit(solution)/shard_map/two_late/pallas_call | solution.py:558
Async XLA Ops:
  0.0 10.9 %collective-permute-start = (bf16[64,8,256]{2,1,0:T(8,128)(2,1)}, bf16[64,8,256]{2,1,0:T(8,128)(2,1)S(1)}, u32[]{:S(2)}, u32[]{:S(2)}) collective-permute-start(bf16[64,8,256]{2,1,0:T(8,128)(2,1)} %param.5), channel_id=1, source_target_pairs={{1,2},{3,4},{5,6},{7,8},{9,10},{11,12},{13,14},{15,16},{17,18},{19... | collective-permute-start | bytes 786440 | tf_op jit(solution)/shard_map/ppermute | solution.py:615
  30.3 10.3 %collective-permute-start.1 = (bf16[8,64,256]{2,1,0:T(8,128)(2,1)S(1)}, bf16[8,64,256]{2,1,0:T(8,128)(2,1)S(1)}, u32[]{:S(2)}, u32[]{:S(2)}) collective-permute-start(bf16[8,64,256]{2,1,0:T(8,128)(2,1)S(1)} %symmetrize.1), channel_id=1, source_target_pairs={{1,2},{3,4},{5,6},{7,8},{9,10},{11,12},{13,14},{15,16},{17,18},{19... | collective-permute-start | bytes 786440 | tf_op jit(solution)/shard_map/ppermute | solution.py:615

commit v13 on v11

--- a/solution.py
+++ b/solution.py
@@ -11,7 +11,7 @@
 dilations = (1, 2, 4)
 LANES = 128
 LAG = 3
-PARTS = 4
+PARTS = 2
 F32 = jnp.float32
 BF16 = jnp.bfloat16
 

time: 43.6 us -> 43.6 us (level)
  no operation moved by 1% of the time
where the time goes in v13:
time: 43.6 us; the launch traced here: 43.4 us
  blocking collectives  21.5 us (49%)
  Pallas kernels  11.7 us (27%)
  starting transfers between devices  6.86 us (16%)
  waiting for transfers between devices  3.34 us (8%)
    all_to_all x1, blocking collectives, on_device(): lax.all_to_all(tiles, 'row', split_axis=0, concat_axis=0, tiled=True)  16.9 us
    pallas_call x6, Pallas kernels, call(): pl.pallas_call(body, out_shape=shapes[0] if single else shapes, in_specs=...  11.7 us
    ppermute x2, starting transfers between devices, neighbours(): across = lax.ppermute(array, axis, edges)  6.86 us
    all_gather x2, blocking collectives, neighbours(): lax.all_gather(array, axis, axis_index_groups=[[i, i + 1] for i in range(...  4.57 us
    ppermute x2, waiting for transfers between devices, neighbours(): across = lax.ppermute(array, axis, edges)  3.34 us
  transfers between devices with their start and end apart: 2, of which 2 were waited for; matrix products, arithmetic and copies ran while one was open for 0% of the time, Pallas kernels for 15%

profile of v13, /device:TPU:1, one launch (start us, length us, event | category | flops | bytes accessed | tf_op | source)
XLA Modules:
  0.0 43.4 jit_solution(16790630280612963113)
XLA Ops:
  0.0 4.5 %collective-permute-start = (bf16[64,8,256]{2,1,0:T(8,128)(2,1)}, bf16[64,8,256]{2,1,0:T(8,128)(2,1)S(1)}, u32[]{:S(2)}, u32[]{:S(2)}) collective-permute-start(bf16[64,8,256]{2,1,0:T(8,128)(2,1)} %param.5), channel_id=1, source_target_pairs={{1,2},{3,4},{5,6},{7,8},{9,10},{11,12},{13,14},{15,16},{17,18},{19... | collective-permute-start | bytes 786440 | tf_op jit(solution)/shard_map/ppermute | solution.py:627
  4.5 1.8 %prepare.1 = (bf16[5,64,768]{2,1,0:T(8,128)(2,1)S(1)}, bf16[2,128,1152]{2,1,0:T(8,128)(2,1)S(1)}, bf16[2,64,768]{2,1,0:T(8,128)(2,1)S(1)}, bf16[1,128,1152]{2,1,...) custom-call(bf16[7,9,32,64]{3,2,1,0:T(8,128)(2,1)} %w_conv.1, ...), custom_call_target="tpu_custom_call" | custom-call | tf_op jit(solution)/shard_map/prepare/pallas_call | solution.py:568
  6.3 2.4 %all-gather = bf16[128,8,256]{2,1,0:T(8,128)(2,1)S(1)} all-gather(bf16[64,8,256]{2,1,0:T(8,128)(2,1)} %param.5), channel_id=2, replica_groups={{0,1},{2,3},{4,5},{6,7},{8,9},{10,11},{12,13},{14,15},{16,17},{18,19},{..., dimensions={0}, use_global_device_ids=true | all-gather | bytes 786432 | tf_op jit(solution)/shard_map/all_gather | solution.py:628
  8.7 1.8 %one_early.1 = (bf16[15,192,256]{2,1,0:T(8,128)(2,1)S(1)}, bf16[12,192,256]{2,1,0:T(8,128)(2,1)S(1)}, bf16[8,192,256]{2,1,0:T(8,128)(2,1)S(1)}, f32[1,64,256]{2,...) custom-call(bf16[2,64,8,256]{3,2,1,0:T(8,128)(2,1)S(1)} %bitcast.4, ...), custom_call_target="tpu_custom_call" | custom-call | tf_op jit(solution)/shard_map/one_early/pallas_call | solution.py:568
  10.4 0.5 %collective-permute-done.across = bf16[64,8,256]{2,1,0:T(8,128)(2,1)S(1)} collective-permute-done((bf16[64,8,256]{2,1,0:T(8,128)(2,1)}, bf16[64,8,256]{2,1,0:T(8,128)(2,1)S(1)}, u32[]{:S(2)}, u32[]{:S(2)}) %collective-permute-start) | collective-permute-done | bytes 262176 | tf_op jit(solution)/shard_map/ppermute | solution.py:627
  10.9 1.9 %one_late.1 = (bf16[8,64,256]{2,1,0:T(8,128)(2,1)S(1)}, bf16[32,32,128]{2,1,0:T(8,128)(2,1)S(1)}) custom-call(bf16[64,8,256]{2,1,0:T(8,128)(2,1)S(1)} %collective-permute-done.across, bf16[15,192,256]{2,1,0:T(8,128)(2,1)S(1)} %get-tuple-element.39.kept_0, bf16[12,192,256]{2,1,0:T(8,128)(2,1)S(1)} %get-tuple-element.40.kept_1, ...), custom_call_target="tpu_custom_call" | custom-call | tf_op jit(solution)/shard_map/one_late/pallas_call | solution.py:568
  12.9 16.9 %all_to_all.5.tiles = bf16[32,32,128]{2,1,0:T(8,128)(2,1)S(1)} all-to-all(bf16[32,32,128]{2,1,0:T(8,128)(2,1)S(1)} %get-tuple-element.45), channel_id=1, replica_groups=mesh['groups'=1,'row'=32] {'row'}, dimensions={0} | all-to-all | bytes 524288 | tf_op jit(solution)/shard_map/all_to_all | solution.py:639
  29.8 0.5 %symmetrize.1 = bf16[8,64,256]{2,1,0:T(8,128)(2,1)S(1)} custom-call(bf16[32,32,128]{2,1,0:T(8,128)(2,1)S(1)} %all_to_all.5.tiles, bf16[8,64,256]{2,1,0:T(8,128)(2,1)S(1)} %get-tuple-element.46.own), custom_call_target="tpu_custom_call" | custom-call | tf_op jit(solution)/shard_map/symmetrize/pallas_call | solution.py:568
  30.3 2.4 %collective-permute-start.1 = (bf16[8,64,256]{2,1,0:T(8,128)(2,1)S(1)}, bf16[8,64,256]{2,1,0:T(8,128)(2,1)S(1)}, u32[]{:S(2)}, u32[]{:S(2)}) collective-permute-start(bf16[8,64,256]{2,1,0:T(8,128)(2,1)S(1)} %symmetrize.1), channel_id=1, source_target_pairs={{1,2},{3,4},{5,6},{7,8},{9,10},{11,12},{13,14},{15,16},{17,18},{19... | collective-permute-start | bytes 786440 | tf_op jit(solution)/shard_map/ppermute | solution.py:627
  32.7 2.2 %all-gather.1 = bf16[16,64,256]{2,1,0:T(8,128)(2,1)S(1)} all-gather(bf16[8,64,256]{2,1,0:T(8,128)(2,1)S(1)} %symmetrize.1), channel_id=3, replica_groups={{0,1},{2,3},{4,5},{6,7},{8,9},{10,11},{12,13},{14,15},{16,17},{18,19},{..., dimensions={0}, use_global_device_ids=true | all-gather | bytes 786432 | tf_op jit(solution)/shard_map/all_gather | solution.py:628
  34.8 2.8 %two_early.1 = (bf16[16,192,256]{2,1,0:T(8,128)(2,1)S(1)}, bf16[14,192,256]{2,1,0:T(8,128)(2,1)S(1)}, bf16[14,192,256]{2,1,0:T(8,128)(2,1)S(1)}, bf16[10,192,256...) custom-call(bf16[2,8,64,256]{3,2,1,0:T(8,128)(2,1)S(1)} %bitcast.3, ...), custom_call_target="tpu_custom_call" | custom-call | tf_op jit(solution)/shard_map/two_early/pallas_call | solution.py:568
  37.7 2.9 %collective-permute-done.1.across = bf16[8,64,256]{2,1,0:T(8,128)(2,1)S(1)} collective-permute-done((bf16[8,64,256]{2,1,0:T(8,128)(2,1)S(1)}, bf16[8,64,256]{2,1,0:T(8,128)(2,1)S(1)}, u32[]{:S(2)}, u32[]{:S(2)}) %collective-permute-start.1) | collective-permute-done | bytes 262176 | tf_op jit(solution)/shard_map/ppermute | solution.py:627
  40.6 2.8 %two_late.1 = bf16[64,8,256]{2,1,0:T(8,128)(2,1)} custom-call(bf16[8,64,256]{2,1,0:T(8,128)(2,1)S(1)} %collective-permute-done.1.across, bf16[16,192,256]{2,1,0:T(8,128)(2,1)S(1)} %get-tuple-element.47.refs_0_, bf16[14,192,256]{2,1,0:T(8,128)(2,1)S(1)} %get-tuple-element.48.refs_1_, bf16[14,192,256]{2,1,0:T(8,128)(2,1)S(1)} %get-tuple-element.49.refs_2_, ...), custom_call_target="tpu_custom_call" | custom-call | tf_op jit(solution)/shard_map/two_late/pallas_call | solution.py:568
Async XLA Ops:
  0.0 10.9 %collective-permute-start = (bf16[64,8,256]{2,1,0:T(8,128)(2,1)}, bf16[64,8,256]{2,1,0:T(8,128)(2,1)S(1)}, u32[]{:S(2)}, u32[]{:S(2)}) collective-permute-start(bf16[64,8,256]{2,1,0:T(8,128)(2,1)} %param.5), channel_id=1, source_target_pairs={{1,2},{3,4},{5,6},{7,8},{9,10},{11,12},{13,14},{15,16},{17,18},{19... | collective-permute-start | bytes 786440 | tf_op jit(solution)/shard_map/ppermute | solution.py:627
  30.3 10.3 %collective-permute-start.1 = (bf16[8,64,256]{2,1,0:T(8,128)(2,1)S(1)}, bf16[8,64,256]{2,1,0:T(8,128)(2,1)S(1)}, u32[]{:S(2)}, u32[]{:S(2)}) collective-permute-start(bf16[8,64,256]{2,1,0:T(8,128)(2,1)S(1)} %symmetrize.1), channel_id=1, source_target_pairs={{1,2},{3,4},{5,6},{7,8},{9,10},{11,12},{13,14},{15,16},{17,18},{19... | collective-permute-start | bytes 786440 | tf_op jit(solution)/shard_map/ppermute | solution.py:627
